TPU v7x, 32 devices: a whole 2x2x4 slice. The times are simulated.
32 devices in a mesh: src: 4 (over y, x), space: 8 (over z, core).
Axes of the slice: x: 2, y: 2, z: 4, core: 2. Of those that a mesh axis runs over, the one named last changes fastest.
Arguments:
- contrast: float32 [2, 64, 256, 256], P(None, None, 'space'), may hold values from -0.4 to 0.45
- measured: float32 [4, 2, 256, 256], P('src', None, 'space'), may hold values from -7 to 7
- positions: int32 [4, 2], P('src'), may hold values from 0 to 255
Outputs:
- contrast_sources: float32 [4, 2, 64, 256, 256], P('src', None, None, 'space')
- contrast_new: float32 [2, 64, 256, 256], P(None, None, 'space')
All inputs are finite; a program needn't handle non-finite values.
Results may differ from a plain program's by a relative error of at most 0.0003.
Values sent between devices are 32-bit elements; how exact they have to be, the bound alone decides.
No kernel may reach another device: no remote copies, remote signals or barrier semaphores. Data moves between devices by JAX's collectives and lax.ppermute only.
A program may use at most 128 MiB of HBM per device.

v0:
```python
from functools import partial
import math

import jax
import jax.numpy as jnp
from jax import lax
from jax.sharding import PartitionSpec as P

NX = 256
NY = 256
NZ = 64
OUTER = 2


WAVENUMBER = 2.0 * math.pi / 6.0
DAMPING = 0.3
SOURCE_GAP = 8.0
FLOOR_SHARE = 0.75
REAL_LOW = -0.25
REAL_HIGH = 0.35
IMAG_HIGH = 0.1
DEPTH_PATTERN = "akbn,sbnxy->sakxy"
FIRST_PATTERN = "akbn,sbznj->sazkj"
SECOND_PATTERN = "akbn,sbzxn->sazxk"


def laplace_modes(start_mode, length, total):
    mode_index = (start_mode + jnp.arange(length)).astype(jnp.float32)
    half_sine = jnp.sin(math.pi * mode_index / total)
    return 4.0 * half_sine * half_sine


def green_spectrum(depth_modes, first_modes, second_modes):
    eigen = depth_modes[:, None, None] + first_modes[None, :, None] + second_modes[None, None, :]
    wave_sq = WAVENUMBER * WAVENUMBER
    real_den = eigen - wave_sq
    imag_den = wave_sq * DAMPING
    factor = wave_sq / (real_den * real_den + imag_den * imag_den)
    return (factor * real_den, factor * imag_den)


def incident(positions, start_row, row_count):
    heights = jnp.arange(NZ).astype(jnp.float32) + SOURCE_GAP
    across = (start_row + jnp.arange(row_count)).astype(jnp.float32)
    along_y = jnp.arange(NY).astype(jnp.float32)
    source_x = positions[:, 0].astype(jnp.float32)
    source_y = positions[:, 1].astype(jnp.float32)
    offset_x = across[None, :] - source_x[:, None]
    offset_y = along_y[None, :] - source_y[:, None]
    dist_sq = (
        heights[None, :, None, None] * heights[None, :, None, None]
        + offset_x[:, None, :, None] * offset_x[:, None, :, None]
    )
    dist_sq = dist_sq + offset_y[:, None, None, :] * offset_y[:, None, None, :]
    phases = WAVENUMBER * jnp.sqrt(dist_sq)
    return (jnp.cos(phases), jnp.sin(phases))


def dft_table(length, orient, factor):
    indices = jnp.arange(length)
    turn_index = indices[:, None] * indices[None, :] % length
    angles = 2.0 * math.pi / length * turn_index.astype(jnp.float32)
    cosine = jnp.cos(angles) * factor
    sine_part = orient * jnp.sin(angles) * factor
    upper_rows = jnp.stack([cosine, sine_part], axis=1)
    bottom = jnp.stack([-sine_part, cosine], axis=1)
    return jnp.stack([upper_rows, bottom], axis=0)


def apply_table(table, fields, pattern):
    return jnp.einsum(pattern, table, fields, precision=lax.Precision.HIGHEST)


def times_green(spectrum, green_real, green_imag):
    real_part = spectrum[:, 0] * green_real - spectrum[:, 1] * green_imag
    imag_part = spectrum[:, 0] * green_imag + spectrum[:, 1] * green_real
    return jnp.stack([real_part, imag_part], axis=1)


def transform(fields, spectral, tables):
    z_forward, x_forward, y_forward, z_inverse, x_inverse, y_inverse = tables
    depth_done = apply_table(z_forward, fields, DEPTH_PATTERN)
    planes = apply_table(
        x_forward,
        lax.all_to_all(depth_done, "space", split_axis=2, concat_axis=3, tiled=True),
        FIRST_PATTERN,
    )
    spectrum = spectral(apply_table(y_forward, planes, SECOND_PATTERN))
    returned = apply_table(
        x_inverse, apply_table(y_inverse, spectrum, SECOND_PATTERN), FIRST_PATTERN
    )
    return apply_table(
        z_inverse,
        lax.all_to_all(returned, "space", split_axis=3, concat_axis=2, tiled=True),
        DEPTH_PATTERN,
    )


def descent_total(descent):
    local_sum = jnp.sum(descent * descent)
    return lax.psum(local_sum, ("src", "space"))


def bounded(numerator, power_sum, total_sources):
    floored = jnp.maximum(power_sum, FLOOR_SHARE * total_sources)
    return jnp.stack(
        [
            jnp.clip(numerator[0] / floored, REAL_LOW, REAL_HIGH),
            jnp.clip(numerator[1] / floored, 0.0, IMAG_HIGH),
        ],
        axis=0,
    )


def on_device(contrast, measured, positions):
    spaces = lax.axis_size("space")
    sources = positions.shape[0]
    row_count = contrast.shape[2]
    plane_count = NZ // spaces
    start_row = lax.axis_index("space") * row_count
    total_sources = sources * lax.axis_size("src")
    chi_real, chi_imag = (contrast[0], contrast[1])
    inc_real, inc_imag = incident(positions, start_row, row_count)
    tables = (
        dft_table(NZ, 1.0, 1.0),
        dft_table(NX, 1.0, 1.0),
        dft_table(NY, 1.0, 1.0),
        dft_table(NZ, -1.0, 1.0 / NZ),
        dft_table(NX, -1.0, 1.0 / NX),
        dft_table(NY, -1.0, 1.0 / NY),
    )
    green_real, green_imag = green_spectrum(
        laplace_modes(lax.axis_index("space") * plane_count, plane_count, NZ),
        laplace_modes(0, NX, NX),
        laplace_modes(0, NY, NY),
    )
    forward_green = partial(times_green, green_real=green_real, green_imag=green_imag)
    adjoint_green = partial(times_green, green_real=green_real, green_imag=-green_imag)
    sources_field = jnp.stack(
        [chi_real * inc_real - chi_imag * inc_imag, chi_real * inc_imag + chi_imag * inc_real],
        axis=1,
    )
    scattered = transform(sources_field, forward_green, tables)
    data_real = measured[:, 0]
    data_imag = measured[:, 1]
    data_local = jnp.sum(data_real * data_real + data_imag * data_imag)
    for outer_step in range(OUTER):
        chi_inc_real = chi_real * inc_real - chi_imag * inc_imag
        chi_inc_imag = chi_real * inc_imag + chi_imag * inc_real
        object_local = jnp.sum(chi_inc_real * chi_inc_real + chi_inc_imag * chi_inc_imag)
        data_total, object_total = lax.psum((data_local, object_local), ("src", "space"))
        data_weight = 1.0 / data_total
        object_weight = 1.0 / object_total
        total_real = inc_real + scattered[:, 0]
        total_imag = inc_imag + scattered[:, 1]
        resid_real = chi_real * total_real - chi_imag * total_imag - sources_field[:, 0]
        resid_imag = chi_real * total_imag + chi_imag * total_real - sources_field[:, 1]
        adjoint_real = -object_weight * (chi_real * resid_real + chi_imag * resid_imag)
        adjoint_imag = -object_weight * (chi_real * resid_imag - chi_imag * resid_real)
        adjoint_real = adjoint_real.at[:, 0].add(data_weight * (data_real - scattered[:, 0, 0]))
        adjoint_imag = adjoint_imag.at[:, 0].add(data_weight * (data_imag - scattered[:, 1, 0]))
        adjoint_input = jnp.stack([adjoint_real, adjoint_imag], axis=1)
        residual = jnp.stack([resid_real, resid_imag], axis=1)
        adjoint_image = transform(adjoint_input, adjoint_green, tables)
        descent = object_weight * residual + adjoint_image
        descent_early = descent_total(descent)
        descent_image = transform(descent, forward_green, tables)
        image_real = descent_image[:, 0]
        image_imag = descent_image[:, 1]
        change_real = descent[:, 0] - (chi_real * image_real - chi_imag * image_imag)
        change_imag = descent[:, 1] - (chi_real * image_imag + chi_imag * image_real)
        image_local = jnp.sum(
            image_real[:, 0] * image_real[:, 0] + image_imag[:, 0] * image_imag[:, 0]
        )
        change_local = jnp.sum(change_real * change_real + change_imag * change_imag)
        image_total, change_total = lax.psum((image_local, change_local), ("src", "space"))
        step_length = descent_early / (data_weight * image_total + object_weight * change_total)
        sources_field = sources_field + step_length * descent
        scattered = scattered + step_length * descent_image
        total_real = inc_real + scattered[:, 0]
        total_imag = inc_imag + scattered[:, 1]
        numerator_real = jnp.sum(
            sources_field[:, 0] * total_real + sources_field[:, 1] * total_imag, axis=0
        )
        numerator_imag = jnp.sum(
            sources_field[:, 1] * total_real - sources_field[:, 0] * total_imag, axis=0
        )
        power_sum = jnp.sum(total_real * total_real + total_imag * total_imag, axis=0)
        numerator = jnp.stack([numerator_real, numerator_imag], axis=0)
        numerator_part, power_part = (
            lax.psum_scatter(numerator, "src", scatter_dimension=1, tiled=True),
            lax.psum_scatter(power_sum, "src", scatter_dimension=0, tiled=True),
        )
        contrast_now = lax.all_gather(
            bounded(numerator_part, power_part, total_sources), "src", axis=1, tiled=True
        )
        chi_real = contrast_now[0]
        chi_imag = contrast_now[1]
    return (sources_field, contrast_now)


def solution(mesh):
    placed = (P(None, None, "space", None), P("src", None, "space", None), P("src", None))
    return jax.shard_map(
        on_device,
        mesh=mesh,
        in_specs=placed,
        out_specs=(P("src", None, None, "space", None), P(None, None, "space", None)),
        check_vma=False,
    )
```

profile of v0, /device:TPU:0, one launch (start us, length us, event | category | flops | bytes accessed | tf_op | source)
XLA Modules:
  0.0 1977.4 jit_solution(16921165929742797344)
XLA Ops:
  48.5 89.5 %all-to-all-done = f32[1,2,64,32,256]{4,1,3,0,2:T(2,128)} async-done(((f32[1,2,64,32,256]{4,1,3,0,2:T(2,128)}), f32[1,2,64,32,256]{4,1,3,0,2:T(2,128)}, u32[]{:S(2)}, u32[]{:S(2)}) %all-to-all-start) | async-done | bytes 4194336 | tf_op jit(solution)/shard_map/all_to_all | solution.py:85
  177.8 15.4 fusion.103
  205.8 113.8 %all-reduce.2 = (f32[]{:T(128)}, f32[]{:T(128)}) all-reduce(f32[]{:T(128)} %get-tuple-element.77, f32[]{:T(128)} %add_reduce_fusion.2), channel_id=1, replica_groups=mesh['src'=4,'space'=8] {'src','space'}, use_global_device_ids=true, to_apply=%region_1.2 | all-reduce | flops 2 | bytes 16 | tf_op jit(solution)/shard_map/psum | solution.py:151
  372.3 97.4 %all_to_all.150 = f32[1,2,64,32,256]{4,1,3,0,2:T(2,128)S(1)} all-to-all(f32[1,2,64,32,256]{4,1,3,0,2:T(2,128)S(1)} %copy.207), channel_id=1, replica_groups=mesh['src'=4,'space'=8] {'space'}, dimensions={2} | all-to-all | bytes 8388608 | tf_op jit(solution)/shard_map/all_to_all | solution.py:85
  506.8 15.2 fusion.109
  529.2 97.6 %all_to_all.151 = f32[1,2,8,256,256]{4,1,2,0,3:T(2,128)S(1)} all-to-all(f32[1,2,8,256,256]{4,1,2,0,3:T(2,128)} %copy.213), channel_id=1, replica_groups=mesh['src'=4,'space'=8] {'space'}, dimensions={3} | all-to-all | bytes 8388608 | tf_op jit(solution)/shard_map/all_to_all | solution.py:94
  647.2 96.5 %all_to_all.152 = f32[1,2,64,32,256]{4,1,3,0,2:T(2,128)S(1)} all-to-all(f32[1,2,64,32,256]{4,1,3,0,2:T(2,128)S(1)} %copy.218), channel_id=1, replica_groups=mesh['src'=4,'space'=8] {'space'}, dimensions={2} | all-to-all | bytes 8388608 | tf_op jit(solution)/shard_map/all_to_all | solution.py:85
  782.3 15.2 fusion.115
  804.9 97.6 %all_to_all.153 = f32[1,2,8,256,256]{4,1,2,0,3:T(2,128)S(1)} all-to-all(f32[1,2,8,256,256]{4,1,2,0,3:T(2,128)} %copy.224), channel_id=1, replica_groups=mesh['src'=4,'space'=8] {'space'}, dimensions={3} | all-to-all | bytes 8388608 | tf_op jit(solution)/shard_map/all_to_all | solution.py:94
  916.4 38.5 %all-reduce.1 = (f32[]{:T(128)}, f32[]{:T(128)}, f32[]{:T(128)}) all-reduce(f32[]{:T(128)} %get-tuple-element.117, f32[]{:T(128)} %fusion.202, f32[]{:T(128)} %fusion.139), channel_id=1, replica_groups=mesh['src'=4,'space'=8] {'src','space'}, use_global_device_ids=true, to_apply=%region_5.6 | all-reduce | flops 3 | bytes 24 | tf_op jit(solution)/shard_map/psum | solution.py:101
  1000.1 19.7 reduce-scatter.7.cloned.1.call-done
  1019.8 55.6 %reduce-scatter.5.cloned.1.call-done = f32[2,16,32,256]{3,1,2,0:T(8,128)} async-done(((f32[2,64,32,256]{3,1,2,0:T(8,128)}), f32[2,16,32,256]{3,1,2,0:T(8,128)}) %reduce-scatter.5.cloned.1.call-update) | async-done | bytes 1048592 | tf_op jit(solution)/shard_map/reduce_scatter | solution.py:191
  1078.1 52.7 %all-gather.3.cloned.1.call-done = f32[2,64,32,256]{3,1,2,0:T(8,128)} async-done(((f32[2,16,32,256]{3,1,2,0:T(8,128)}), f32[2,64,32,256]{3,1,2,0:T(8,128)}) %all-gather.3.cloned.1.call-update) | async-done | bytes 4194320 | tf_op jit(solution)/shard_map/all_gather | solution.py:194
  1142.8 39.4 %psum.71 = f32[]{:T(128)} all-reduce(f32[]{:T(128)} %add_reduce_fusion), channel_id=1, replica_groups=mesh['src'=4,'space'=8] {'src','space'}, use_global_device_ids=true, to_apply=%region_13.14 | all-reduce | flops 1 | bytes 8 | tf_op jit(solution)/shard_map/psum | solution.py:151
  1211.3 97.3 %all_to_all.154 = f32[1,2,64,32,256]{4,1,3,0,2:T(2,128)S(1)} all-to-all(f32[1,2,64,32,256]{4,1,3,0,2:T(2,128)S(1)} %copy.237), channel_id=1, replica_groups=mesh['src'=4,'space'=8] {'space'}, dimensions={2} | all-to-all | bytes 8388608 | tf_op jit(solution)/shard_map/all_to_all | solution.py:85
  1345.7 15.2 fusion.121
  1368.3 97.6 %all_to_all.155 = f32[1,2,8,256,256]{4,1,2,0,3:T(2,128)S(1)} all-to-all(f32[1,2,8,256,256]{4,1,2,0,3:T(2,128)} %copy.243), channel_id=1, replica_groups=mesh['src'=4,'space'=8] {'space'}, dimensions={3} | all-to-all | bytes 8388608 | tf_op jit(solution)/shard_map/all_to_all | solution.py:94
  1486.1 96.5 %all_to_all.156 = f32[1,2,64,32,256]{4,1,3,0,2:T(2,128)S(1)} all-to-all(f32[1,2,64,32,256]{4,1,3,0,2:T(2,128)S(1)} %copy.248), channel_id=1, replica_groups=mesh['src'=4,'space'=8] {'space'}, dimensions={2} | all-to-all | bytes 8388608 | tf_op jit(solution)/shard_map/all_to_all | solution.py:85
  1620.6 15.5 fusion.127
  1643.4 98.0 %all_to_all.157 = f32[1,2,8,256,256]{4,1,2,0,3:T(2,128)S(1)} all-to-all(f32[1,2,8,256,256]{4,1,2,0,3:T(2,128)} %copy.254), channel_id=1, replica_groups=mesh['src'=4,'space'=8] {'space'}, dimensions={3} | all-to-all | bytes 8388608 | tf_op jit(solution)/shard_map/all_to_all | solution.py:94
  1757.5 39.9 %all-reduce = (f32[]{:T(128)}, f32[]{:T(128)}, f32[]{:T(128)}) all-reduce(f32[]{:T(128)} %get-tuple-element.119, f32[]{:T(128)} %fusion.203, f32[]{:T(128)} %fusion.133), channel_id=1, replica_groups=mesh['src'=4,'space'=8] {'src','space'}, use_global_device_ids=true, to_apply=%region_15.16 | all-reduce | flops 3 | bytes 24 | tf_op jit(solution)/shard_map/psum | solution.py:101
  1835.8 16.5 reduce-scatter.11.cloned.1.call-done
  1852.3 56.0 %reduce-scatter.9.cloned.1.call-done = f32[2,16,32,256]{3,1,2,0:T(8,128)} async-done(((f32[2,64,32,256]{3,1,2,0:T(8,128)}), f32[2,16,32,256]{3,1,2,0:T(8,128)}) %reduce-scatter.9.cloned.1.call-update) | async-done | bytes 1048592 | tf_op jit(solution)/shard_map/reduce_scatter | solution.py:191
  1917.6 46.1 %all-gather.5.cloned.1.call-done = f32[2,64,32,256]{3,1,2,0:T(8,128)} async-done(((f32[2,16,32,256]{3,1,2,0:T(8,128)}), f32[2,64,32,256]{3,1,2,0:T(8,128)}) %all-gather.5.cloned.1.call-update) | async-done | bytes 4194320 | tf_op jit(solution)/shard_map/all_gather | solution.py:194
  (209 shorter events, 532.3 us)
Async XLA Ops:
  14.1 11.9 copy-start.10
  37.6 100.4 %all-to-all-start = ((f32[1,2,64,32,256]{4,1,3,0,2:T(2,128)}), f32[1,2,64,32,256]{4,1,3,0,2:T(2,128)}, u32[]{:S(2)}, u32[]{:S(2)}) async-start(f32[1,2,64,32,256]{4,1,3,0,2:T(2,128)} %copy.190), calls=%async_computation | async-start | bytes 8388608 | tf_op jit(solution)/shard_map/all_to_all | solution.py:85
  200.4 4.7 copy-start.38
  200.4 121.0 %all-to-all-start.1 = ((f32[1,2,8,256,256]{4,1,2,0,3:T(2,128)}), f32[1,2,8,256,256]{4,1,2,0,3:T(2,128)}, u32[]{:S(2)}, u32[]{:S(2)}) async-start(f32[1,2,8,256,256]{4,1,2,0,3:T(2,128)} %copy.196), calls=%async_computation.1 | async-start | bytes 8388608 | tf_op jit(solution)/shard_map/all_to_all | solution.py:94
  205.1 814.7 %reduce-scatter.7.cloned.1.call-start = ((), (), s32[]{:S(2)}) async-start(), calls=%async_computation.15 | async-start | bytes 2621440 | tf_op jit(solution)/shard_map/reduce_scatter | solution.py:192
  336.1 6.1 copy-start.33
  336.1 6.1 copy-start.11
  336.1 6.1 copy-start.13
  904.9 6.7 copy-start.1
  904.9 6.7 copy-start.12
  904.9 6.7 copy-start.14
  911.6 3.8 copy-start.3
  956.7 4.9 copy-start.17
  983.4 92.0 %reduce-scatter.5.cloned.1.call-start = ((), (), s32[]{:S(2)}) async-start(), calls=%async_computation.14 | async-start | bytes 5242880 | tf_op jit(solution)/shard_map/reduce_scatter | solution.py:191
  983.4 4.6 copy-start.7
  988.1 9.6 copy-start.18
  1000.0 130.7 %all-gather.3.cloned.1.call-start = ((), (), s32[]{:S(2)}) async-start(), calls=%async_computation.16 | async-start | bytes 5242880 | tf_op jit(solution)/shard_map/all_gather | solution.py:194
  1078.0 774.3 %reduce-scatter.11.cloned.1.call-start = ((), (), s32[]{:S(2)}) async-start(), calls=%async_computation.18 | async-start | bytes 2621440 | tf_op jit(solution)/shard_map/reduce_scatter | solution.py:192
  1183.0 12.3 copy-start.4
  1750.4 5.0 copy-start.9
  1816.8 91.5 %reduce-scatter.9.cloned.1.call-start = ((), (), s32[]{:S(2)}) async-start(), calls=%async_computation.17 | async-start | bytes 5242880 | tf_op jit(solution)/shard_map/reduce_scatter | solution.py:191
  1818.4 5.6 copy-start.20
  1824.0 9.2 copy-start.21
  1835.6 128.1 %all-gather.5.cloned.1.call-start = ((), (), s32[]{:S(2)}) async-start(), calls=%async_computation.19 | async-start | bytes 5242880 | tf_op jit(solution)/shard_map/all_gather | solution.py:194
  (23 other events, 51.3 us)
Sparse Core Ops, SparseCore 0:
  983.5 36.2 reduce-scatter.6
  1022.8 52.5 reduce-scatter.4
  1078.2 52.5 all-gather.2
  1816.9 35.3 reduce-scatter.10
  1855.7 52.5 reduce-scatter.8
  1911.1 52.5 all-gather.4
where the time goes:
time: 1990 us; the launch traced here: 1980 us
  blocking collectives  1010 us (51%)
  waiting for transfers between devices  336 us (17%)
  matrix products  314 us (16%)
  other arithmetic  150 us (8%)
  local copies, waits for them, and re-layouts  133 us (7%)
  between operations  22.4 us (1%)
    all_to_all x4, blocking collectives, transform(): lax.all_to_all(returned, 'space', split_axis=3, concat_axis=2, tiled=True)  391 us
    all_to_all x4, blocking collectives, transform(): lax.all_to_all(depth_done, 'space', split_axis=2, concat_axis=3, tiled=True)  388 us
    dot_general x30, matrix products, apply_table(): return jnp.einsum(pattern, table, fields, precision=lax.Precision.HIGHEST)  314 us
    psum x2, blocking collectives, on_device(): lax.psum((data_local, object_local), ('src', 'space'))  153 us
    reduce_scatter x2, waiting for transfers between devices, on_device(): lax.psum_scatter(numerator, 'src', scatter_dimension=1, tiled=True)  112 us
    all_gather x2, waiting for transfers between devices, on_device(): lax.all_gather(bounded(numerator_part, power_part, total_sources), 'src',...  98.8 us
    all_to_all x1, waiting for transfers between devices, transform(): lax.all_to_all(depth_done, 'space', split_axis=2, concat_axis=3, tiled=True)  89.5 us
    psum x2, blocking collectives, descent_total(): return lax.psum(local_sum, ('src', 'space'))  78.3 us
  transfers between devices with their start and end apart: 8, of which 7 were waited for; matrix products, arithmetic and copies ran while one was open for 2% of the time, Pallas kernels for 0%

commit v1 on v0

v1 whole, which is shorter than its diff:
```python
from functools import partial
import math

import jax
import jax.numpy as jnp
import ml_dtypes
import numpy as np
from jax import lax
from jax.experimental import pallas as pl
from jax.experimental.pallas import tpu as pltpu
from jax.sharding import Mesh, PartitionSpec as P

OUTER = 2
WAVENUMBER = 2.0 * math.pi / 6.0
DAMPING = 0.3
SOURCE_GAP = 8.0
FLOOR_SHARE = 0.75
REAL_LOW = -0.25
REAL_HIGH = 0.35
IMAG_HIGH = 0.1
ALL = ("src", "half", "rest")
GROUP = ("src", "rest")
F32 = jnp.float32


def times_const(value, factor):
    re, im = value
    a, b = factor.real, factor.imag
    if abs(b) < 1e-12:
        return (re, im) if abs(a - 1) < 1e-12 else (re * a, im * a)
    if abs(a) < 1e-12:
        return (im * -b, re * b) if abs(abs(b) - 1) > 1e-12 else ((-im, re) if b > 0 else (im, -re))
    if abs(abs(a) - abs(b)) < 1e-12:
        if a * b > 0:
            return ((re - im) * a, (re + im) * a)
        return ((re + im) * a, (im - re) * a)
    return (re * a - im * b, re * b + im * a)


def small_dft(values, sign):
    count = len(values)
    if count == 1:
        return values
    even, odd = small_dft(values[0::2], sign), small_dft(values[1::2], sign)
    low, high = [], []
    for k in range(count // 2):
        turned = times_const(odd[k], np.exp(sign * 2j * math.pi * k / count))
        low.append((even[k][0] + turned[0], even[k][1] + turned[1]))
        high.append((even[k][0] - turned[0], even[k][1] - turned[1]))
    return low + high


def factors(total):
    bits = total.bit_length() - 1
    return 1 << (bits // 2), total // (1 << (bits // 2))


def stage_one(values, n0, count, sign, keep):
    width = len(values)
    for k1, value in enumerate(small_dft(values, sign)):
        re, im = times_const(value, np.exp(sign * 2j * math.pi * n0 * k1 / count))
        keep[n0 * width + k1, 0] = re
        keep[n0 * width + k1, 1] = im


def stage_two(k1, width, count, sign, keep):
    values = [(keep[n0 * width + k1, 0], keep[n0 * width + k1, 1]) for n0 in range(count // width)]
    return small_dft(values, sign)


def pair(ref, s, z):
    return ref[s, z, 0, 0], ref[s, z, 1, 0]


def put(ref, s, z, value):
    ref[s, z, 0, 0] = value[0]
    ref[s, z, 1, 0] = value[1]


def cell(ref, z):
    return ref[0, z, 0], ref[1, z, 0]


def start_kernel(chi, inc, source, spec, keep):
    sources, depth = inc.shape[:2]
    width, rest = factors(depth)

    def body(s, _):
        for n0 in range(rest):
            values = []
            for n1 in range(width):
                z = n0 + rest * n1
                cr, ci = cell(chi, z)
                er, ei = pair(inc, s, z)
                w = (cr * er - ci * ei, cr * ei + ci * er)
                put(source, s, z, w)
                values.append(w)
            stage_one(values, n0, depth, -1, keep)
        for k1 in range(width):
            for k0, value in enumerate(stage_two(k1, width, depth, -1, keep)):
                put(spec, s, k1 + width * k0, value)
        return 0

    lax.fori_loop(0, sources, body, 0)


def adjoint_kernel(first, scal, field, chi, inc, source, data, *rest_refs):
    if first:
        scat_out, resid, spec, keep_in, keep = rest_refs
    else:
        resid, spec, keep = rest_refs
    sources, depth = inc.shape[:2]
    width, rest = factors(depth)
    object_weight, data_weight = scal[0, 0], scal[0, 1]

    def body(s, _):
        if first:
            for n0 in range(rest):
                stage_one([pair(field, s, n0 + rest * n1) for n1 in range(width)], n0, depth, 1, keep_in)
        for k1 in range(width):
            scattered = stage_two(k1, width, depth, 1, keep_in) if first else None
            values = []
            for k0 in range(rest):
                z = k1 + width * k0
                if first:
                    sr, si = scattered[k0]
                    put(scat_out, s, z, (sr, si))
                else:
                    sr, si = pair(field, s, z)
                cr, ci = cell(chi, z)
                er, ei = pair(inc, s, z)
                wr, wi = pair(source, s, z)
                ur, ui = er + sr, ei + si
                rr = cr * ur - ci * ui - wr
                ri = cr * ui + ci * ur - wi
                put(resid, s, z, (rr, ri))
                vr = -object_weight * (cr * rr + ci * ri)
                vi = -object_weight * (cr * ri - ci * rr)
                if z == 0:
                    vr = vr + data_weight * (data[s, 0, 0] - sr)
                    vi = vi + data_weight * (data[s, 1, 0] - si)
                values.append((vr, vi))
            stage_one(values, k1, depth, -1, keep)
        for j1 in range(rest):
            for j0, value in enumerate(stage_two(j1, rest, depth, -1, keep)):
                put(spec, s, j1 + rest * j0, value)
        return 0

    lax.fori_loop(0, sources, body, 0)


def descent_kernel(scal, field, resid, descent, spec, sums, keep_in, keep):
    sources, depth = resid.shape[:2]
    width, rest = factors(depth)
    object_weight = scal[0, 0]

    def body(s, total):
        for n0 in range(rest):
            stage_one([pair(field, s, n0 + rest * n1) for n1 in range(width)], n0, depth, 1, keep_in)
        for k1 in range(width):
            values = []
            for k0, (gr, gi) in enumerate(stage_two(k1, width, depth, 1, keep_in)):
                z = k1 + width * k0
                rr, ri = pair(resid, s, z)
                dr, di = gr + object_weight * rr, gi + object_weight * ri
                put(descent, s, z, (dr, di))
                total = total + (dr * dr + di * di)
                values.append((dr, di))
            stage_one(values, k1, depth, -1, keep)
        for j1 in range(rest):
            for j0, value in enumerate(stage_two(j1, rest, depth, -1, keep)):
                put(spec, s, j1 + rest * j0, value)
        return total

    sums[0, 0, 0] = lax.fori_loop(0, sources, body, jnp.zeros(sums.shape[3:], F32))


def image_kernel(field, descent, chi, image, sums, keep_in):
    sources, depth = descent.shape[:2]
    width, rest = factors(depth)

    def body(s, totals):
        change, plane = totals
        for n0 in range(rest):
            stage_one([pair(field, s, n0 + rest * n1) for n1 in range(width)], n0, depth, 1, keep_in)
        for k1 in range(width):
            for k0, (hr, hi) in enumerate(stage_two(k1, width, depth, 1, keep_in)):
                z = k1 + width * k0
                put(image, s, z, (hr, hi))
                dr, di = pair(descent, s, z)
                cr, ci = cell(chi, z)
                qr = dr - (cr * hr - ci * hi)
                qi = di - (cr * hi + ci * hr)
                change = change + (qr * qr + qi * qi)
                if z == 0:
                    plane = plane + (hr * hr + hi * hi)
        return change, plane

    zero = jnp.zeros(sums.shape[3:], F32)
    change, plane = lax.fori_loop(0, sources, body, (zero, zero))
    sums[0, 0, 0] = change
    sums[0, 0, 1] = plane


def step_kernel(last, scal, source, descent, scattered, image, inc, source_out, *rest_refs):
    if last:
        (parts,) = rest_refs
    else:
        scat_out, parts = rest_refs
    sources, depth = inc.shape[:2]
    step = scal[0, 0]

    def body(z, _):
        nr = ni = power = None
        for s in range(sources):
            wr, wi = pair(source, s, z)
            dr, di = pair(descent, s, z)
            wr, wi = wr + step * dr, wi + step * di
            put(source_out, s, z, (wr, wi))
            sr, si = pair(scattered, s, z)
            hr, hi = pair(image, s, z)
            sr, si = sr + step * hr, si + step * hi
            if not last:
                put(scat_out, s, z, (sr, si))
            er, ei = pair(inc, s, z)
            ur, ui = er + sr, ei + si
            a, b, c = wr * ur + wi * ui, wi * ur - wr * ui, ur * ur + ui * ui
            nr, ni, power = (a, b, c) if s == 0 else (nr + a, ni + b, power + c)
        parts[0, 0, z] = nr
        parts[0, 1, z] = ni
        parts[0, 2, z] = power
        return 0

    lax.fori_loop(0, depth, body, 0, unroll=4)


def half_tables(total, order):
    half = total // 2
    modes = np.arange(half)[:, None]
    place = np.asarray(order)[None, :]
    out = []
    for odd in (0, 1):
        angle = 2.0 * math.pi * ((2 * modes + odd) * place % total) / total
        cosine, sine = np.cos(angle), np.sin(angle)
        out.append(np.block([[cosine, sine], [-sine, cosine]]).astype(np.float32))
    return np.stack(out)


def high_low(table):
    high = table.astype(ml_dtypes.bfloat16)
    low = (table - high.astype(np.float32)).astype(ml_dtypes.bfloat16)
    return np.stack([high, low])


def lateral_modes(total):
    index = np.concatenate([np.arange(0, total, 2), np.arange(1, total, 2)])
    return (4.0 * np.sin(math.pi * index / total) ** 2).astype(np.float32)


def split(value):
    high = value.astype(jnp.bfloat16)
    return high, (value - high.astype(F32)).astype(jnp.bfloat16)


def left_mul(table, odd, value):
    high, low = split(value)
    return jnp.dot(
        jnp.concatenate([table[0, odd], table[0, odd], table[1, odd]], axis=1),
        jnp.concatenate([high, low, high], axis=0),
        preferred_element_type=F32,
    )


def right_mul(value, table, odd):
    high, low = split(value)
    return jnp.dot(
        jnp.concatenate([high, low, high], axis=1),
        jnp.concatenate([table[0, odd], table[0, odd], table[1, odd]], axis=0),
        preferred_element_type=F32,
    )


def plane_kernel(sign, scale, lz, lx, ly, xf, xb, yf, yb, planes, out):
    senders, _, _, _, rows, ny = planes.shape
    hx, hy = senders * rows, ny // 2
    own = [planes[:, 0, c, 0].reshape(hx, ny) for c in (0, 1)]
    other = [planes[:, 0, c, 1].reshape(hx, ny) for c in (0, 1)]
    across = [
        left_mul(xf, 0, jnp.concatenate([own[0] + other[0], own[1] + other[1]], axis=0)),
        left_mul(xf, 1, jnp.concatenate([own[0] - other[0], own[1] - other[1]], axis=0)),
    ]
    real = jnp.concatenate([across[0][:hx], across[1][:hx]], axis=0)
    imag = jnp.concatenate([across[0][hx:], across[1][hx:]], axis=0)
    wave_sq = WAVENUMBER * WAVENUMBER
    back = []
    for odd in (0, 1):
        flip = -1.0 if odd else 1.0
        folded = jnp.concatenate(
            [real[:, :hy] + flip * real[:, hy:], imag[:, :hy] + flip * imag[:, hy:]], axis=1
        )
        freq = right_mul(folded, yf, odd)
        eigen = (lx[...] + lz[pl.program_id(0)]) + ly[odd]
        real_den = eigen - wave_sq
        imag_den = wave_sq * DAMPING
        factor = (wave_sq * scale) / (real_den * real_den + imag_den * imag_den)
        gr, gi = factor * real_den, factor * (imag_den * sign)
        fr, fi = freq[:, :hy], freq[:, hy:]
        filtered = jnp.concatenate([fr * gr - fi * gi, fr * gi + fi * gr], axis=1)
        back.append(right_mul(filtered, yb, odd))
    plus, minus = back[0] + back[1], back[0] - back[1]
    real = jnp.concatenate([plus[:, :hy], minus[:, :hy]], axis=1)
    imag = jnp.concatenate([plus[:, hy:], minus[:, hy:]], axis=1)
    even = left_mul(xb, 0, jnp.concatenate([real[:hx], imag[:hx]], axis=0))
    odd = left_mul(xb, 1, jnp.concatenate([real[hx:], imag[hx:]], axis=0))
    plus, minus = even + odd, even - odd
    for c in (0, 1):
        out[:, 0, c, 0] = plus[c * hx : (c + 1) * hx].reshape(senders, rows, ny)
        out[:, 0, c, 1] = minus[c * hx : (c + 1) * hx].reshape(senders, rows, ny)


SMEM = pl.BlockSpec(memory_space=pltpu.SMEM)


class Slabs:
    def __init__(self, sources, depth, rows, ny):
        self.sources, self.depth, self.rows, self.ny = sources, depth, rows, ny
        self.lanes = 128 if ny % 128 == 0 else ny
        self.grid = (2, ny // self.lanes)

    def kind(self, name):
        s, z, q, y, lanes = self.sources, self.depth, self.rows, self.ny, self.lanes
        return {
            "field": ((s, z, 2, 2, q, y), (s, z, 2, 1, q, lanes), lambda i, j: (0, 0, 0, i, 0, j)),
            "chi": ((2, z, 2, q, y), (2, z, 1, q, lanes), lambda i, j: (0, 0, i, 0, j)),
            "data": ((s, 2, 2, q, y), (s, 2, 1, q, lanes), lambda i, j: (0, 0, i, 0, j)),
            "parts": ((2, 3, z, q, y), (1, 3, z, q, lanes), lambda i, j: (i, 0, 0, 0, j)),
            "sum1": (self.grid + (1, q, lanes), (1, 1, 1, q, lanes), lambda i, j: (i, j, 0, 0, 0)),
            "sum2": (self.grid + (2, q, lanes), (1, 1, 2, q, lanes), lambda i, j: (i, j, 0, 0, 0)),
        }[name]

    def call(self, kernel, name, ins, outs, scratch, *args):
        def spec(kind):
            if kind == "scal":
                return SMEM
            _, block, index = self.kind(kind)
            return pl.BlockSpec(block, index)

        moved = sum(math.prod(self.kind(k)[0]) * 4 for k in (*ins, *outs) if k != "scal")
        return pl.pallas_call(
            kernel,
            grid=self.grid,
            in_specs=[spec(k) for k in ins],
            out_specs=[spec(k) for k in outs],
            out_shape=[jax.ShapeDtypeStruct(self.kind(k)[0], F32) for k in outs],
            scratch_shapes=[pltpu.VMEM((self.depth, 2, self.rows, self.lanes), F32)] * scratch,
            cost_estimate=pl.CostEstimate(flops=moved * 4, bytes_accessed=moved, transcendentals=0),
            name=name,
        )(*args)


def filter_planes(spectrum, senders, lz, shared, sign, scale):
    _, parts, chunks, rows, ny = spectrum.shape
    planes = spectrum.shape[0] // senders
    shape = (senders, planes, parts, chunks, rows, ny)
    spectrum = spectrum.reshape(shape)
    dense = rows % 8 != 0
    if dense:
        spectrum = spectrum.transpose(1, 2, 3, 0, 4, 5).reshape(1, planes, parts, chunks, senders * rows, ny)
    block = (spectrum.shape[0], 1) + spectrum.shape[2:]
    at = lambda i: (0, i, 0, 0, 0, 0)
    whole = lambda t: pl.BlockSpec(t.shape, lambda i, n=t.ndim: (0,) * n)
    nx = 2 * senders * rows
    out = pl.pallas_call(
        partial(plane_kernel, sign, scale),
        grid=(planes,),
        in_specs=[SMEM] + [whole(t) for t in shared] + [pl.BlockSpec(block, at)],
        out_specs=pl.BlockSpec(block, at),
        out_shape=jax.ShapeDtypeStruct(spectrum.shape, F32),
        cost_estimate=pl.CostEstimate(
            flops=planes * 24 * nx * nx * ny * 2, bytes_accessed=2 * spectrum.size * 4, transcendentals=0
        ),
        name="planes",
    )(lz, *shared, spectrum)
    if dense:
        out = out.reshape(planes, parts, chunks, senders, rows, ny).transpose(3, 0, 1, 2, 4, 5)
    return out.reshape(senders * planes, parts, chunks, rows, ny)


def everyone(values):
    count = math.prod(lax.axis_size(name) for name in ALL)
    row = jnp.zeros((128,), F32).at[: len(values)].set(jnp.stack(values))
    sent = jnp.broadcast_to(row[None], (count, 128))
    return jnp.sum(lax.all_to_all(sent, ALL, 0, 0, tiled=True), axis=0)


def swap_halves(value):
    return lax.ppermute(value, "half", [(0, 1), (1, 0)])


def bounded(numer_real, numer_imag, power, total_sources):
    floored = jnp.maximum(power, FLOOR_SHARE * total_sources)
    return jnp.stack(
        [
            jnp.clip(numer_real / floored, REAL_LOW, REAL_HIGH),
            jnp.clip(numer_imag / floored, 0.0, IMAG_HIGH),
        ]
    )


def on_device(contrast, measured, positions):
    shares, rest_count = lax.axis_size("src"), lax.axis_size("rest")
    share, half, rest = (lax.axis_index(name) for name in ALL)
    senders = shares * rest_count
    _, depth, block_rows, ny = contrast.shape
    rows = block_rows // shares
    nx = block_rows * 2 * rest_count
    per_share = positions.shape[0]
    total_sources = per_share * shares
    sources = total_sources // 2
    slabs = Slabs(sources, depth, rows, ny)

    chi_own = lax.dynamic_index_in_dim(
        contrast.reshape(2, depth, shares, rows, ny), share, axis=2, keepdims=False
    )
    chi_other = swap_halves(chi_own)

    sent = jnp.concatenate(
        [
            measured.reshape(per_share, 2, shares, rows * ny).transpose(2, 0, 1, 3).reshape(shares, -1),
            jnp.broadcast_to(jnp.pad(positions.astype(F32).reshape(1, -1), ((0, 0), (0, 126))), (shares, 2 * per_share + 126)),
        ],
        axis=1,
    )
    got = lax.all_to_all(sent, "src", 0, 0, tiled=True)
    cells = per_share * 2 * rows * ny
    data_own = got[:, :cells].reshape(total_sources, 2, rows, ny)
    spots = got[:, cells : cells + 2 * per_share].reshape(total_sources, 2)
    mine = lambda v, h: lax.dynamic_slice_in_dim(v, h * sources, sources, axis=0)
    data = jnp.stack([mine(data_own, half), swap_halves(mine(data_own, 1 - half))], axis=2)
    spots = mine(spots, half)

    heights = jnp.arange(depth).astype(F32) + SOURCE_GAP
    starts = (jnp.stack([half, 1 - half]) * rest_count + rest) * block_rows + share * rows
    across = (starts[:, None] + jnp.arange(rows)[None, :]).astype(F32)
    offset_x = across[None] - spots[:, 0][:, None, None]
    offset_y = jnp.arange(ny).astype(F32)[None] - spots[:, 1][:, None]
    dist_sq = (heights * heights)[None, :, None, None, None] + (offset_x * offset_x)[:, None, :, :, None]
    dist_sq = dist_sq + (offset_y * offset_y)[:, None, None, None, :]
    phases = WAVENUMBER * jnp.sqrt(dist_sq)
    inc = jnp.stack([jnp.cos(phases), jnp.sin(phases)], axis=2)

    order = [(k * shares + a) * rows + q for a in range(shares) for k in range(rest_count) for q in range(rows)]
    x_table, y_table = half_tables(nx, order), half_tables(ny, range(ny // 2))
    flip = lambda t: high_low(np.swapaxes(t, -1, -2))
    lx = np.broadcast_to(lateral_modes(nx)[:, None], (nx, ny // 2))
    ly = lateral_modes(ny).reshape(2, 1, ny // 2)
    shared = [jnp.asarray(t) for t in (lx, ly, high_low(x_table), flip(x_table), flip(y_table), high_low(y_table))]
    planes = sources * depth // senders
    place = share * rest_count + rest
    modes = (place * planes + jnp.arange(planes)) % depth
    half_sine = jnp.sin(math.pi * modes.astype(F32) / depth)
    lz = 4.0 * half_sine * half_sine
    scale = 1.0 / (nx * ny * depth)

    def convolve(spec, sign):
        flat = spec.reshape(sources * depth, 2, 2, rows, ny)
        flat = lax.all_to_all(flat, GROUP, 0, 0, tiled=True)
        flat = filter_planes(flat, senders, lz, shared, sign, scale)
        return lax.all_to_all(flat, GROUP, 0, 0, tiled=True).reshape(spec.shape)

    totals = everyone([jnp.sum(measured * measured), total_sources * jnp.sum(chi_own * chi_own)])
    data_weight = 1.0 / totals[0]
    object_total = totals[1]
    chi = jnp.stack([chi_own, chi_other], axis=2)
    source, spec = slabs.call(start_kernel, "start", ("chi", "field"), ("field", "field"), 1, chi, inc)
    scattered = convolve(spec, 1.0)
    for outer in range(OUTER):
        object_weight = 1.0 / object_total
        weights = jnp.stack([object_weight, data_weight]).reshape(1, 2)
        first, last = outer == 0, outer == OUTER - 1
        out = slabs.call(
            partial(adjoint_kernel, first),
            "adjoint",
            ("scal", "field", "chi", "field", "field", "data"),
            ("field",) * (3 if first else 2),
            2 if first else 1,
            weights, scattered, chi, inc, source, data,
        )
        if first:
            scattered, resid, spec = out
        else:
            resid, spec = out
        descent, spec, sum_d = slabs.call(
            descent_kernel, "descent", ("scal", "field", "field"), ("field", "field", "sum1"), 2,
            weights, convolve(spec, -1.0), resid,
        )
        image, sum_q = slabs.call(
            image_kernel, "image", ("field", "field", "chi"), ("field", "sum2"), 1,
            convolve(spec, 1.0), descent, chi,
        )
        totals = everyone([jnp.sum(sum_d), jnp.sum(sum_q[:, :, 0]), jnp.sum(sum_q[:, :, 1])])
        step = totals[0] / (data_weight * totals[2] + object_weight * totals[1])
        out = slabs.call(
            partial(step_kernel, last),
            "step",
            ("scal",) + ("field",) * 5,
            ("field",) * (1 if last else 2) + ("parts",),
            0,
            step.reshape(1, 1), source, descent, scattered, image, inc,
        )
        if last:
            source, parts = out
        else:
            source, scattered, parts = out
        sums = parts[0] + swap_halves(parts[1])
        chi_own = bounded(sums[0], sums[1], sums[2], total_sources)
        if not last:
            chi = jnp.stack([chi_own, swap_halves(chi_own)], axis=2)
            object_total = everyone([total_sources * jnp.sum(chi_own * chi_own)])[0]

    own, theirs = source[:, :, :, 0], swap_halves(source[:, :, :, 1])
    lower, upper = jnp.where(half == 0, own, theirs), jnp.where(half == 0, theirs, own)
    fields = jnp.concatenate([lower, upper], axis=0)
    fields = lax.all_to_all(fields, "src", 0, 0, tiled=True)
    fields = fields.reshape(shares, per_share, depth, 2, rows, ny).transpose(1, 3, 2, 0, 4, 5)
    fields = fields.reshape(per_share, 2, depth, block_rows, ny)
    sent = jnp.broadcast_to(chi_own[None], (shares,) + chi_own.shape)
    contrast_new = lax.all_to_all(sent, "src", 0, 0, tiled=True)
    contrast_new = contrast_new.transpose(1, 2, 0, 3, 4).reshape(contrast.shape)
    return fields, contrast_new


def solution(mesh):
    shares, spaces = mesh.shape["src"], mesh.shape["space"]
    split_mesh = Mesh(mesh.devices.reshape(shares, 2, spaces // 2), ALL)
    space = ("half", "rest")
    return jax.shard_map(
        on_device,
        mesh=split_mesh,
        in_specs=(P(None, None, space, None), P("src", None, space, None), P("src", None)),
        out_specs=(P("src", None, None, space, None), P(None, None, space, None)),
        check_vma=False,
    )
```

time: 1990 us -> 1180 us (0.59)
  blocking collectives: 1010 us -> 399 us
  matrix products: 314 us -> 0 us
  waiting for transfers between devices: 336 us -> 508 us
  Pallas kernels: 0 us -> 157 us
  other arithmetic: 150 us -> 34.3 us
  local copies, waits for them, and re-layouts: 133 us -> 24 us
  starting transfers between devices: 11.6 us -> 47.5 us
    all_to_all x8 -> x9, blocking collectives: 778 us -> 399 us  [the longest x4 220 us: convolve(): flat = lax.all_to_all(flat, GROUP, 0, 0, tiled=True)]
    dot_general x30 -> x0, matrix products: 314 us -> none  [apply_table(): return jnp.einsum(pattern, table, fields, precision=lax.Precision.HIGHEST)]
    ppermute x0 -> x6, waiting for transfers between devices: none -> 313 us  [swap_halves(): return lax.ppermute(value, 'half', [(0, 1), (1, 0)])]
    psum x4 -> x0, blocking collectives: 232 us -> none  [the longest x2 153 us: on_device(): lax.psum((data_local, object_local), ('src', 'space'))]
    pallas_call x0 -> x14, Pallas kernels: none -> 157 us  [the longest x9 83.3 us: call(): pl.pallas_call(kernel, grid=self.grid, in_specs=[spec(k) for k in ins], o...]
    reduce_scatter x4 -> x0, waiting for transfers between devices: 148 us -> none  [the longest x2 112 us: on_device(): lax.psum_scatter(numerator, 'src', scatter_dimension=1, tiled=True)]
    all_to_all x2 -> x8, waiting for transfers between devices: 89.5 us -> 195 us  [the longest x3 103 us: convolve(): return lax.all_to_all(flat, GROUP, 0, 0, tiled=True).reshape(spec.shape)]
    all_gather x2 -> x0, waiting for transfers between devices: 98.8 us -> none  [on_device(): lax.all_gather(bounded(numerator_part, power_part, total_sources), 'src',...]
  transfers between devices with their start and end apart: 8 -> 14, of which waited for: 7 -> 9; matrix products, arithmetic and copies ran while one was open for 2% -> 3% of each run, Pallas kernels for 0% -> 1%
where the time goes in v1:
time: 1180 us
  waiting for transfers between devices  508 us (43%)
  blocking collectives  399 us (34%)
  Pallas kernels  157 us (13%)
  starting transfers between devices  47.5 us (4%)
  other arithmetic  34.3 us (3%)
  local copies, waits for them, and re-layouts  24 us (2%)
    ppermute x6, waiting for transfers between devices, swap_halves(): return lax.ppermute(value, 'half', [(0, 1), (1, 0)])  313 us
    all_to_all x4, blocking collectives, convolve(): flat = lax.all_to_all(flat, GROUP, 0, 0, tiled=True)  220 us
    all_to_all x2, blocking collectives, convolve(): return lax.all_to_all(flat, GROUP, 0, 0, tiled=True).reshape(spec.shape)  109 us
    all_to_all x3, waiting for transfers between devices, convolve(): return lax.all_to_all(flat, GROUP, 0, 0, tiled=True).reshape(spec.shape)  103 us
    pallas_call x9, Pallas kernels, call(): pl.pallas_call(kernel, grid=self.grid, in_specs=[spec(k) for k in ins], o...  83.3 us
    pallas_call x5, Pallas kernels, filter_planes(): pl.pallas_call(partial(plane_kernel, sign, scale), grid=(planes,), in_spe...  74.2 us
    all_to_all x3, blocking collectives, everyone(): return jnp.sum(lax.all_to_all(sent, ALL, 0, 0, tiled=True), axis=0)  70.5 us
    all_to_all x1, waiting for transfers between devices, convolve(): flat = lax.all_to_all(flat, GROUP, 0, 0, tiled=True)  49.4 us
  transfers between devices with their start and end apart: 14, of which 9 were waited for; matrix products, arithmetic and copies ran while one was open for 3% of the time, Pallas kernels for 1%

profile of v1, /device:TPU:0, one launch (start us, length us, event | category | flops | bytes accessed | tf_op | source)
XLA Modules:
  0.0 1177.8 jit_solution(4594728583776470347)
XLA Ops:
  24.3 34.1 %collective-permute-done = f32[2,64,8,256]{3,2,1,0:T(8,128)S(1)} collective-permute-done((f32[2,64,8,256]{3,2,1,0:T(8,128)S(1)}, f32[2,64,8,256]{3,2,1,0:T(8,128)S(1)}, u32[]{:S(2)}, u32[]{:S(2)}) %collective-permute-start) | collective-permute-done | bytes 1048608 | tf_op jit(solution)/shard_map/ppermute | solution.py:397
  74.5 49.4 %all-to-all-done.2 = f32[128,2,2,8,256]{4,3,2,1,0:T(8,128)} async-done(((f32[128,2,2,8,256]{4,3,2,1,0:T(8,128)}), f32[128,2,2,8,256]{4,3,2,1,0:T(8,128)}, u32[]{:S(2)}, u32[]{:S(2)}) %all-to-all-start.2) | async-done | bytes 4194336 | tf_op jit(solution)/shard_map/all_to_all | solution.py:467
  132.7 14.9 %planes.5 = f32[16,8,2,2,8,256]{5,4,3,2,1,0:T(8,128)} custom-call(f32[8]{0:T(128)} %multiply_multiply_fusion.lz, f32[256,128]{1,0:T(8,128)} %jit_solution_.3.lx, f32[2,1,128]{2,1,0:T(1,128)} %constant.179.clone.ly, bf16[2,2,256,256]{3,2,1,0:T(8,128)(2,1)} %constant.180.clone.xf, bf16[2,2,256,256]{3,2,1,0:T(8,128)(2,1)} %constant.181.clone.xb, ...), custom_call_target="tpu_custom_call" | custom-call | flops 6442450944 | bytes 8388608 | tf_op jit(solution)/shard_map/planes/pallas_call | solution.py:373
  157.6 47.6 %collective-permute-done.1 = f32[2,2,8,256]{3,2,1,0:T(8,128)S(1)} collective-permute-done((f32[2,2,8,256]{3,2,1,0:T(8,128)S(1)}, f32[2,2,8,256]{3,2,1,0:T(8,128)S(1)}, u32[]{:S(2)}, u32[]{:S(2)}) %collective-permute-start.1) | collective-permute-done | bytes 32800 | tf_op jit(solution)/shard_map/ppermute | solution.py:397
  217.4 56.6 %all_to_all.96 = f32[128,2,2,8,256]{4,3,2,1,0:T(8,128)} all-to-all(f32[128,2,2,8,256]{4,3,2,1,0:T(8,128)} %bitcast.109), channel_id=1, replica_groups=mesh['src'=4,'half'=2,'rest'=4] {'src','rest'}, dimensions={0} | all-to-all | bytes 8388608 | tf_op jit(solution)/shard_map/all_to_all | solution.py:467
  274.0 14.9 %planes.6 = f32[16,8,2,2,8,256]{5,4,3,2,1,0:T(8,128)} custom-call(f32[8]{0:T(128)} %multiply_multiply_fusion.lz, f32[256,128]{1,0:T(8,128)} %jit_solution_.3.lx, f32[2,1,128]{2,1,0:T(1,128)} %constant.179.clone.ly, bf16[2,2,256,256]{3,2,1,0:T(8,128)(2,1)} %constant.180.clone.xf, bf16[2,2,256,256]{3,2,1,0:T(8,128)(2,1)} %constant.181.clone.xb, ...), custom_call_target="tpu_custom_call" | custom-call | flops 6442450944 | bytes 8388608 | tf_op jit(solution)/shard_map/planes/pallas_call | solution.py:373
  288.8 54.4 %all_to_all.97 = f32[128,2,2,8,256]{4,3,2,1,0:T(8,128)} all-to-all(f32[128,2,2,8,256]{4,3,2,1,0:T(8,128)} %bitcast.112), channel_id=1, replica_groups=mesh['src'=4,'half'=2,'rest'=4] {'src','rest'}, dimensions={0} | all-to-all | bytes 8388608 | tf_op jit(solution)/shard_map/all_to_all | solution.py:469
  351.9 54.4 %all_to_all.98 = f32[128,2,2,8,256]{4,3,2,1,0:T(8,128)} all-to-all(f32[128,2,2,8,256]{4,3,2,1,0:T(8,128)} %bitcast.107), channel_id=1, replica_groups=mesh['src'=4,'half'=2,'rest'=4] {'src','rest'}, dimensions={0} | all-to-all | bytes 8388608 | tf_op jit(solution)/shard_map/all_to_all | solution.py:467
  406.3 14.8 %planes.7 = f32[16,8,2,2,8,256]{5,4,3,2,1,0:T(8,128)} custom-call(f32[8]{0:T(128)} %multiply_multiply_fusion.lz, f32[256,128]{1,0:T(8,128)} %jit_solution_.3.lx, f32[2,1,128]{2,1,0:T(1,128)} %constant.179.clone.ly, bf16[2,2,256,256]{3,2,1,0:T(8,128)(2,1)} %constant.180.clone.xf, bf16[2,2,256,256]{3,2,1,0:T(8,128)(2,1)} %constant.181.clone.xb, ...), custom_call_target="tpu_custom_call" | custom-call | flops 6442450944 | bytes 8388608 | tf_op jit(solution)/shard_map/planes/pallas_call | solution.py:373
  426.5 51.5 %all-to-all-done.7 = f32[128,2,2,8,256]{4,3,2,1,0:T(8,128)} async-done(((f32[128,2,2,8,256]{4,3,2,1,0:T(8,128)}), f32[128,2,2,8,256]{4,3,2,1,0:T(8,128)}, u32[]{:S(2)}, u32[]{:S(2)}) %all-to-all-start.7) | async-done | bytes 4194336 | tf_op jit(solution)/shard_map/all_to_all | solution.py:469
  488.7 12.3 %all_to_all.99 = f32[32,1,128]{2,1,0:T(1,128)S(1)} all-to-all(f32[32,1,128]{2,1,0:T(1,128)S(1)} %broadcast_in_dim.17), channel_id=1, replica_groups=mesh['src'=4,'half'=2,'rest'=4] {'src','half','rest'}, dimensions={0} | all-to-all | bytes 32768 | tf_op jit(solution)/shard_map/all_to_all | solution.py:393
  503.6 11.7 step.2
  517.6 70.2 %collective-permute-done.2 = f32[3,64,8,256]{3,2,1,0:T(8,128)S(1)} collective-permute-done((f32[3,64,8,256]{3,2,1,0:T(8,128)S(1)}, f32[3,64,8,256]{3,2,1,0:T(8,128)S(1)}, u32[]{:S(2)}, u32[]{:S(2)}) %collective-permute-start.2) | collective-permute-done | bytes 1572896 | tf_op jit(solution)/shard_map/ppermute | solution.py:397
  589.7 45.1 %all_to_all.100 = f32[32,1,128]{2,1,0:T(1,128)S(1)} all-to-all(f32[32,1,128]{2,1,0:T(1,128)S(1)} %broadcast_in_dim.18), channel_id=1, replica_groups=mesh['src'=4,'half'=2,'rest'=4] {'src','half','rest'}, dimensions={0} | all-to-all | bytes 32768 | tf_op jit(solution)/shard_map/all_to_all | solution.py:393
  647.1 54.4 %all_to_all.101 = f32[128,2,2,8,256]{4,3,2,1,0:T(8,128)} all-to-all(f32[128,2,2,8,256]{4,3,2,1,0:T(8,128)} %bitcast.110), channel_id=1, replica_groups=mesh['src'=4,'half'=2,'rest'=4] {'src','rest'}, dimensions={0} | all-to-all | bytes 8388608 | tf_op jit(solution)/shard_map/all_to_all | solution.py:467
  701.5 14.8 %planes.8 = f32[16,8,2,2,8,256]{5,4,3,2,1,0:T(8,128)} custom-call(f32[8]{0:T(128)} %multiply_multiply_fusion.lz, f32[256,128]{1,0:T(8,128)} %jit_solution_.3.lx, f32[2,1,128]{2,1,0:T(1,128)} %constant.179.clone.ly, bf16[2,2,256,256]{3,2,1,0:T(8,128)(2,1)} %constant.180.clone.xf, bf16[2,2,256,256]{3,2,1,0:T(8,128)(2,1)} %constant.181.clone.xb, ...), custom_call_target="tpu_custom_call" | custom-call | flops 6442450944 | bytes 8388608 | tf_op jit(solution)/shard_map/planes/pallas_call | solution.py:373
  716.3 54.4 %all_to_all.102 = f32[128,2,2,8,256]{4,3,2,1,0:T(8,128)} all-to-all(f32[128,2,2,8,256]{4,3,2,1,0:T(8,128)} %bitcast.115), channel_id=1, replica_groups=mesh['src'=4,'half'=2,'rest'=4] {'src','rest'}, dimensions={0} | all-to-all | bytes 8388608 | tf_op jit(solution)/shard_map/all_to_all | solution.py:469
  779.7 54.4 %all_to_all.103 = f32[128,2,2,8,256]{4,3,2,1,0:T(8,128)} all-to-all(f32[128,2,2,8,256]{4,3,2,1,0:T(8,128)} %bitcast.108), channel_id=1, replica_groups=mesh['src'=4,'half'=2,'rest'=4] {'src','rest'}, dimensions={0} | all-to-all | bytes 8388608 | tf_op jit(solution)/shard_map/all_to_all | solution.py:467
  834.1 14.8 %planes.9 = f32[16,8,2,2,8,256]{5,4,3,2,1,0:T(8,128)} custom-call(f32[8]{0:T(128)} %multiply_multiply_fusion.lz, f32[256,128]{1,0:T(8,128)} %jit_solution_.3.lx, f32[2,1,128]{2,1,0:T(1,128)} %constant.179.clone.ly, bf16[2,2,256,256]{3,2,1,0:T(8,128)(2,1)} %constant.180.clone.xf, bf16[2,2,256,256]{3,2,1,0:T(8,128)(2,1)} %constant.181.clone.xb, ...), custom_call_target="tpu_custom_call" | custom-call | flops 6442450944 | bytes 8388608 | tf_op jit(solution)/shard_map/planes/pallas_call | solution.py:373
  854.3 51.5 %all-to-all-done.13 = f32[128,2,2,8,256]{4,3,2,1,0:T(8,128)} async-done(((f32[128,2,2,8,256]{4,3,2,1,0:T(8,128)}), f32[128,2,2,8,256]{4,3,2,1,0:T(8,128)}, u32[]{:S(2)}, u32[]{:S(2)}) %all-to-all-start.13) | async-done | bytes 4194336 | tf_op jit(solution)/shard_map/all_to_all | solution.py:469
  916.4 13.0 %all_to_all.104 = f32[32,1,128]{2,1,0:T(1,128)S(1)} all-to-all(f32[32,1,128]{2,1,0:T(1,128)S(1)} %broadcast_in_dim.19), channel_id=1, replica_groups=mesh['src'=4,'half'=2,'rest'=4] {'src','half','rest'}, dimensions={0} | all-to-all | bytes 32768 | tf_op jit(solution)/shard_map/all_to_all | solution.py:393
  944.8 70.2 %collective-permute-done.5 = f32[3,64,8,256]{3,2,1,0:T(8,128)S(1)} collective-permute-done((f32[3,64,8,256]{3,2,1,0:T(8,128)S(1)}, f32[3,64,8,256]{3,2,1,0:T(8,128)S(1)}, u32[]{:S(2)}, u32[]{:S(2)}) %collective-permute-start.5) | collective-permute-done | bytes 1572896 | tf_op jit(solution)/shard_map/ppermute | solution.py:397
  1024.6 90.5 %collective-permute-done.4 = f32[2,64,2,8,256]{4,3,2,1,0:T(8,128)} collective-permute-done((f32[2,64,2,8,256]{4,3,2,1,0:T(8,128)S(1)}, f32[2,64,2,8,256]{4,3,2,1,0:T(8,128)}, u32[]{:S(2)}, u32[]{:S(2)}) %collective-permute-start.4) | collective-permute-done | bytes 2097184 | tf_op jit(solution)/shard_map/ppermute | solution.py:397
  1129.9 43.0 %all-to-all-done.15 = f32[4,64,2,8,256]{4,3,2,1,0:T(8,128)} async-done(((f32[4,64,2,8,256]{4,3,2,1,0:T(8,128)}), f32[4,64,2,8,256]{4,3,2,1,0:T(8,128)}, u32[]{:S(2)}, u32[]{:S(2)}) %all-to-all-start.15) | async-done | bytes 4194336 | tf_op jit(solution)/shard_map/all_to_all | solution.py:524
  (106 shorter events, 177.4 us)
Async XLA Ops:
  3.0 10.1 all-to-all-start.1
  10.4 48.0 %collective-permute-start = (f32[2,64,8,256]{3,2,1,0:T(8,128)S(1)}, f32[2,64,8,256]{3,2,1,0:T(8,128)S(1)}, u32[]{:S(2)}, u32[]{:S(2)}) collective-permute-start(f32[2,64,8,256]{3,2,1,0:T(8,128)S(1)} %bitcast.116), channel_id=1, source_target_pairs={{0,4},{4,0},{1,5},{5,1},{2,6},{6,2},{3,7},{7,3},{8,12},{12,8},{9,1... | collective-permute-start | bytes 3145736 | tf_op jit(solution)/shard_map/ppermute | solution.py:397
  67.1 6.0 copy-start.2
  67.1 64.8 %copy-start.5 = (f32[256]{0:T(256)S(1)}, f32[256]{0:T(256)}, u32[]{:S(2)}) copy-start(f32[256]{0:T(256)} %constant.178.clone) | copy-start | bytes 3076
  67.1 56.8 %all-to-all-start.2 = ((f32[128,2,2,8,256]{4,3,2,1,0:T(8,128)}), f32[128,2,2,8,256]{4,3,2,1,0:T(8,128)}, u32[]{:S(2)}, u32[]{:S(2)}) async-start(f32[128,2,2,8,256]{4,3,2,1,0:T(8,128)} %bitcast.102), calls=%async_computation.2 | async-start | bytes 8388608 | tf_op jit(solution)/shard_map/all_to_all | solution.py:467
  124.5 23.0 %all-to-all-start = ((f32[32,1,128]{2,1,0:T(1,128)}), f32[32,1,128]{2,1,0:T(1,128)S(1)}, u32[]{:S(2)}, u32[]{:S(2)}) async-start(f32[32,1,128]{2,1,0:T(1,128)} %broadcast_in_dim.14), calls=%async_computation | async-start | bytes 32768 | tf_op jit(solution)/shard_map/all_to_all | solution.py:393
  147.5 58.4 %all-to-all-start.3 = ((f32[128,2,2,8,256]{4,3,2,1,0:T(8,128)}), f32[128,2,2,8,256]{4,3,2,1,0:T(8,128)}, u32[]{:S(2)}, u32[]{:S(2)}) async-start(f32[128,2,2,8,256]{4,3,2,1,0:T(8,128)} %bitcast.101), calls=%async_computation.3 | async-start | bytes 8388608 | tf_op jit(solution)/shard_map/all_to_all | solution.py:469
  154.5 50.8 %collective-permute-start.1 = (f32[2,2,8,256]{3,2,1,0:T(8,128)S(1)}, f32[2,2,8,256]{3,2,1,0:T(8,128)S(1)}, u32[]{:S(2)}, u32[]{:S(2)}) collective-permute-start(f32[2,2,8,256]{3,2,1,0:T(8,128)S(1)} %get-tuple-element.114), channel_id=1, source_target_pairs={{0,4},{4,0},{1,5},{5,1},{2,6},{6,2},{3,7},{7,3},{8,12},{12,8},{9,1... | collective-permute-start | bytes 98312 | tf_op jit(solution)/shard_map/ppermute | solution.py:397
  421.2 4.7 copy-start.4
  421.2 56.8 %all-to-all-start.7 = ((f32[128,2,2,8,256]{4,3,2,1,0:T(8,128)}), f32[128,2,2,8,256]{4,3,2,1,0:T(8,128)}, u32[]{:S(2)}, u32[]{:S(2)}) async-start(f32[128,2,2,8,256]{4,3,2,1,0:T(8,128)} %bitcast.106), calls=%async_computation.7 | async-start | bytes 8388608 | tf_op jit(solution)/shard_map/all_to_all | solution.py:469
  515.3 72.5 %copy-start = (f32[2,3,64,8,256]{4,3,2,1,0:T(8,128)S(1)}, f32[2,3,64,8,256]{4,3,2,1,0:T(8,128)}, u32[]{:S(2)}) copy-start(f32[2,3,64,8,256]{4,3,2,1,0:T(8,128)} %get-tuple-element.82) | copy-start | bytes 9437188
  517.0 70.8 %collective-permute-start.2 = (f32[3,64,8,256]{3,2,1,0:T(8,128)S(1)}, f32[3,64,8,256]{3,2,1,0:T(8,128)S(1)}, u32[]{:S(2)}, u32[]{:S(2)}) collective-permute-start(f32[3,64,8,256]{3,2,1,0:T(8,128)S(1)} %slice_bitcast_fusion.3), channel_id=1, source_target_pairs={{0,4},{4,0},{1,5},{5,1},{2,6},{6,2},{3,7},{7,3},{8,12},{12,8},{9,1... | collective-permute-start | bytes 4718600 | tf_op jit(solution)/shard_map/ppermute | solution.py:397
  589.0 46.6 %collective-permute-start.3 = (f32[2,64,8,256]{3,2,1,0:T(8,128)S(1)}, f32[2,64,8,256]{3,2,1,0:T(8,128)S(1)}, u32[]{:S(2)}, u32[]{:S(2)}) collective-permute-start(f32[2,64,8,256]{3,2,1,0:T(8,128)S(1)} %get-tuple-element.110), channel_id=1, source_target_pairs={{0,4},{4,0},{1,5},{5,1},{2,6},{6,2},{3,7},{7,3},{8,12},{12,8},{9,1... | collective-permute-start | bytes 3145736 | tf_op jit(solution)/shard_map/ppermute | solution.py:397
  849.0 4.7 copy-start.3
  849.0 56.8 %all-to-all-start.13 = ((f32[128,2,2,8,256]{4,3,2,1,0:T(8,128)}), f32[128,2,2,8,256]{4,3,2,1,0:T(8,128)}, u32[]{:S(2)}, u32[]{:S(2)}) async-start(f32[128,2,2,8,256]{4,3,2,1,0:T(8,128)} %bitcast.103), calls=%async_computation.13 | async-start | bytes 8388608 | tf_op jit(solution)/shard_map/all_to_all | solution.py:469
  942.6 72.5 %copy-start.1 = (f32[2,3,64,8,256]{4,3,2,1,0:T(8,128)S(1)}, f32[2,3,64,8,256]{4,3,2,1,0:T(8,128)}, u32[]{:S(2)}) copy-start(f32[2,3,64,8,256]{4,3,2,1,0:T(8,128)} %get-tuple-element.93) | copy-start | bytes 9437188
  944.3 70.8 %collective-permute-start.5 = (f32[3,64,8,256]{3,2,1,0:T(8,128)S(1)}, f32[3,64,8,256]{3,2,1,0:T(8,128)S(1)}, u32[]{:S(2)}, u32[]{:S(2)}) collective-permute-start(f32[3,64,8,256]{3,2,1,0:T(8,128)S(1)} %slice_bitcast_fusion.2), channel_id=1, source_target_pairs={{0,4},{4,0},{1,5},{5,1},{2,6},{6,2},{3,7},{7,3},{8,12},{12,8},{9,1... | collective-permute-start | bytes 4718600 | tf_op jit(solution)/shard_map/ppermute | solution.py:397
  1017.9 102.3 %all-to-all-start.16 = ((f32[4,2,64,8,256]{4,3,2,1,0:T(8,128)}), f32[4,2,64,8,256]{4,3,2,1,0:T(8,128)}, u32[]{:S(2)}, u32[]{:S(2)}) async-start(f32[4,2,64,8,256]{4,3,2,1,0:T(8,128)} %broadcast_in_dim.20), calls=%async_computation.16 | async-start | bytes 8388608 | tf_op jit(solution)/shard_map/all_to_all | solution.py:528
  1024.5 90.5 %collective-permute-start.4 = (f32[2,64,2,8,256]{4,3,2,1,0:T(8,128)S(1)}, f32[2,64,2,8,256]{4,3,2,1,0:T(8,128)}, u32[]{:S(2)}, u32[]{:S(2)}) collective-permute-start(f32[2,64,2,8,256]{4,3,2,1,0:T(8,128)S(1)} %slice_bitcast_fusion.1), channel_id=1, source_target_pairs={{0,4},{4,0},{1,5},{5,1},{2,6},{6,2},{3,7},{7,3},{8,12},{12,8},{9,1... | collective-permute-start | bytes 6291464 | tf_op jit(solution)/shard_map/ppermute | solution.py:397
  1120.2 52.7 %all-to-all-start.15 = ((f32[4,64,2,8,256]{4,3,2,1,0:T(8,128)}), f32[4,64,2,8,256]{4,3,2,1,0:T(8,128)}, u32[]{:S(2)}, u32[]{:S(2)}) async-start(f32[4,64,2,8,256]{4,3,2,1,0:T(8,128)} %pad_maximum_fusion.1), calls=%async_computation.15 | async-start | bytes 8388608 | tf_op jit(solution)/shard_map/all_to_all | solution.py:524

commit v2 on v1

v2 whole, which is shorter than its diff:
```python
from functools import partial
import math

import jax
import jax.numpy as jnp
import ml_dtypes
import numpy as np
from jax import lax
from jax.experimental import pallas as pl
from jax.experimental.pallas import tpu as pltpu
from jax.sharding import Mesh, PartitionSpec as P

OUTER = 2
WAVENUMBER = 2.0 * math.pi / 6.0
DAMPING = 0.3
SOURCE_GAP = 8.0
FLOOR_SHARE = 0.75
REAL_LOW = -0.25
REAL_HIGH = 0.35
IMAG_HIGH = 0.1
ALL = ("src", "half", "rest")
GROUP = ("src", "rest")
F32 = jnp.float32


def times_const(value, factor):
    re, im = value
    a, b = factor.real, factor.imag
    if abs(b) < 1e-12:
        return (re, im) if abs(a - 1) < 1e-12 else (re * a, im * a)
    if abs(a) < 1e-12:
        return (im * -b, re * b) if abs(abs(b) - 1) > 1e-12 else ((-im, re) if b > 0 else (im, -re))
    if abs(abs(a) - abs(b)) < 1e-12:
        if a * b > 0:
            return ((re - im) * a, (re + im) * a)
        return ((re + im) * a, (im - re) * a)
    return (re * a - im * b, re * b + im * a)


def small_dft(values, sign):
    count = len(values)
    if count == 1:
        return values
    even, odd = small_dft(values[0::2], sign), small_dft(values[1::2], sign)
    low, high = [], []
    for k in range(count // 2):
        turned = times_const(odd[k], np.exp(sign * 2j * math.pi * k / count))
        low.append((even[k][0] + turned[0], even[k][1] + turned[1]))
        high.append((even[k][0] - turned[0], even[k][1] - turned[1]))
    return low + high


def factors(total):
    bits = total.bit_length() - 1
    return 1 << (bits // 2), total // (1 << (bits // 2))


def stage_one(values, n0, count, sign, keep):
    width = len(values)
    for k1, value in enumerate(small_dft(values, sign)):
        re, im = times_const(value, np.exp(sign * 2j * math.pi * n0 * k1 / count))
        keep[n0 * width + k1, 0] = re
        keep[n0 * width + k1, 1] = im


def stage_two(k1, width, count, sign, keep):
    values = [(keep[n0 * width + k1, 0], keep[n0 * width + k1, 1]) for n0 in range(count // width)]
    return small_dft(values, sign)


def pair(ref, z):
    return ref[0, z, 0], ref[0, z, 1]


def put(ref, z, value):
    ref[0, z, 0] = value[0]
    ref[0, z, 1] = value[1]


def put_spec(ref, z, value):
    ref[z, 0] = value[0]
    ref[z, 1] = value[1]


def returned(refs, z):
    place, plane = divmod(z, sum(ref.shape[1] for ref in refs))
    for ref in refs:
        if plane < ref.shape[1]:
            return ref[place, plane, 0, 0], ref[place, plane, 1, 0]
        plane -= ref.shape[1]


def invert_one(refs, depth, width, rest, keep):
    for n0 in range(rest):
        stage_one([returned(refs, n0 + rest * n1) for n1 in range(width)], n0, depth, 1, keep)


def finish(spec, depth, width, rest, keep):
    for j1 in range(rest):
        for j0, value in enumerate(stage_two(j1, rest, depth, -1, keep)):
            put_spec(spec, j1 + rest * j0, value)


def start_kernel(chi, inc, source, spec, keep):
    depth = inc.shape[1]
    width, rest = factors(depth)
    for n0 in range(width):
        values = []
        for n1 in range(rest):
            z = n0 + width * n1
            cr, ci = chi[0, z], chi[1, z]
            er, ei = pair(inc, z)
            w = (cr * er - ci * ei, cr * ei + ci * er)
            put(source, z, w)
            values.append(w)
        stage_one(values, n0, depth, -1, keep)
    finish(spec, depth, width, rest, keep)


def adjoint_kernel(first, scal, chi, inc, source, data, *refs):
    if first:
        *fields, scat_out, resid, spec, keep_in, keep = refs
    else:
        field, resid, spec, keep = refs
    depth = inc.shape[1]
    width, rest = factors(depth)
    object_weight, data_weight = scal[0, 0], scal[0, 1]
    if first:
        invert_one(fields, depth, width, rest, keep_in)
    for k1 in range(width):
        scattered = stage_two(k1, width, depth, 1, keep_in) if first else None
        values = []
        for k0 in range(rest):
            z = k1 + width * k0
            if first:
                sr, si = scattered[k0]
                put(scat_out, z, (sr, si))
            else:
                sr, si = pair(field, z)
            cr, ci = chi[0, z], chi[1, z]
            er, ei = pair(inc, z)
            wr, wi = pair(source, z)
            ur, ui = er + sr, ei + si
            rr = cr * ur - ci * ui - wr
            ri = cr * ui + ci * ur - wi
            put(resid, z, (rr, ri))
            vr = -object_weight * (cr * rr + ci * ri)
            vi = -object_weight * (cr * ri - ci * rr)
            if z == 0:
                vr = vr + data_weight * (data[0, 0] - sr)
                vi = vi + data_weight * (data[0, 1] - si)
            values.append((vr, vi))
        stage_one(values, k1, depth, -1, keep)
    finish(spec, depth, width, rest, keep)


def descent_kernel(scal, resid, *refs):
    *fields, descent, spec, sums, keep_in, keep = refs
    depth = resid.shape[1]
    width, rest = factors(depth)
    object_weight = scal[0, 0]
    invert_one(fields, depth, width, rest, keep_in)
    total = jnp.zeros(sums.shape[3:], F32)
    for k1 in range(width):
        values = []
        for k0, (gr, gi) in enumerate(stage_two(k1, width, depth, 1, keep_in)):
            z = k1 + width * k0
            rr, ri = pair(resid, z)
            dr, di = gr + object_weight * rr, gi + object_weight * ri
            put(descent, z, (dr, di))
            total = total + (dr * dr + di * di)
            values.append((dr, di))
        stage_one(values, k1, depth, -1, keep)
    finish(spec, depth, width, rest, keep)
    sums[0, 0, 0] = total


def image_kernel(descent, chi, *refs):
    *fields, image, sums, keep_in = refs
    depth = descent.shape[1]
    width, rest = factors(depth)
    invert_one(fields, depth, width, rest, keep_in)
    change = plane = jnp.zeros(sums.shape[3:], F32)
    for k1 in range(width):
        for k0, (hr, hi) in enumerate(stage_two(k1, width, depth, 1, keep_in)):
            z = k1 + width * k0
            put(image, z, (hr, hi))
            dr, di = pair(descent, z)
            cr, ci = chi[0, z], chi[1, z]
            qr = dr - (cr * hr - ci * hi)
            qi = di - (cr * hi + ci * hr)
            change = change + (qr * qr + qi * qi)
            if z == 0:
                plane = hr * hr + hi * hi
    sums[0, 0, 0] = change
    sums[0, 0, 1] = plane


def step_kernel(last, scal, source, descent, scattered, image, inc, source_out, *rest_refs):
    if last:
        (parts,) = rest_refs
    else:
        scat_out, parts = rest_refs
    sources, depth = inc.shape[:2]
    step = scal[0, 0]

    def body(z, _):
        nr = ni = power = None
        for s in range(sources):
            dr, di = descent[s, z, 0], descent[s, z, 1]
            wr, wi = source[s, z, 0] + step * dr, source[s, z, 1] + step * di
            source_out[s, z, 0] = wr
            source_out[s, z, 1] = wi
            sr = scattered[s, z, 0] + step * image[s, z, 0]
            si = scattered[s, z, 1] + step * image[s, z, 1]
            if not last:
                scat_out[s, z, 0] = sr
                scat_out[s, z, 1] = si
            ur, ui = inc[s, z, 0] + sr, inc[s, z, 1] + si
            a, b, c = wr * ur + wi * ui, wi * ur - wr * ui, ur * ur + ui * ui
            nr, ni, power = (a, b, c) if s == 0 else (nr + a, ni + b, power + c)
        parts[0, z] = nr
        parts[1, z] = ni
        parts[2, z] = power
        return 0

    lax.fori_loop(0, depth, body, 0, unroll=4)


def assemble_kernel(spot, *refs):
    *rounds, out = refs
    turn = lax.rem(spot[0] + len(rounds) - pl.program_id(0), len(rounds))
    for t, ref in enumerate(rounds):

        @pl.when(turn == t)
        def _(ref=ref):
            for z in range(out.shape[2]):
                out[:, 0, z] = ref[:, z, 0]
                out[:, 1, z] = ref[:, z, 1]


def half_tables(total, order):
    half = total // 2
    modes = np.arange(half)[:, None]
    place = np.asarray(order)[None, :]
    out = []
    for odd in (0, 1):
        angle = 2.0 * math.pi * ((2 * modes + odd) * place % total) / total
        cosine, sine = np.cos(angle), np.sin(angle)
        out.append(np.block([[cosine, sine], [-sine, cosine]]).astype(np.float32))
    return np.stack(out)


def high_low(table):
    high = table.astype(ml_dtypes.bfloat16)
    low = (table - high.astype(np.float32)).astype(ml_dtypes.bfloat16)
    return np.stack([high, low])


def lateral_modes(total):
    index = np.concatenate([np.arange(0, total, 2), np.arange(1, total, 2)])
    return (4.0 * np.sin(math.pi * index / total) ** 2).astype(np.float32)


def split(value):
    high = value.astype(jnp.bfloat16)
    return high, (value - high.astype(F32)).astype(jnp.bfloat16)


def left_mul(table, odd, value):
    high, low = split(value)
    return jnp.dot(
        jnp.concatenate([table[0, odd], table[0, odd], table[1, odd]], axis=1),
        jnp.concatenate([high, low, high], axis=0),
        preferred_element_type=F32,
    )


def right_mul(value, table, odd):
    high, low = split(value)
    return jnp.dot(
        jnp.concatenate([high, low, high], axis=1),
        jnp.concatenate([table[0, odd], table[0, odd], table[1, odd]], axis=0),
        preferred_element_type=F32,
    )


def plane_kernel(sign, scale, lz, lx, ly, xf, xb, yf, yb, own_ref, other_ref, out):
    senders, _, _, rows, ny = own_ref.shape
    hx, hy = senders * rows, ny // 2
    own = [own_ref[:, 0, c].reshape(hx, ny) for c in (0, 1)]
    other = [other_ref[:, 0, c].reshape(hx, ny) for c in (0, 1)]
    across = [
        left_mul(xf, 0, jnp.concatenate([own[0] + other[0], own[1] + other[1]], axis=0)),
        left_mul(xf, 1, jnp.concatenate([own[0] - other[0], own[1] - other[1]], axis=0)),
    ]
    real = jnp.concatenate([across[0][:hx], across[1][:hx]], axis=0)
    imag = jnp.concatenate([across[0][hx:], across[1][hx:]], axis=0)
    wave_sq = WAVENUMBER * WAVENUMBER
    back = []
    for odd in (0, 1):
        flip = -1.0 if odd else 1.0
        folded = jnp.concatenate(
            [real[:, :hy] + flip * real[:, hy:], imag[:, :hy] + flip * imag[:, hy:]], axis=1
        )
        freq = right_mul(folded, yf, odd)
        eigen = (lx[...] + lz[pl.program_id(0)]) + ly[odd]
        real_den = eigen - wave_sq
        imag_den = wave_sq * DAMPING
        factor = (wave_sq * scale) / (real_den * real_den + imag_den * imag_den)
        gr, gi = factor * real_den, factor * (imag_den * sign)
        fr, fi = freq[:, :hy], freq[:, hy:]
        filtered = jnp.concatenate([fr * gr - fi * gi, fr * gi + fi * gr], axis=1)
        back.append(right_mul(filtered, yb, odd))
    plus, minus = back[0] + back[1], back[0] - back[1]
    real = jnp.concatenate([plus[:, :hy], minus[:, :hy]], axis=1)
    imag = jnp.concatenate([plus[:, hy:], minus[:, hy:]], axis=1)
    even = left_mul(xb, 0, jnp.concatenate([real[:hx], imag[:hx]], axis=0))
    odd = left_mul(xb, 1, jnp.concatenate([real[hx:], imag[hx:]], axis=0))
    plus, minus = even + odd, even - odd
    for c in (0, 1):
        out[:, 0, c, 0] = plus[c * hx : (c + 1) * hx].reshape(senders, rows, ny)
        out[:, 0, c, 1] = minus[c * hx : (c + 1) * hx].reshape(senders, rows, ny)


SMEM = pl.BlockSpec(memory_space=pltpu.SMEM)


class Slabs:
    def __init__(self, sources, depth, rows, ny, pieces):
        self.sources, self.depth, self.rows, self.ny, self.pieces = sources, depth, rows, ny, pieces
        self.lanes = 128 if ny % 128 == 0 else ny
        self.deep = depth // 4 if depth % 4 == 0 else depth

    def kind(self, name, chunk):
        s, z, q, y, lanes, deep = self.sources, self.depth, self.rows, self.ny, self.lanes, self.deep
        turns = (y // lanes, s)
        if name.startswith("piece"):
            count = self.pieces[int(name[5:])]
            owners = z // sum(self.pieces)
            return (
                (s * owners, count, 2, 2, q, y),
                (owners, count, 2, 1, q, lanes),
                lambda j, i: (i, 0, 0, chunk, 0, j),
            )
        return {
            "field": ((s, z, 2, q, y), (1, z, 2, q, lanes), lambda j, i: (i, 0, 0, 0, j)),
            "spec": ((s * z, 2, q, y), (z, 2, q, lanes), lambda j, i: (i, 0, 0, j)),
            "chi": ((2, z, q, y), (2, z, q, lanes), lambda j, i: (0, 0, 0, j)),
            "data": ((s, 2, q, y), (1, 2, q, lanes), lambda j, i: (i, 0, 0, j)),
            "sum1": (turns + (1, q, lanes), (1, 1, 1, q, lanes), lambda j, i: (j, i, 0, 0, 0)),
            "sum2": (turns + (2, q, lanes), (1, 1, 2, q, lanes), lambda j, i: (j, i, 0, 0, 0)),
            "every": ((s, z, 2, q, y), (s, deep, 2, q, lanes), lambda j, i: (0, i, 0, 0, j)),
            "parts": ((3, z, q, y), (3, deep, q, lanes), lambda j, i: (0, i, 0, j)),
        }[name]

    def call(self, kernel, name, chunk, ins, outs, scratch, *args):
        def spec(kind):
            if kind == "scal":
                return SMEM
            _, block, index = self.kind(kind, chunk)
            return pl.BlockSpec(block, index)

        sizes = [math.prod(self.kind(k, chunk)[0]) * 4 for k in (*ins, *outs) if k != "scal"]
        moved = sum(sizes)
        second = self.depth // self.deep if "parts" in outs else self.sources
        return pl.pallas_call(
            kernel,
            grid=(self.ny // self.lanes, second),
            in_specs=[spec(k) for k in ins],
            out_specs=[spec(k) for k in outs],
            out_shape=[jax.ShapeDtypeStruct(self.kind(k, chunk)[0], F32) for k in outs],
            scratch_shapes=[pltpu.VMEM((self.depth, 2, self.rows, self.lanes), F32)] * scratch,
            cost_estimate=pl.CostEstimate(flops=moved * 4, bytes_accessed=moved, transcendentals=0),
            name=name,
        )(*args)

    def piece_kinds(self):
        return tuple("piece%d" % m for m in range(len(self.pieces)))


def filter_planes(own, other, first, count, senders, lz, shared, sign, scale):
    _, parts, rows, ny = own.shape
    planes = own.shape[0] // senders
    dense = rows % 8 != 0

    def shaped(value):
        value = value.reshape(senders, planes, parts, rows, ny)
        if dense:
            value = value.transpose(1, 2, 0, 3, 4).reshape(1, planes, parts, senders * rows, ny)
        return value

    own, other = shaped(own), shaped(other)
    lead, deep = own.shape[0], own.shape[3]
    out_shape = (lead, count, parts, 2, deep, ny)
    whole = lambda t: pl.BlockSpec(t.shape, lambda i, n=t.ndim: (0,) * n)
    block = pl.BlockSpec((lead, 1, parts, deep, ny), lambda i: (0, i + first, 0, 0, 0))
    nx = 2 * senders * rows
    out = pl.pallas_call(
        partial(plane_kernel, sign, scale),
        grid=(count,),
        in_specs=[SMEM] + [whole(t) for t in shared] + [block, block],
        out_specs=pl.BlockSpec((lead, 1, parts, 2, deep, ny), lambda i: (0, i, 0, 0, 0, 0)),
        out_shape=jax.ShapeDtypeStruct(out_shape, F32),
        cost_estimate=pl.CostEstimate(
            flops=count * 24 * nx * nx * ny * 2,
            bytes_accessed=2 * math.prod(out_shape) * 4,
            transcendentals=0,
        ),
        name="planes",
    )(lz[first : first + count], *shared, own, other)
    if dense:
        out = out.reshape(count, parts, 2, senders, rows, ny).transpose(3, 0, 1, 2, 4, 5)
    return out


def everyone(values):
    count = math.prod(lax.axis_size(name) for name in ALL)
    row = jnp.zeros((128,), F32).at[: len(values)].set(jnp.stack(values))
    sent = jnp.broadcast_to(row[None], (count, 128))
    return jnp.sum(lax.all_to_all(sent, ALL, 0, 0, tiled=True), axis=0)


def swap_halves(value):
    return lax.ppermute(value, "half", [(0, 1), (1, 0)])


def after(value, *others):
    return lax.optimization_barrier((value, *others))[0]


def bounded(numer_real, numer_imag, power, total_sources):
    floored = jnp.maximum(power, FLOOR_SHARE * total_sources)
    return jnp.stack(
        [
            jnp.clip(numer_real / floored, REAL_LOW, REAL_HIGH),
            jnp.clip(numer_imag / floored, 0.0, IMAG_HIGH),
        ]
    )


def deliver(chunks, shares, per_share, share, half, gate):
    slots = shares // 2
    rounds = []
    for t in range(shares):
        number = lax.rem(share + t, shares)
        slot = number // 2
        cut = [lax.dynamic_slice_in_dim(w, slot * per_share, per_share, axis=0) for w in chunks]
        sent = after(jnp.where(number % 2 == 0, cut[0], cut[1]), gate)
        pairs = []
        for a in range(shares):
            g, c = divmod((a + t) % shares, 2)
            for h in (0, 1):
                pairs.append((a * 2 + h, (h * slots + g) * 2 + (h + c) % 2))
        rounds.append(lax.ppermute(sent, ("src", "half"), pairs))
    spot = 2 * lax.rem(share, slots) + lax.rem(half + share // slots, 2)
    _, depth, _, rows, ny = rounds[0].shape
    whole = pl.BlockSpec(rounds[0].shape, lambda a: (0, 0, 0, 0, 0))
    out = pl.pallas_call(
        assemble_kernel,
        grid=(shares,),
        in_specs=[SMEM] + [whole] * shares,
        out_specs=pl.BlockSpec((per_share, 2, depth, None, rows, ny), lambda a: (0, 0, 0, a, 0, 0)),
        out_shape=jax.ShapeDtypeStruct((per_share, 2, depth, shares, rows, ny), F32),
        name="assemble",
    )(spot.reshape(1).astype(jnp.int32), *rounds)
    return out.reshape(per_share, 2, depth, shares * rows, ny)


def on_device(contrast, measured, positions):
    shares, rest_count = lax.axis_size("src"), lax.axis_size("rest")
    share, half, rest = (lax.axis_index(name) for name in ALL)
    senders = shares * rest_count
    _, depth, block_rows, ny = contrast.shape
    rows = block_rows // shares
    nx = block_rows * 2 * rest_count
    per_share = positions.shape[0]
    total_sources = per_share * shares
    sources = total_sources // 2
    planes = sources * depth // senders
    pieces = (planes // 4, planes - planes // 4) if planes >= 4 else (planes,)
    slabs = Slabs(sources, depth, rows, ny, pieces)

    chi_own = lax.dynamic_index_in_dim(
        contrast.reshape(2, depth, shares, rows, ny), share, axis=2, keepdims=False
    )
    chi = [chi_own, swap_halves(chi_own)]

    spots = jnp.pad(positions.astype(F32).reshape(1, -1), ((0, 0), (0, 126)))
    sent = jnp.concatenate(
        [
            measured.reshape(per_share, 2, shares, rows * ny).transpose(2, 0, 1, 3).reshape(shares, -1),
            jnp.broadcast_to(spots, (shares, spots.shape[1])),
        ],
        axis=1,
    )
    got = lax.all_to_all(sent, "src", 0, 0, tiled=True)
    cells = per_share * 2 * rows * ny
    data_own = got[:, :cells].reshape(total_sources, 2, rows, ny)
    spots = got[:, cells : cells + 2 * per_share].reshape(total_sources, 2)
    mine = lambda v, h: lax.dynamic_slice_in_dim(v, h * sources, sources, axis=0)
    data = [mine(data_own, half), swap_halves(mine(data_own, 1 - half))]
    spots = mine(spots, half)

    heights = jnp.arange(depth).astype(F32) + SOURCE_GAP
    offset_y = jnp.arange(ny).astype(F32)[None] - spots[:, 1][:, None]
    inc = []
    for where in (half, 1 - half):
        start = (where * rest_count + rest) * block_rows + share * rows
        offset_x = (start + jnp.arange(rows)).astype(F32)[None] - spots[:, 0][:, None]
        dist_sq = (heights * heights)[None, :, None, None] + (offset_x * offset_x)[:, None, :, None]
        dist_sq = dist_sq + (offset_y * offset_y)[:, None, None, :]
        phases = WAVENUMBER * jnp.sqrt(dist_sq)
        inc.append(jnp.stack([jnp.cos(phases), jnp.sin(phases)], axis=2))

    order = [(k * shares + a) * rows + q for a in range(shares) for k in range(rest_count) for q in range(rows)]
    x_table, y_table = half_tables(nx, order), half_tables(ny, range(ny // 2))
    flip = lambda t: high_low(np.swapaxes(t, -1, -2))
    lx = np.broadcast_to(lateral_modes(nx)[:, None], (nx, ny // 2))
    ly = lateral_modes(ny).reshape(2, 1, ny // 2)
    shared = [jnp.asarray(t) for t in (lx, ly, high_low(x_table), flip(x_table), flip(y_table), high_low(y_table))]
    place = share * rest_count + rest
    modes = (place * planes + jnp.arange(planes)) % depth
    half_sine = jnp.sin(math.pi * modes.astype(F32) / depth)
    lz = 4.0 * half_sine * half_sine
    scale = 1.0 / (nx * ny * depth)

    def forward(spec):
        return lax.all_to_all(spec, GROUP, 0, 0, tiled=True)

    def back(came, sign):
        out, first = [], 0
        for count in pieces:
            part = filter_planes(*came, first, count, senders, lz, shared, sign, scale)
            shape = part.shape
            part = lax.all_to_all(part.reshape((-1,) + shape[2:]), GROUP, 0, 0, tiled=True)
            out.append(part.reshape(shape))
            first += count
        return out

    both = (0, 1)
    piece_kinds = slabs.piece_kinds()
    totals = everyone([jnp.sum(measured * measured), total_sources * jnp.sum(chi_own * chi_own)])
    data_weight = 1.0 / totals[0]
    object_total = totals[1]
    source, came = [None, None], [None, None]
    for c in both:
        source[c], spec = slabs.call(
            start_kernel, "start", c, ("chi", "field"), ("field", "spec"), 1, chi[c], inc[c]
        )
        came[c] = forward(spec)
    fields = back(came, 1.0)
    scattered = [None, None]
    for outer in range(OUTER):
        object_weight = 1.0 / object_total
        weights = jnp.stack([object_weight, data_weight]).reshape(1, 2)
        first, last = outer == 0, outer == OUTER - 1
        resid, descent, image = [None, None], [None, None], [None, None]
        came = [None, None]
        for c in both:
            out = slabs.call(
                partial(adjoint_kernel, first),
                "adjoint",
                c,
                ("scal", "chi", "field", "field", "data") + (piece_kinds if first else ("field",)),
                ("field", "field", "spec") if first else ("field", "spec"),
                2 if first else 1,
                weights, chi[c], inc[c], source[c], data[c], *(fields if first else (scattered[c],)),
            )
            if first:
                scattered[c] = out[0]
            resid[c] = out[-2]
            came[c] = forward(out[-1])
        fields = back(came, -1.0)
        came, sums = [None, None], []
        for c in both:
            descent[c], spec, part = slabs.call(
                descent_kernel, "descent", c, ("scal", "field") + piece_kinds, ("field", "spec", "sum1"), 2,
                weights, resid[c], *fields,
            )
            came[c] = forward(spec)
            sums.append(part)
        sum_d = jnp.sum(sums[0]) + jnp.sum(sums[1])
        fields = back(came, 1.0)
        sums = []
        for c in both:
            image[c], part = slabs.call(
                image_kernel, "image", c, ("field", "chi") + piece_kinds, ("field", "sum2"), 1,
                descent[c], chi[c], *fields,
            )
            sums.append(part)
        sum_q = sums[0] + sums[1]
        totals = everyone([sum_d, jnp.sum(sum_q[:, :, 0]), jnp.sum(sum_q[:, :, 1])])
        step = totals[0] / (data_weight * totals[2] + object_weight * totals[1])
        parts = [None, None]
        for c in (1, 0):
            out = slabs.call(
                partial(step_kernel, last),
                "step",
                c,
                ("scal",) + ("every",) * 5,
                ("every",) * (1 if last else 2) + ("parts",),
                0,
                step.reshape(1, 1), source[c], descent[c], scattered[c], image[c], inc[c],
            )
            source[c], parts[c] = out[0], out[-1]
            if not last:
                scattered[c] = out[1]
        received = swap_halves(parts[1])
        sums = parts[0] + received
        chi_own = bounded(sums[0], sums[1], sums[2], total_sources)
        if not last:
            object_total = everyone([total_sources * jnp.sum(chi_own * chi_own)])[0]
            chi = [chi_own, swap_halves(after(chi_own, object_total))]

    contrast_sources = deliver(source, shares, per_share, share, half, received)
    sent = jnp.broadcast_to(chi_own[None], (shares,) + chi_own.shape)
    contrast_new = lax.all_to_all(sent, "src", 0, 0, tiled=True)
    contrast_new = contrast_new.transpose(1, 2, 0, 3, 4).reshape(contrast.shape)
    return contrast_sources, contrast_new


def solution(mesh):
    shares, spaces = mesh.shape["src"], mesh.shape["space"]
    split_mesh = Mesh(mesh.devices.reshape(shares, 2, spaces // 2), ALL)
    space = ("half", "rest")
    return jax.shard_map(
        on_device,
        mesh=split_mesh,
        in_specs=(P(None, None, space, None), P("src", None, space, None), P("src", None)),
        out_specs=(P("src", None, None, space, None), P(None, None, space, None)),
        check_vma=False,
    )
```

time: 1180 us -> 1150 us (0.975)
  blocking collectives: 399 us -> 248 us
  Pallas kernels: 157 us -> 203 us
  starting transfers between devices: 47.5 us -> 92.9 us
  waiting for transfers between devices: 508 us -> 521 us
    all_to_all x6, blocking collectives: 329 us -> 214 us  [the longest x4 128 us: forward(): return lax.all_to_all(spec, GROUP, 0, 0, tiled=True)]
    ppermute x0 -> x4, waiting for transfers between devices: none -> 84.8 us  [deliver(): rounds.append(lax.ppermute(sent, ('src', 'half'), pairs))]
    ppermute x6 -> x5, waiting for transfers between devices: 313 us -> 249 us  [swap_halves(): return lax.ppermute(value, 'half', [(0, 1), (1, 0)])]
    pallas_call x14 -> x29, Pallas kernels: 157 us -> 203 us  [the longest x18 111 us: call(): pl.pallas_call(kernel, grid=(self.ny // self.lanes, second), in_specs=[sp...]
    all_to_all x5 -> x14, starting transfers between devices: 23.7 us -> 60.1 us  [the longest x8 30.5 us: back(): lax.all_to_all(part.reshape((-1,) + shape[2:]), GROUP, 0, 0, tiled=True)]
    all_to_all x3, blocking collectives: 70.5 us -> 34.4 us  [everyone(): return jnp.sum(lax.all_to_all(sent, ALL, 0, 0, tiled=True), axis=0)]
    ppermute x0 -> x4, starting transfers between devices: none -> 12.4 us  [deliver(): rounds.append(lax.ppermute(sent, ('src', 'half'), pairs))]
    all_to_all x5 -> x14, waiting for transfers between devices: 195 us -> 185 us  [the longest x8 94.5 us: back(): lax.all_to_all(part.reshape((-1,) + shape[2:]), GROUP, 0, 0, tiled=True)]
  transfers between devices with their start and end apart: 14 -> 26, of which waited for: 9 -> 20; matrix products, arithmetic and copies ran while one was open for 3% -> 2% of each run, Pallas kernels for 1% -> 10%
where the time goes in v2:
time: 1150 us; the launch traced here: 1140 us
  waiting for transfers between devices  521 us (45%)
  blocking collectives  248 us (22%)
  Pallas kernels  203 us (18%)
  starting transfers between devices  92.9 us (8%)
  other arithmetic  38.4 us (3%)
  local copies, waits for them, and re-layouts  24.9 us (2%)
    ppermute x5, waiting for transfers between devices, swap_halves(): return lax.ppermute(value, 'half', [(0, 1), (1, 0)])  249 us
    all_to_all x4, blocking collectives, forward(): return lax.all_to_all(spec, GROUP, 0, 0, tiled=True)  128 us
    pallas_call x18, Pallas kernels, call(): pl.pallas_call(kernel, grid=(self.ny // self.lanes, second), in_specs=[sp...  111 us
    all_to_all x8, waiting for transfers between devices, back(): lax.all_to_all(part.reshape((-1,) + shape[2:]), GROUP, 0, 0, tiled=True)  94.5 us
    all_to_all x6, waiting for transfers between devices, forward(): return lax.all_to_all(spec, GROUP, 0, 0, tiled=True)  90.1 us
    pallas_call x10, Pallas kernels, filter_planes(): pl.pallas_call(partial(plane_kernel, sign, scale), grid=(count,), in_spec...  87.5 us
    all_to_all x2, blocking collectives, back(): lax.all_to_all(part.reshape((-1,) + shape[2:]), GROUP, 0, 0, tiled=True)  86.2 us
    ppermute x4, waiting for transfers between devices, deliver(): rounds.append(lax.ppermute(sent, ('src', 'half'), pairs))  84.8 us
  transfers between devices with their start and end apart: 26, of which 20 were waited for; matrix products, arithmetic and copies ran while one was open for 2% of the time, Pallas kernels for 10%

profile of v2, /device:TPU:0, one launch (start us, length us, event | category | flops | bytes accessed | tf_op | source)
XLA Modules:
  0.0 1139.0 jit_solution(9948223479173754882)
XLA Ops:
  38.6 42.9 %collective-permute-done.chi = f32[2,64,8,256]{3,2,1,0:T(8,128)S(1)} collective-permute-done((f32[2,64,8,256]{3,2,1,0:T(8,128)S(1)}, f32[2,64,8,256]{3,2,1,0:T(8,128)S(1)}, u32[]{:S(2)}, u32[]{:S(2)}) %collective-permute-start) | collective-permute-done | bytes 1048608 | tf_op jit(solution)/shard_map/ppermute | solution.py:425
  97.3 25.0 %all-to-all-done.3 = f32[128,2,8,256]{3,2,1,0:T(8,128)S(1)} async-done(((f32[128,2,8,256]{3,2,1,0:T(8,128)}), f32[128,2,8,256]{3,2,1,0:T(8,128)S(1)}, u32[]{:S(2)}, u32[]{:S(2)}) %all-to-all-start.3) | async-done | bytes 2097184 | tf_op jit(solution)/shard_map/all_to_all | solution.py:529
  164.6 34.4 %collective-permute-done.1.data = f32[2,2,8,256]{3,2,1,0:T(8,128)S(1)} collective-permute-done((f32[2,2,8,256]{3,2,1,0:T(8,128)S(1)}, f32[2,2,8,256]{3,2,1,0:T(8,128)S(1)}, u32[]{:S(2)}, u32[]{:S(2)}) %collective-permute-start.1) | collective-permute-done | bytes 32800 | tf_op jit(solution)/shard_map/ppermute | solution.py:425
  221.1 20.8 %all-to-all-done.7 = f32[128,2,8,256]{3,2,1,0:T(8,128)S(1)} async-done(((f32[128,2,8,256]{3,2,1,0:T(8,128)}), f32[128,2,8,256]{3,2,1,0:T(8,128)S(1)}, u32[]{:S(2)}, u32[]{:S(2)}) %all-to-all-start.7) | async-done | bytes 2097184 | tf_op jit(solution)/shard_map/all_to_all | solution.py:529
  241.8 31.8 %all_to_all.141 = f32[128,2,8,256]{3,2,1,0:T(8,128)} all-to-all(f32[128,2,8,256]{3,2,1,0:T(8,128)} %get-tuple-element.103), channel_id=1, replica_groups=mesh['src'=4,'half'=2,'rest'=4] {'src','rest'}, dimensions={0} | all-to-all | bytes 4194304 | tf_op jit(solution)/shard_map/all_to_all | solution.py:529
  283.1 11.9 %planes.13 = f32[16,6,2,2,8,256]{5,4,3,2,1,0:T(8,128)} custom-call(f32[6]{0:T(128)} %slice.135.lz, f32[256,128]{1,0:T(8,128)} %jit_solution_.3.lx, f32[2,1,128]{2,1,0:T(1,128)} %constant.250.clone.ly, bf16[2,2,256,256]{3,2,1,0:T(8,128)(2,1)} %constant.251.clone.xf, bf16[2,2,256,256]{3,2,1,0:T(8,128)(2,1)} %constant.252.clone.xb, ...), custom_call_target="tpu_custom_call" | custom-call | flops 4831838208 | bytes 6291456 | tf_op jit(solution)/shard_map/planes/pallas_call | solution.py:399
  299.0 43.1 %all_to_all.142 = f32[96,2,2,8,256]{4,3,2,1,0:T(8,128)} all-to-all(f32[96,2,2,8,256]{4,3,2,1,0:T(8,128)} %bitcast.136), channel_id=1, replica_groups=mesh['src'=4,'half'=2,'rest'=4] {'src','rest'}, dimensions={0} | all-to-all | bytes 6291456 | tf_op jit(solution)/shard_map/all_to_all | solution.py:536
  356.9 22.2 %all-to-all-done.11 = f32[128,2,8,256]{3,2,1,0:T(8,128)S(1)} async-done(((f32[128,2,8,256]{3,2,1,0:T(8,128)}), f32[128,2,8,256]{3,2,1,0:T(8,128)S(1)}, u32[]{:S(2)}, u32[]{:S(2)}) %all-to-all-start.11) | async-done | bytes 2097184 | tf_op jit(solution)/shard_map/all_to_all | solution.py:529
  379.0 31.8 %all_to_all.143 = f32[128,2,8,256]{3,2,1,0:T(8,128)} all-to-all(f32[128,2,8,256]{3,2,1,0:T(8,128)} %get-tuple-element.110), channel_id=1, replica_groups=mesh['src'=4,'half'=2,'rest'=4] {'src','rest'}, dimensions={0} | all-to-all | bytes 4194304 | tf_op jit(solution)/shard_map/all_to_all | solution.py:529
  420.2 11.9 %planes.15 = f32[16,6,2,2,8,256]{5,4,3,2,1,0:T(8,128)} custom-call(f32[6]{0:T(128)} %slice.135.lz, f32[256,128]{1,0:T(8,128)} %jit_solution_.3.lx, f32[2,1,128]{2,1,0:T(1,128)} %constant.250.clone.ly, bf16[2,2,256,256]{3,2,1,0:T(8,128)(2,1)} %constant.251.clone.xf, bf16[2,2,256,256]{3,2,1,0:T(8,128)(2,1)} %constant.252.clone.xb, ...), custom_call_target="tpu_custom_call" | custom-call | flops 4831838208 | bytes 6291456 | tf_op jit(solution)/shard_map/planes/pallas_call | solution.py:399
  443.4 37.3 %all-to-all-done.13 = f32[96,2,2,8,256]{4,3,2,1,0:T(8,128)S(1)} async-done(((f32[96,2,2,8,256]{4,3,2,1,0:T(8,128)}), f32[96,2,2,8,256]{4,3,2,1,0:T(8,128)S(1)}, u32[]{:S(2)}, u32[]{:S(2)}) %all-to-all-start.13) | async-done | bytes 3145760 | tf_op jit(solution)/shard_map/all_to_all | solution.py:536
  495.0 11.9 %all_to_all.144 = f32[32,1,128]{2,1,0:T(1,128)S(1)} all-to-all(f32[32,1,128]{2,1,0:T(1,128)S(1)} %broadcast_in_dim.17), channel_id=1, replica_groups=mesh['src'=4,'half'=2,'rest'=4] {'src','half','rest'}, dimensions={0} | all-to-all | bytes 32768 | tf_op jit(solution)/shard_map/all_to_all | solution.py:421
  527.7 61.7 %collective-permute-done.2 = f32[3,64,8,256]{3,2,1,0:T(8,128)S(1)} collective-permute-done((f32[3,64,8,256]{3,2,1,0:T(8,128)}, f32[3,64,8,256]{3,2,1,0:T(8,128)S(1)}, u32[]{:S(2)}, u32[]{:S(2)}) %collective-permute-start.2) | collective-permute-done | bytes 1572896 | tf_op jit(solution)/shard_map/ppermute | solution.py:425
  613.3 47.8 %collective-permute-done.3.chi = f32[2,64,8,256]{3,2,1,0:T(8,128)S(1)} collective-permute-done((f32[2,64,8,256]{3,2,1,0:T(8,128)S(1)}, f32[2,64,8,256]{3,2,1,0:T(8,128)S(1)}, u32[]{:S(2)}, u32[]{:S(2)}) %collective-permute-start.3) | collective-permute-done | bytes 1048608 | tf_op jit(solution)/shard_map/ppermute | solution.py:425
  668.0 32.4 %all_to_all.146 = f32[128,2,8,256]{3,2,1,0:T(8,128)} all-to-all(f32[128,2,8,256]{3,2,1,0:T(8,128)} %get-tuple-element.128), channel_id=1, replica_groups=mesh['src'=4,'half'=2,'rest'=4] {'src','rest'}, dimensions={0} | all-to-all | bytes 4194304 | tf_op jit(solution)/shard_map/all_to_all | solution.py:529
  710.0 11.9 %planes.17 = f32[16,6,2,2,8,256]{5,4,3,2,1,0:T(8,128)} custom-call(f32[6]{0:T(128)} %slice.135.lz, f32[256,128]{1,0:T(8,128)} %jit_solution_.3.lx, f32[2,1,128]{2,1,0:T(1,128)} %constant.250.clone.ly, bf16[2,2,256,256]{3,2,1,0:T(8,128)(2,1)} %constant.251.clone.xf, bf16[2,2,256,256]{3,2,1,0:T(8,128)(2,1)} %constant.252.clone.xb, ...), custom_call_target="tpu_custom_call" | custom-call | flops 4831838208 | bytes 6291456 | tf_op jit(solution)/shard_map/planes/pallas_call | solution.py:399
  725.9 43.1 %all_to_all.147 = f32[96,2,2,8,256]{4,3,2,1,0:T(8,128)} all-to-all(f32[96,2,2,8,256]{4,3,2,1,0:T(8,128)} %bitcast.137), channel_id=1, replica_groups=mesh['src'=4,'half'=2,'rest'=4] {'src','rest'}, dimensions={0} | all-to-all | bytes 6291456 | tf_op jit(solution)/shard_map/all_to_all | solution.py:536
  783.8 22.2 %all-to-all-done.21 = f32[128,2,8,256]{3,2,1,0:T(8,128)S(1)} async-done(((f32[128,2,8,256]{3,2,1,0:T(8,128)}), f32[128,2,8,256]{3,2,1,0:T(8,128)S(1)}, u32[]{:S(2)}, u32[]{:S(2)}) %all-to-all-start.21) | async-done | bytes 2097184 | tf_op jit(solution)/shard_map/all_to_all | solution.py:529
  805.9 31.8 %all_to_all.148 = f32[128,2,8,256]{3,2,1,0:T(8,128)} all-to-all(f32[128,2,8,256]{3,2,1,0:T(8,128)} %get-tuple-element.133), channel_id=1, replica_groups=mesh['src'=4,'half'=2,'rest'=4] {'src','rest'}, dimensions={0} | all-to-all | bytes 4194304 | tf_op jit(solution)/shard_map/all_to_all | solution.py:529
  870.5 37.1 %all-to-all-done.23 = f32[96,2,2,8,256]{4,3,2,1,0:T(8,128)S(1)} async-done(((f32[96,2,2,8,256]{4,3,2,1,0:T(8,128)}), f32[96,2,2,8,256]{4,3,2,1,0:T(8,128)S(1)}, u32[]{:S(2)}, u32[]{:S(2)}) %all-to-all-start.23) | async-done | bytes 3145760 | tf_op jit(solution)/shard_map/all_to_all | solution.py:536
  922.1 13.6 %all_to_all.149 = f32[32,1,128]{2,1,0:T(1,128)S(1)} all-to-all(f32[32,1,128]{2,1,0:T(1,128)S(1)} %broadcast_in_dim.19), channel_id=1, replica_groups=mesh['src'=4,'half'=2,'rest'=4] {'src','half','rest'}, dimensions={0} | all-to-all | bytes 32768 | tf_op jit(solution)/shard_map/all_to_all | solution.py:421
  955.1 62.3 %collective-permute-done.4 = f32[3,64,8,256]{3,2,1,0:T(8,128)S(1)} collective-permute-done((f32[3,64,8,256]{3,2,1,0:T(8,128)}, f32[3,64,8,256]{3,2,1,0:T(8,128)S(1)}, u32[]{:S(2)}, u32[]{:S(2)}) %collective-permute-start.4) | collective-permute-done | bytes 1572896 | tf_op jit(solution)/shard_map/ppermute | solution.py:425
  1043.7 59.8 %collective-permute-done.8.refs_3_ = f32[1,64,2,8,256]{4,3,2,1,0:T(8,128)S(1)} collective-permute-done((f32[1,64,2,8,256]{4,3,2,1,0:T(8,128)}, f32[1,64,2,8,256]{4,3,2,1,0:T(8,128)S(1)}, u32[]{:S(2)}, u32[]{:S(2)}) %collective-permute-start.8) | collective-permute-done | bytes 1048608 | tf_op jit(solution)/shard_map/ppermute | solution.py:455
  1103.5 25.1 %collective-permute-done.7.refs_2_ = f32[1,64,2,8,256]{4,3,2,1,0:T(8,128)S(1)} collective-permute-done((f32[1,64,2,8,256]{4,3,2,1,0:T(8,128)}, f32[1,64,2,8,256]{4,3,2,1,0:T(8,128)S(1)}, u32[]{:S(2)}, u32[]{:S(2)}) %collective-permute-start.7) | collective-permute-done | bytes 1048608 | tf_op jit(solution)/shard_map/ppermute | solution.py:455
  (189 shorter events, 354.8 us)
Async XLA Ops:
  28.6 58.8 %all-to-all-start.2 = ((f32[128,2,8,256]{3,2,1,0:T(8,128)}), f32[128,2,8,256]{3,2,1,0:T(8,128)}, u32[]{:S(2)}, u32[]{:S(2)}) async-start(f32[128,2,8,256]{3,2,1,0:T(8,128)} %get-tuple-element.100), calls=%async_computation.2 | async-start | bytes 4194304 | tf_op jit(solution)/shard_map/all_to_all | solution.py:529
  33.2 48.3 %collective-permute-start = (f32[2,64,8,256]{3,2,1,0:T(8,128)S(1)}, f32[2,64,8,256]{3,2,1,0:T(8,128)S(1)}, u32[]{:S(2)}, u32[]{:S(2)}) collective-permute-start(f32[2,64,8,256]{3,2,1,0:T(8,128)S(1)} %copy-done.3), channel_id=1, source_target_pairs={{0,4},{4,0},{1,5},{5,1},{2,6},{6,2},{3,7},{7,3},{8,12},{12,8},{9,1... | collective-permute-start | bytes 3145736 | tf_op jit(solution)/shard_map/ppermute | solution.py:425
  87.4 34.9 %all-to-all-start.3 = ((f32[128,2,8,256]{3,2,1,0:T(8,128)}), f32[128,2,8,256]{3,2,1,0:T(8,128)S(1)}, u32[]{:S(2)}, u32[]{:S(2)}) async-start(f32[128,2,8,256]{3,2,1,0:T(8,128)} %get-tuple-element.101), calls=%async_computation.3 | async-start | bytes 4194304 | tf_op jit(solution)/shard_map/all_to_all | solution.py:529
  133.6 20.4 %all-to-all-start.4 = ((f32[32,2,2,8,256]{4,3,2,1,0:T(8,128)}), f32[32,2,2,8,256]{4,3,2,1,0:T(8,128)S(1)}, u32[]{:S(2)}, u32[]{:S(2)}) async-start(f32[32,2,2,8,256]{4,3,2,1,0:T(8,128)} %bitcast.129), calls=%async_computation.4 | async-start | bytes 2097152 | tf_op jit(solution)/shard_map/all_to_all | solution.py:536
  155.0 44.1 %all-to-all-start.5 = ((f32[96,2,2,8,256]{4,3,2,1,0:T(8,128)}), f32[96,2,2,8,256]{4,3,2,1,0:T(8,128)S(1)}, u32[]{:S(2)}, u32[]{:S(2)}) async-start(f32[96,2,2,8,256]{4,3,2,1,0:T(8,128)} %bitcast.133), calls=%async_computation.5 | async-start | bytes 6291456 | tf_op jit(solution)/shard_map/all_to_all | solution.py:536
  161.5 37.6 %collective-permute-start.1 = (f32[2,2,8,256]{3,2,1,0:T(8,128)S(1)}, f32[2,2,8,256]{3,2,1,0:T(8,128)S(1)}, u32[]{:S(2)}, u32[]{:S(2)}) collective-permute-start(f32[2,2,8,256]{3,2,1,0:T(8,128)S(1)} %get-tuple-element.170), channel_id=1, source_target_pairs={{0,4},{4,0},{1,5},{5,1},{2,6},{6,2},{3,7},{7,3},{8,12},{12,8},{9,1... | collective-permute-start | bytes 98312 | tf_op jit(solution)/shard_map/ppermute | solution.py:425
  207.6 34.2 %all-to-all-start.7 = ((f32[128,2,8,256]{3,2,1,0:T(8,128)}), f32[128,2,8,256]{3,2,1,0:T(8,128)S(1)}, u32[]{:S(2)}, u32[]{:S(2)}) async-start(f32[128,2,8,256]{3,2,1,0:T(8,128)} %get-tuple-element.105), calls=%async_computation.7 | async-start | bytes 4194304 | tf_op jit(solution)/shard_map/all_to_all | solution.py:529
  279.2 19.8 %all-to-all-start.8 = ((f32[32,2,2,8,256]{4,3,2,1,0:T(8,128)}), f32[32,2,2,8,256]{4,3,2,1,0:T(8,128)S(1)}, u32[]{:S(2)}, u32[]{:S(2)}) async-start(f32[32,2,2,8,256]{4,3,2,1,0:T(8,128)} %bitcast.130), calls=%async_computation.8 | async-start | bytes 2097152 | tf_op jit(solution)/shard_map/all_to_all | solution.py:536
  347.6 31.4 %all-to-all-start.11 = ((f32[128,2,8,256]{3,2,1,0:T(8,128)}), f32[128,2,8,256]{3,2,1,0:T(8,128)S(1)}, u32[]{:S(2)}, u32[]{:S(2)}) async-start(f32[128,2,8,256]{3,2,1,0:T(8,128)} %get-tuple-element.111), calls=%async_computation.11 | async-start | bytes 4194304 | tf_op jit(solution)/shard_map/all_to_all | solution.py:529
  416.5 19.8 %all-to-all-start.12 = ((f32[32,2,2,8,256]{4,3,2,1,0:T(8,128)}), f32[32,2,2,8,256]{4,3,2,1,0:T(8,128)S(1)}, u32[]{:S(2)}, u32[]{:S(2)}) async-start(f32[32,2,2,8,256]{4,3,2,1,0:T(8,128)} %bitcast.131), calls=%async_computation.12 | async-start | bytes 2097152 | tf_op jit(solution)/shard_map/all_to_all | solution.py:536
  437.3 43.5 %all-to-all-start.13 = ((f32[96,2,2,8,256]{4,3,2,1,0:T(8,128)}), f32[96,2,2,8,256]{4,3,2,1,0:T(8,128)S(1)}, u32[]{:S(2)}, u32[]{:S(2)}) async-start(f32[96,2,2,8,256]{4,3,2,1,0:T(8,128)} %bitcast.135), calls=%async_computation.13 | async-start | bytes 6291456 | tf_op jit(solution)/shard_map/all_to_all | solution.py:536
  518.4 71.0 %collective-permute-start.2 = (f32[3,64,8,256]{3,2,1,0:T(8,128)}, f32[3,64,8,256]{3,2,1,0:T(8,128)S(1)}, u32[]{:S(2)}, u32[]{:S(2)}) collective-permute-start(f32[3,64,8,256]{3,2,1,0:T(8,128)} %get-tuple-element.120), channel_id=1, source_target_pairs={{0,4},{4,0},{1,5},{5,1},{2,6},{6,2},{3,7},{7,3},{8,12},{12,8},{9,1... | collective-permute-start | bytes 4718600 | tf_op jit(solution)/shard_map/ppermute | solution.py:425
  608.8 59.2 %all-to-all-start.16 = ((f32[128,2,8,256]{3,2,1,0:T(8,128)}), f32[128,2,8,256]{3,2,1,0:T(8,128)S(1)}, u32[]{:S(2)}, u32[]{:S(2)}) async-start(f32[128,2,8,256]{3,2,1,0:T(8,128)} %get-tuple-element.124), calls=%async_computation.16 | async-start | bytes 4194304 | tf_op jit(solution)/shard_map/all_to_all | solution.py:529
  612.7 48.4 %collective-permute-start.3 = (f32[2,64,8,256]{3,2,1,0:T(8,128)S(1)}, f32[2,64,8,256]{3,2,1,0:T(8,128)S(1)}, u32[]{:S(2)}, u32[]{:S(2)}) collective-permute-start(f32[2,64,8,256]{3,2,1,0:T(8,128)S(1)} %copy-done.10), channel_id=1, source_target_pairs={{0,4},{4,0},{1,5},{5,1},{2,6},{6,2},{3,7},{7,3},{8,12},{12,8},{9,1... | collective-permute-start | bytes 3145736 | tf_op jit(solution)/shard_map/ppermute | solution.py:425
  706.1 19.8 %all-to-all-start.18 = ((f32[32,2,2,8,256]{4,3,2,1,0:T(8,128)}), f32[32,2,2,8,256]{4,3,2,1,0:T(8,128)S(1)}, u32[]{:S(2)}, u32[]{:S(2)}) async-start(f32[32,2,2,8,256]{4,3,2,1,0:T(8,128)} %bitcast.132), calls=%async_computation.18 | async-start | bytes 2097152 | tf_op jit(solution)/shard_map/all_to_all | solution.py:536
  774.5 31.4 %all-to-all-start.21 = ((f32[128,2,8,256]{3,2,1,0:T(8,128)}), f32[128,2,8,256]{3,2,1,0:T(8,128)S(1)}, u32[]{:S(2)}, u32[]{:S(2)}) async-start(f32[128,2,8,256]{3,2,1,0:T(8,128)} %get-tuple-element.134), calls=%async_computation.21 | async-start | bytes 4194304 | tf_op jit(solution)/shard_map/all_to_all | solution.py:529
  843.4 19.8 %all-to-all-start.22 = ((f32[32,2,2,8,256]{4,3,2,1,0:T(8,128)}), f32[32,2,2,8,256]{4,3,2,1,0:T(8,128)S(1)}, u32[]{:S(2)}, u32[]{:S(2)}) async-start(f32[32,2,2,8,256]{4,3,2,1,0:T(8,128)} %bitcast.128), calls=%async_computation.22 | async-start | bytes 2097152 | tf_op jit(solution)/shard_map/all_to_all | solution.py:536
  864.2 43.5 %all-to-all-start.23 = ((f32[96,2,2,8,256]{4,3,2,1,0:T(8,128)}), f32[96,2,2,8,256]{4,3,2,1,0:T(8,128)S(1)}, u32[]{:S(2)}, u32[]{:S(2)}) async-start(f32[96,2,2,8,256]{4,3,2,1,0:T(8,128)} %bitcast.134), calls=%async_computation.23 | async-start | bytes 6291456 | tf_op jit(solution)/shard_map/all_to_all | solution.py:536
  946.4 71.0 %collective-permute-start.4 = (f32[3,64,8,256]{3,2,1,0:T(8,128)}, f32[3,64,8,256]{3,2,1,0:T(8,128)S(1)}, u32[]{:S(2)}, u32[]{:S(2)}) collective-permute-start(f32[3,64,8,256]{3,2,1,0:T(8,128)} %get-tuple-element.142), channel_id=1, source_target_pairs={{0,4},{4,0},{1,5},{5,1},{2,6},{6,2},{3,7},{7,3},{8,12},{12,8},{9,1... | collective-permute-start | bytes 4718600 | tf_op jit(solution)/shard_map/ppermute | solution.py:425
  1021.6 112.6 %all-to-all-start.25 = ((f32[4,2,64,8,256]{4,3,2,1,0:T(8,128)}), f32[4,2,64,8,256]{4,3,2,1,0:T(8,128)}, u32[]{:S(2)}, u32[]{:S(2)}) async-start(f32[4,2,64,8,256]{4,3,2,1,0:T(8,128)} %broadcast_in_dim.20), calls=%async_computation.25 | async-start | bytes 8388608 | tf_op jit(solution)/shard_map/all_to_all | solution.py:618
  1031.3 72.2 %collective-permute-start.8 = (f32[1,64,2,8,256]{4,3,2,1,0:T(8,128)}, f32[1,64,2,8,256]{4,3,2,1,0:T(8,128)S(1)}, u32[]{:S(2)}, u32[]{:S(2)}) collective-permute-start(f32[1,64,2,8,256]{4,3,2,1,0:T(8,128)} %get-tuple-element.146), channel_id=1, source_target_pairs={{0,12},{4,24},{8,0},{12,20},{16,4},{20,16},{24,8},{28,28},{1,13},{... | collective-permute-start | bytes 3145736 | tf_op jit(solution)/shard_map/ppermute | solution.py:455
  1034.1 94.5 %collective-permute-start.7 = (f32[1,64,2,8,256]{4,3,2,1,0:T(8,128)}, f32[1,64,2,8,256]{4,3,2,1,0:T(8,128)S(1)}, u32[]{:S(2)}, u32[]{:S(2)}) collective-permute-start(f32[1,64,2,8,256]{4,3,2,1,0:T(8,128)} %get-tuple-element.145), channel_id=1, source_target_pairs={{0,8},{4,28},{8,12},{12,24},{16,0},{20,20},{24,4},{28,16},{1,9},{5... | collective-permute-start | bytes 3145736 | tf_op jit(solution)/shard_map/ppermute | solution.py:455
  1037.2 91.4 %collective-permute-start.6 = (f32[1,64,2,8,256]{4,3,2,1,0:T(8,128)}, f32[1,64,2,8,256]{4,3,2,1,0:T(8,128)}, u32[]{:S(2)}, u32[]{:S(2)}) collective-permute-start(f32[1,64,2,8,256]{4,3,2,1,0:T(8,128)} %get-tuple-element.144), channel_id=1, source_target_pairs={{0,4},{4,16},{8,8},{12,28},{16,12},{20,24},{24,0},{28,20},{1,5},{5... | collective-permute-start | bytes 3145736 | tf_op jit(solution)/shard_map/ppermute | solution.py:455
  1042.1 86.5 %collective-permute-start.5 = (f32[1,64,2,8,256]{4,3,2,1,0:T(8,128)S(1)}, f32[1,64,2,8,256]{4,3,2,1,0:T(8,128)}, u32[]{:S(2)}, u32[]{:S(2)}) collective-permute-start(f32[1,64,2,8,256]{4,3,2,1,0:T(8,128)S(1)} %get-tuple-element.143), channel_id=1, source_target_pairs={{0,0},{4,20},{8,4},{12,16},{16,8},{20,28},{24,12},{28,24},{1,1},{5... | collective-permute-start | bytes 3145736 | tf_op jit(solution)/shard_map/ppermute | solution.py:455
  (32 other events, 372.9 us)

commit v3 on v2

--- a/solution.py
+++ b/solution.py
@@ -9,6 +9,7 @@
 from jax.experimental import pallas as pl
 from jax.experimental.pallas import tpu as pltpu
 from jax.sharding import Mesh, PartitionSpec as P
+
 
 OUTER = 2
 WAVENUMBER = 2.0 * math.pi / 6.0
@@ -77,11 +78,6 @@
     ref[0, z, 1] = value[1]
 
 
-def put_spec(ref, z, value):
-    ref[z, 0] = value[0]
-    ref[z, 1] = value[1]
-
-
 def returned(refs, z):
     place, plane = divmod(z, sum(ref.shape[1] for ref in refs))
     for ref in refs:
@@ -95,10 +91,11 @@
         stage_one([returned(refs, n0 + rest * n1) for n1 in range(width)], n0, depth, 1, keep)
 
 
-def finish(spec, depth, width, rest, keep):
+def finish(spec, depth, rest, keep, *at):
     for j1 in range(rest):
-        for j0, value in enumerate(stage_two(j1, rest, depth, -1, keep)):
-            put_spec(spec, j1 + rest * j0, value)
+        for j0, (re, im) in enumerate(stage_two(j1, rest, depth, -1, keep)):
+            spec[(j1 + rest * j0, *at, 0)] = re
+            spec[(j1 + rest * j0, *at, 1)] = im
 
 
 def start_kernel(chi, inc, source, spec, keep):
@@ -114,14 +111,14 @@
             put(source, z, w)
             values.append(w)
         stage_one(values, n0, depth, -1, keep)
-    finish(spec, depth, width, rest, keep)
+    finish(spec, depth, rest, keep)
 
 
 def adjoint_kernel(first, scal, chi, inc, source, data, *refs):
     if first:
-        *fields, scat_out, resid, spec, keep_in, keep = refs
+        *fields, scat_out, spec, keep_in, keep, keep_resid = refs
     else:
-        field, resid, spec, keep = refs
+        field, spec, keep, keep_resid = refs
     depth = inc.shape[1]
     width, rest = factors(depth)
     object_weight, data_weight = scal[0, 0], scal[0, 1]
@@ -129,7 +126,7 @@
         invert_one(fields, depth, width, rest, keep_in)
     for k1 in range(width):
         scattered = stage_two(k1, width, depth, 1, keep_in) if first else None
-        values = []
+        values, resid = [], []
         for k0 in range(rest):
             z = k1 + width * k0
             if first:
@@ -141,37 +138,31 @@
             er, ei = pair(inc, z)
             wr, wi = pair(source, z)
             ur, ui = er + sr, ei + si
-            rr = cr * ur - ci * ui - wr
-            ri = cr * ui + ci * ur - wi
-            put(resid, z, (rr, ri))
-            vr = -object_weight * (cr * rr + ci * ri)
-            vi = -object_weight * (cr * ri - ci * rr)
+            rr = object_weight * (cr * ur - ci * ui - wr)
+            ri = object_weight * (cr * ui + ci * ur - wi)
+            vr = -(cr * rr + ci * ri)
+            vi = ci * rr - cr * ri
             if z == 0:
                 vr = vr + data_weight * (data[0, 0] - sr)
                 vi = vi + data_weight * (data[0, 1] - si)
             values.append((vr, vi))
+            resid.append((rr, ri))
         stage_one(values, k1, depth, -1, keep)
-    finish(spec, depth, width, rest, keep)
-
-
-def descent_kernel(scal, resid, *refs):
-    *fields, descent, spec, sums, keep_in, keep = refs
-    depth = resid.shape[1]
+        stage_one(resid, k1, depth, -1, keep_resid)
+    finish(spec, depth, rest, keep, 0)
+    finish(spec, depth, rest, keep_resid, 1)
+
+
+def descent_kernel(*refs):
+    *fields, descent, sums, keep_in = refs
+    depth = descent.shape[1]
     width, rest = factors(depth)
-    object_weight = scal[0, 0]
     invert_one(fields, depth, width, rest, keep_in)
     total = jnp.zeros(sums.shape[3:], F32)
     for k1 in range(width):
-        values = []
-        for k0, (gr, gi) in enumerate(stage_two(k1, width, depth, 1, keep_in)):
-            z = k1 + width * k0
-            rr, ri = pair(resid, z)
-            dr, di = gr + object_weight * rr, gi + object_weight * ri
-            put(descent, z, (dr, di))
+        for k0, (dr, di) in enumerate(stage_two(k1, width, depth, 1, keep_in)):
+            put(descent, k1 + width * k0, (dr, di))
             total = total + (dr * dr + di * di)
-            values.append((dr, di))
-        stage_one(values, k1, depth, -1, keep)
-    finish(spec, depth, width, rest, keep)
     sums[0, 0, 0] = total
 
 
@@ -285,33 +276,30 @@
     )
 
 
-def plane_kernel(sign, scale, lz, lx, ly, xf, xb, yf, yb, own_ref, other_ref, out):
-    senders, _, _, rows, ny = own_ref.shape
-    hx, hy = senders * rows, ny // 2
-    own = [own_ref[:, 0, c].reshape(hx, ny) for c in (0, 1)]
-    other = [other_ref[:, 0, c].reshape(hx, ny) for c in (0, 1)]
+def lateral(own, other, xf, yf):
+    hx, ny = own[0].shape
+    hy = ny // 2
     across = [
         left_mul(xf, 0, jnp.concatenate([own[0] + other[0], own[1] + other[1]], axis=0)),
         left_mul(xf, 1, jnp.concatenate([own[0] - other[0], own[1] - other[1]], axis=0)),
     ]
     real = jnp.concatenate([across[0][:hx], across[1][:hx]], axis=0)
     imag = jnp.concatenate([across[0][hx:], across[1][hx:]], axis=0)
-    wave_sq = WAVENUMBER * WAVENUMBER
-    back = []
+    spectra = []
     for odd in (0, 1):
         flip = -1.0 if odd else 1.0
         folded = jnp.concatenate(
             [real[:, :hy] + flip * real[:, hy:], imag[:, :hy] + flip * imag[:, hy:]], axis=1
         )
         freq = right_mul(folded, yf, odd)
-        eigen = (lx[...] + lz[pl.program_id(0)]) + ly[odd]
-        real_den = eigen - wave_sq
-        imag_den = wave_sq * DAMPING
-        factor = (wave_sq * scale) / (real_den * real_den + imag_den * imag_den)
-        gr, gi = factor * real_den, factor * (imag_den * sign)
-        fr, fi = freq[:, :hy], freq[:, hy:]
-        filtered = jnp.concatenate([fr * gr - fi * gi, fr * gi + fi * gr], axis=1)
-        back.append(right_mul(filtered, yb, odd))
+        spectra.append((freq[:, :hy], freq[:, hy:]))
+    return spectra
+
+
+def lateral_back(spectra, xb, yb, out):
+    back = [right_mul(jnp.concatenate(spectra[odd], axis=1), yb, odd) for odd in (0, 1)]
+    senders, _, _, _, rows, ny = out.shape
+    hx, hy = senders * rows, ny // 2
     plus, minus = back[0] + back[1], back[0] - back[1]
     real = jnp.concatenate([plus[:, :hy], minus[:, :hy]], axis=1)
     imag = jnp.concatenate([plus[:, hy:], minus[:, hy:]], axis=1)
@@ -321,6 +309,45 @@
     for c in (0, 1):
         out[:, 0, c, 0] = plus[c * hx : (c + 1) * hx].reshape(senders, rows, ny)
         out[:, 0, c, 1] = minus[c * hx : (c + 1) * hx].reshape(senders, rows, ny)
+
+
+def filtered(value, sign, scale, lz, lx, ly, odd):
+    wave_sq = WAVENUMBER * WAVENUMBER
+    eigen = (lx[...] + lz[pl.program_id(0)]) + ly[odd]
+    real_den = eigen - wave_sq
+    imag_den = wave_sq * DAMPING
+    factor = (wave_sq * scale) / (real_den * real_den + imag_den * imag_den)
+    gr, gi = factor * real_den, factor * (imag_den * sign)
+    fr, fi = value
+    return fr * gr - fi * gi, fr * gi + fi * gr
+
+
+def loaded(ref, *at):
+    return [ref[(slice(None), 0, *at, c)].reshape(-1, ref.shape[-1]) for c in (0, 1)]
+
+
+def plane_kernel(scale, lz, lx, ly, xf, xb, yf, yb, own, other, out):
+    spectra = lateral(loaded(own), loaded(other), xf, yf)
+    lateral_back([filtered(spectra[odd], 1.0, scale, lz, lx, ly, odd) for odd in (0, 1)], xb, yb, out)
+
+
+def adjoint_plane_kernel(scale, lz, lx, ly, xf, xb, yf, yb, own, other, out, keep):
+    inner = lateral(loaded(own, 0), loaded(other, 0), xf, yf)
+    resid = lateral(loaded(own, 1), loaded(other, 1), xf, yf)
+    spectra = []
+    for odd in (0, 1):
+        re, im = filtered(inner[odd], -1.0, scale, lz, lx, ly, odd)
+        re, im = re + scale * resid[odd][0], im + scale * resid[odd][1]
+        keep[0, odd, 0], keep[0, odd, 1] = re, im
+        spectra.append((re, im))
+    lateral_back(spectra, xb, yb, out)
+
+
+def image_plane_kernel(lz, lx, ly, xb, yb, kept, out):
+    spectra = [
+        filtered((kept[0, odd, 0], kept[0, odd, 1]), 1.0, 1.0, lz, lx, ly, odd) for odd in (0, 1)
+    ]
+    lateral_back(spectra, xb, yb, out)
 
 
 SMEM = pl.BlockSpec(memory_space=pltpu.SMEM)
@@ -346,6 +373,7 @@
         return {
             "field": ((s, z, 2, q, y), (1, z, 2, q, lanes), lambda j, i: (i, 0, 0, 0, j)),
             "spec": ((s * z, 2, q, y), (z, 2, q, lanes), lambda j, i: (i, 0, 0, j)),
+            "twin": ((s * z, 2, 2, q, y), (z, 2, 2, q, lanes), lambda j, i: (i, 0, 0, 0, j)),
             "chi": ((2, z, q, y), (2, z, q, lanes), lambda j, i: (0, 0, 0, j)),
             "data": ((s, 2, q, y), (1, 2, q, lanes), lambda j, i: (i, 0, 0, j)),
             "sum1": (turns + (1, q, lanes), (1, 1, 1, q, lanes), lambda j, i: (j, i, 0, 0, 0)),
@@ -354,7 +382,7 @@
             "parts": ((3, z, q, y), (3, deep, q, lanes), lambda j, i: (0, i, 0, j)),
         }[name]
 
-    def call(self, kernel, name, chunk, ins, outs, scratch, *args):
+    def call(self, kernel, chunk, ins, outs, scratch, *args):
         def spec(kind):
             if kind == "scal":
                 return SMEM
@@ -372,46 +400,54 @@
             out_shape=[jax.ShapeDtypeStruct(self.kind(k, chunk)[0], F32) for k in outs],
             scratch_shapes=[pltpu.VMEM((self.depth, 2, self.rows, self.lanes), F32)] * scratch,
             cost_estimate=pl.CostEstimate(flops=moved * 4, bytes_accessed=moved, transcendentals=0),
-            name=name,
         )(*args)
 
     def piece_kinds(self):
         return tuple("piece%d" % m for m in range(len(self.pieces)))
 
 
-def filter_planes(own, other, first, count, senders, lz, shared, sign, scale):
-    _, parts, rows, ny = own.shape
-    planes = own.shape[0] // senders
+def plane_call(kernel, senders, lz, tables, ins, work, rows, ny, kept_in=None, keeps=False):
+    planes = lz.shape[0]
     dense = rows % 8 != 0
+    lead, deep = (1, senders * rows) if dense else (senders, rows)
 
     def shaped(value):
-        value = value.reshape(senders, planes, parts, rows, ny)
+        inner = value.shape[1:-2]
+        value = value.reshape((senders, planes) + value.shape[1:])
         if dense:
-            value = value.transpose(1, 2, 0, 3, 4).reshape(1, planes, parts, senders * rows, ny)
+            value = jnp.moveaxis(value, 0, -3).reshape((1, planes) + inner + (deep, ny))
         return value
 
-    own, other = shaped(own), shaped(other)
-    lead, deep = own.shape[0], own.shape[3]
-    out_shape = (lead, count, parts, 2, deep, ny)
+    ins = [shaped(v) for v in ins]
+    nx = 2 * senders * rows
     whole = lambda t: pl.BlockSpec(t.shape, lambda i, n=t.ndim: (0,) * n)
-    block = pl.BlockSpec((lead, 1, parts, deep, ny), lambda i: (0, i + first, 0, 0, 0))
-    nx = 2 * senders * rows
-    out = pl.pallas_call(
-        partial(plane_kernel, sign, scale),
-        grid=(count,),
-        in_specs=[SMEM] + [whole(t) for t in shared] + [block, block],
-        out_specs=pl.BlockSpec((lead, 1, parts, 2, deep, ny), lambda i: (0, i, 0, 0, 0, 0)),
-        out_shape=jax.ShapeDtypeStruct(out_shape, F32),
+    plane = lambda shape: pl.BlockSpec(
+        (shape[0], 1) + tuple(shape[2:]), lambda i, n=len(shape): (0, i) + (0,) * (n - 2)
+    )
+    kept = (planes, 2, 2, nx, ny // 2)
+    kept_spec = pl.BlockSpec((1,) + kept[1:], lambda i: (i, 0, 0, 0, 0))
+    out_shape = (lead, planes, 2, 2, deep, ny)
+    shapes, specs = [jax.ShapeDtypeStruct(out_shape, F32)], [plane(out_shape)]
+    if keeps:
+        shapes.append(jax.ShapeDtypeStruct(kept, F32))
+        specs.append(kept_spec)
+    result = pl.pallas_call(
+        kernel,
+        grid=(planes,),
+        in_specs=[SMEM] + [whole(t) for t in tables] + [plane(v.shape) for v in ins]
+        + ([kept_spec] if kept_in is not None else []),
+        out_specs=specs,
+        out_shape=shapes,
         cost_estimate=pl.CostEstimate(
-            flops=count * 24 * nx * nx * ny * 2,
-            bytes_accessed=2 * math.prod(out_shape) * 4,
+            flops=planes * work * 3 * nx * nx * ny * 2,
+            bytes_accessed=work * math.prod(out_shape),
             transcendentals=0,
         ),
-        name="planes",
-    )(lz[first : first + count], *shared, own, other)
+    )(lz, *tables, *ins, *([kept_in] if kept_in is not None else []))
+    out = result[0]
     if dense:
-        out = out.reshape(count, parts, 2, senders, rows, ny).transpose(3, 0, 1, 2, 4, 5)
-    return out
+        out = jnp.moveaxis(out.reshape((planes, 2, 2, senders, rows, ny)), 3, 0)
+    return (out, result[1]) if keeps else out
 
 
 def everyone(values):
@@ -439,21 +475,26 @@
     )
 
 
-def deliver(chunks, shares, per_share, share, half, gate):
+def payloads(chunks, shares, per_share, share):
+    sent = []
+    for t in range(shares):
+        number = lax.rem(share + t, shares)
+        cut = [lax.dynamic_slice_in_dim(w, number // 2 * per_share, per_share, axis=0) for w in chunks]
+        sent.append(jnp.where(number % 2 == 0, cut[0], cut[1]))
+    return sent
+
+
+def deliver(sent, shares, per_share, share, half, gate):
     slots = shares // 2
     rounds = []
     for t in range(shares):
-        number = lax.rem(share + t, shares)
-        slot = number // 2
-        cut = [lax.dynamic_slice_in_dim(w, slot * per_share, per_share, axis=0) for w in chunks]
-        sent = after(jnp.where(number % 2 == 0, cut[0], cut[1]), gate)
         pairs = []
         for a in range(shares):
             g, c = divmod((a + t) % shares, 2)
             for h in (0, 1):
                 pairs.append((a * 2 + h, (h * slots + g) * 2 + (h + c) % 2))
-        rounds.append(lax.ppermute(sent, ("src", "half"), pairs))
-    spot = 2 * lax.rem(share, slots) + lax.rem(half + share // slots, 2)
+        rounds.append(lax.ppermute(sent[t], ("src", "half"), pairs))
+    spot = after(2 * lax.rem(share, slots) + lax.rem(half + share // slots, 2), gate)
     _, depth, _, rows, ny = rounds[0].shape
     whole = pl.BlockSpec(rounds[0].shape, lambda a: (0, 0, 0, 0, 0))
     out = pl.pallas_call(
@@ -478,8 +519,7 @@
     total_sources = per_share * shares
     sources = total_sources // 2
     planes = sources * depth // senders
-    pieces = (planes // 4, planes - planes // 4) if planes >= 4 else (planes,)
-    slabs = Slabs(sources, depth, rows, ny, pieces)
+    slabs = Slabs(sources, depth, rows, ny, (planes,))
 
     chi_own = lax.dynamic_index_in_dim(
         contrast.reshape(2, depth, shares, rows, ny), share, axis=2, keepdims=False
@@ -518,25 +558,23 @@
     flip = lambda t: high_low(np.swapaxes(t, -1, -2))
     lx = np.broadcast_to(lateral_modes(nx)[:, None], (nx, ny // 2))
     ly = lateral_modes(ny).reshape(2, 1, ny // 2)
-    shared = [jnp.asarray(t) for t in (lx, ly, high_low(x_table), flip(x_table), flip(y_table), high_low(y_table))]
+    lx, ly, xf, xb, yf, yb = (
+        jnp.asarray(t) for t in (lx, ly, high_low(x_table), flip(x_table), flip(y_table), high_low(y_table))
+    )
     place = share * rest_count + rest
     modes = (place * planes + jnp.arange(planes)) % depth
     half_sine = jnp.sin(math.pi * modes.astype(F32) / depth)
     lz = 4.0 * half_sine * half_sine
     scale = 1.0 / (nx * ny * depth)
 
-    def forward(spec):
-        return lax.all_to_all(spec, GROUP, 0, 0, tiled=True)
-
-    def back(came, sign):
-        out, first = [], 0
-        for count in pieces:
-            part = filter_planes(*came, first, count, senders, lz, shared, sign, scale)
-            shape = part.shape
-            part = lax.all_to_all(part.reshape((-1,) + shape[2:]), GROUP, 0, 0, tiled=True)
-            out.append(part.reshape(shape))
-            first += count
-        return out
+    def exchange(value):
+        flat = value.reshape((senders * planes,) + value.shape[-4:])
+        return lax.all_to_all(flat, GROUP, 0, 0, tiled=True).reshape(value.shape)
+
+    call_planes = lambda kernel, tables, ins, work, **kw: plane_call(
+        kernel, senders, lz, tables, ins, work, rows, ny, **kw
+    )
+    tables = (lx, ly, xf, xb, yf, yb)
 
     both = (0, 1)
     piece_kinds = slabs.piece_kinds()
@@ -545,48 +583,40 @@
     object_total = totals[1]
     source, came = [None, None], [None, None]
     for c in both:
-        source[c], spec = slabs.call(
-            start_kernel, "start", c, ("chi", "field"), ("field", "spec"), 1, chi[c], inc[c]
-        )
-        came[c] = forward(spec)
-    fields = back(came, 1.0)
+        source[c], spec = slabs.call(start_kernel, c, ("chi", "field"), ("field", "spec"), 1, chi[c], inc[c])
+        came[c] = lax.all_to_all(spec, GROUP, 0, 0, tiled=True)
+    fields = exchange(call_planes(partial(plane_kernel, scale), tables, came, 8))
     scattered = [None, None]
     for outer in range(OUTER):
         object_weight = 1.0 / object_total
         weights = jnp.stack([object_weight, data_weight]).reshape(1, 2)
         first, last = outer == 0, outer == OUTER - 1
-        resid, descent, image = [None, None], [None, None], [None, None]
-        came = [None, None]
+        descent, image, came = [None, None], [None, None], [None, None]
         for c in both:
             out = slabs.call(
                 partial(adjoint_kernel, first),
-                "adjoint",
                 c,
                 ("scal", "chi", "field", "field", "data") + (piece_kinds if first else ("field",)),
-                ("field", "field", "spec") if first else ("field", "spec"),
-                2 if first else 1,
-                weights, chi[c], inc[c], source[c], data[c], *(fields if first else (scattered[c],)),
+                ("field", "twin") if first else ("twin",),
+                3 if first else 2,
+                weights, chi[c], inc[c], source[c], data[c], *((fields,) if first else (scattered[c],)),
             )
             if first:
                 scattered[c] = out[0]
-            resid[c] = out[-2]
-            came[c] = forward(out[-1])
-        fields = back(came, -1.0)
-        came, sums = [None, None], []
+            came[c] = lax.all_to_all(out[-1], GROUP, 0, 0, tiled=True)
+        part, kept = call_planes(partial(adjoint_plane_kernel, scale), tables, came, 12, keeps=True)
+        fields = exchange(part)
+        fields_image = exchange(call_planes(image_plane_kernel, (lx, ly, xb, yb), [], 4, kept_in=kept))
+        sums = []
         for c in both:
-            descent[c], spec, part = slabs.call(
-                descent_kernel, "descent", c, ("scal", "field") + piece_kinds, ("field", "spec", "sum1"), 2,
-                weights, resid[c], *fields,
-            )
-            came[c] = forward(spec)
+            descent[c], part = slabs.call(descent_kernel, c, piece_kinds, ("field", "sum1"), 1, fields)
             sums.append(part)
         sum_d = jnp.sum(sums[0]) + jnp.sum(sums[1])
-        fields = back(came, 1.0)
         sums = []
         for c in both:
             image[c], part = slabs.call(
-                image_kernel, "image", c, ("field", "chi") + piece_kinds, ("field", "sum2"), 1,
-                descent[c], chi[c], *fields,
+                image_kernel, c, ("field", "chi") + piece_kinds, ("field", "sum2"), 1,
+                descent[c], chi[c], fields_image,
             )
             sums.append(part)
         sum_q = sums[0] + sums[1]
@@ -596,7 +626,6 @@
         for c in (1, 0):
             out = slabs.call(
                 partial(step_kernel, last),
-                "step",
                 c,
                 ("scal",) + ("every",) * 5,
                 ("every",) * (1 if last else 2) + ("parts",),
@@ -607,16 +636,19 @@
             if not last:
                 scattered[c] = out[1]
         received = swap_halves(parts[1])
+        if last:
+            sent = payloads(source, shares, per_share, share)
+            received, *sent = lax.optimization_barrier((received, *sent))
         sums = parts[0] + received
         chi_own = bounded(sums[0], sums[1], sums[2], total_sources)
         if not last:
             object_total = everyone([total_sources * jnp.sum(chi_own * chi_own)])[0]
             chi = [chi_own, swap_halves(after(chi_own, object_total))]
 
-    contrast_sources = deliver(source, shares, per_share, share, half, received)
-    sent = jnp.broadcast_to(chi_own[None], (shares,) + chi_own.shape)
-    contrast_new = lax.all_to_all(sent, "src", 0, 0, tiled=True)
+    copies = jnp.broadcast_to(chi_own[None], (shares,) + chi_own.shape)
+    contrast_new = lax.all_to_all(copies, "src", 0, 0, tiled=True)
     contrast_new = contrast_new.transpose(1, 2, 0, 3, 4).reshape(contrast.shape)
+    contrast_sources = deliver(sent, shares, per_share, share, half, contrast_new)
     return contrast_sources, contrast_new
 
 
@@ -624,6 +656,7 @@
     shares, spaces = mesh.shape["src"], mesh.shape["space"]
     split_mesh = Mesh(mesh.devices.reshape(shares, 2, spaces // 2), ALL)
     space = ("half", "rest")
+
     return jax.shard_map(
         on_device,
         mesh=split_mesh,

time: 1150 us -> 1100 us (0.957)
  blocking collectives: 248 us -> 145 us
  waiting for transfers between devices: 521 us -> 612 us
  Pallas kernels: 203 us -> 184 us
    all_to_all x15 -> x10, waiting for transfers between devices: 185 us -> 310 us  [the longest x5 167 us: exchange(): return lax.all_to_all(flat, GROUP, 0, 0, tiled=True).reshape(value.shape)]
    all_to_all x6 -> x2, blocking collectives: 214 us -> 110 us  [on_device(): came[c] = lax.all_to_all(out[-1], GROUP, 0, 0, tiled=True)]
    ppermute x4, waiting for transfers between devices: 84.8 us -> 16.7 us  [deliver(): rounds.append(lax.ppermute(sent[t], ('src', 'half'), pairs))]
    ppermute x5, waiting for transfers between devices: 249 us -> 283 us  [swap_halves(): return lax.ppermute(value, 'half', [(0, 1), (1, 0)])]
    pallas_call x10 -> x5, Pallas kernels: 87.5 us -> 71.1 us  [plane_call(): pl.pallas_call(kernel, grid=(planes,), in_specs=[SMEM] + [whole(t) for t...]
    all_to_all x15 -> x10, starting transfers between devices: 65.1 us -> 53.8 us  [the longest x5 25.7 us: exchange(): return lax.all_to_all(flat, GROUP, 0, 0, tiled=True).reshape(value.shape)]
  transfers between devices with their start and end apart: 26 -> 21, of which waited for: 20 -> 14; matrix products, arithmetic and copies ran while one was open for 2% -> 2% of each run, Pallas kernels for 10% -> 8%
where the time goes in v3:
time: 1100 us
  waiting for transfers between devices  612 us (56%)
  Pallas kernels  184 us (17%)
  blocking collectives  145 us (13%)
  starting transfers between devices  89.8 us (8%)
  other arithmetic  41.1 us (4%)
  local copies, waits for them, and re-layouts  15.8 us (1%)
    ppermute x5, waiting for transfers between devices, swap_halves(): return lax.ppermute(value, 'half', [(0, 1), (1, 0)])  283 us
    all_to_all x5, waiting for transfers between devices, exchange(): return lax.all_to_all(flat, GROUP, 0, 0, tiled=True).reshape(value.shape)  167 us
    all_to_all x2, blocking collectives, on_device(): came[c] = lax.all_to_all(out[-1], GROUP, 0, 0, tiled=True)  110 us
    pallas_call x18, Pallas kernels, call(): pl.pallas_call(kernel, grid=(self.ny // self.lanes, second), in_specs=[sp...  108 us
    all_to_all x1, waiting for transfers between devices, on_device(): contrast_new = lax.all_to_all(copies, 'src', 0, 0, tiled=True)  73.2 us
    pallas_call x5, Pallas kernels, plane_call(): pl.pallas_call(kernel, grid=(planes,), in_specs=[SMEM] + [whole(t) for t...  71.1 us
    all_to_all x2, waiting for transfers between devices, on_device(): came[c] = lax.all_to_all(out[-1], GROUP, 0, 0, tiled=True)  44.9 us
    all_to_all x3, blocking collectives, everyone(): return jnp.sum(lax.all_to_all(sent, ALL, 0, 0, tiled=True), axis=0)  35.1 us
  transfers between devices with their start and end apart: 21, of which 14 were waited for; matrix products, arithmetic and copies ran while one was open for 2% of the time, Pallas kernels for 8%

profile of v3, /device:TPU:0, one launch (start us, length us, event | category | flops | bytes accessed | tf_op | source)
XLA Modules:
  0.0 1097.0 jit_solution(1207024921427443420)
XLA Ops:
  13.5 9.0 fusion.1
  38.6 42.9 %collective-permute-done.chi = f32[2,64,8,256]{3,2,1,0:T(8,128)S(1)} collective-permute-done((f32[2,64,8,256]{3,2,1,0:T(8,128)S(1)}, f32[2,64,8,256]{3,2,1,0:T(8,128)S(1)}, u32[]{:S(2)}, u32[]{:S(2)}) %collective-permute-start) | collective-permute-done | bytes 1048608 | tf_op jit(solution)/shard_map/ppermute | solution.py:461
  97.1 25.1 %all-to-all-done.3 = f32[128,2,8,256]{3,2,1,0:T(8,128)S(1)} async-done(((f32[128,2,8,256]{3,2,1,0:T(8,128)}), f32[128,2,8,256]{3,2,1,0:T(8,128)S(1)}, u32[]{:S(2)}, u32[]{:S(2)}) %all-to-all-start.3) | async-done | bytes 2097184 | tf_op jit(solution)/shard_map/all_to_all | solution.py:587
  127.1 14.0 %shard_map.106 = f32[16,8,2,2,8,256]{5,4,3,2,1,0:T(8,128)} custom-call(f32[8]{0:T(128)} %multiply_multiply_fusion.lz, f32[256,128]{1,0:T(8,128)} %jit_solution_.3.lx, f32[2,1,128]{2,1,0:T(1,128)} %constant.258.clone.ly, bf16[2,2,256,256]{3,2,1,0:T(8,128)(2,1)} %constant.259.clone.xf, bf16[2,2,256,256]{3,2,1,0:T(8,128)(2,1)} %constant.260.clone.xb, ...), custom_call_target="tpu_custom_call" | custom-call | flops 6442450944 | bytes 8388608 | tf_op jit(solution)/shard_map/pallas_call | solution.py:434
  151.9 47.1 %collective-permute-done.1.data = f32[2,2,8,256]{3,2,1,0:T(8,128)S(1)} collective-permute-done((f32[2,2,8,256]{3,2,1,0:T(8,128)S(1)}, f32[2,2,8,256]{3,2,1,0:T(8,128)S(1)}, u32[]{:S(2)}, u32[]{:S(2)}) %collective-permute-start.1) | collective-permute-done | bytes 32800 | tf_op jit(solution)/shard_map/ppermute | solution.py:461
  221.0 44.9 %all-to-all-done.6 = f32[128,2,2,8,256]{4,3,2,1,0:T(8,128)} async-done(((f32[128,2,2,8,256]{4,3,2,1,0:T(8,128)}), f32[128,2,2,8,256]{4,3,2,1,0:T(8,128)}, u32[]{:S(2)}, u32[]{:S(2)}) %all-to-all-start.6) | async-done | bytes 4194336 | tf_op jit(solution)/shard_map/all_to_all | solution.py:606
  266.0 55.5 %all_to_all.96 = f32[128,2,2,8,256]{4,3,2,1,0:T(8,128)} all-to-all(f32[128,2,2,8,256]{4,3,2,1,0:T(8,128)} %get-tuple-element.98), channel_id=1, replica_groups=mesh['src'=4,'half'=2,'rest'=4] {'src','rest'}, dimensions={0} | all-to-all | bytes 8388608 | tf_op jit(solution)/shard_map/all_to_all | solution.py:606
  321.4 18.4 %shard_map.109 = (f32[16,8,2,2,8,256]{5,4,3,2,1,0:T(8,128)}, f32[8,2,2,256,128]{4,3,2,1,0:T(8,128)}) custom-call(f32[8]{0:T(128)} %multiply_multiply_fusion.lz, f32[256,128]{1,0:T(8,128)} %jit_solution_.3.lx, f32[2,1,128]{2,1,0:T(1,128)} %constant.258.clone.ly, bf16[2,2,256,256]{3,2,1,0:T(8,128)(2,1)} %constant.259.clone.xf, ...), custom_call_target="tpu_custom_call" | custom-call | flops 9663676416 | bytes 12582912 | tf_op jit(solution)/shard_map/pallas_call | solution.py:434
  344.4 10.2 shard_map.112
  354.6 42.0 %all-to-all-done.7 = f32[128,2,2,8,256]{4,3,2,1,0:T(8,128)} async-done(((f32[128,2,2,8,256]{4,3,2,1,0:T(8,128)}), f32[128,2,2,8,256]{4,3,2,1,0:T(8,128)}, u32[]{:S(2)}, u32[]{:S(2)}) %all-to-all-start.7) | async-done | bytes 4194336 | tf_op jit(solution)/shard_map/all_to_all | solution.py:572
  413.4 41.4 %all-to-all-done.8 = f32[128,2,2,8,256]{4,3,2,1,0:T(8,128)} async-done(((f32[128,2,2,8,256]{4,3,2,1,0:T(8,128)}), f32[128,2,2,8,256]{4,3,2,1,0:T(8,128)}, u32[]{:S(2)}, u32[]{:S(2)}) %all-to-all-start.8) | async-done | bytes 4194336 | tf_op jit(solution)/shard_map/all_to_all | solution.py:572
  468.4 12.2 %all_to_all.97 = f32[32,1,128]{2,1,0:T(1,128)S(1)} all-to-all(f32[32,1,128]{2,1,0:T(1,128)S(1)} %broadcast_in_dim.17), channel_id=1, replica_groups=mesh['src'=4,'half'=2,'rest'=4] {'src','half','rest'}, dimensions={0} | all-to-all | bytes 32768 | tf_op jit(solution)/shard_map/all_to_all | solution.py:457
  501.4 61.6 %collective-permute-done.2 = f32[3,64,8,256]{3,2,1,0:T(8,128)S(1)} collective-permute-done((f32[3,64,8,256]{3,2,1,0:T(8,128)}, f32[3,64,8,256]{3,2,1,0:T(8,128)S(1)}, u32[]{:S(2)}, u32[]{:S(2)}) %collective-permute-start.2) | collective-permute-done | bytes 1572896 | tf_op jit(solution)/shard_map/ppermute | solution.py:461
  588.7 73.9 %collective-permute-done.3.chi = f32[2,64,8,256]{3,2,1,0:T(8,128)S(1)} collective-permute-done((f32[2,64,8,256]{3,2,1,0:T(8,128)S(1)}, f32[2,64,8,256]{3,2,1,0:T(8,128)S(1)}, u32[]{:S(2)}, u32[]{:S(2)}) %collective-permute-start.3) | collective-permute-done | bytes 1048608 | tf_op jit(solution)/shard_map/ppermute | solution.py:461
  670.2 54.7 %all_to_all.99 = f32[128,2,2,8,256]{4,3,2,1,0:T(8,128)} all-to-all(f32[128,2,2,8,256]{4,3,2,1,0:T(8,128)} %shard_map.118), channel_id=1, replica_groups=mesh['src'=4,'half'=2,'rest'=4] {'src','rest'}, dimensions={0} | all-to-all | bytes 8388608 | tf_op jit(solution)/shard_map/all_to_all | solution.py:606
  724.9 18.4 %shard_map.119 = (f32[16,8,2,2,8,256]{5,4,3,2,1,0:T(8,128)}, f32[8,2,2,256,128]{4,3,2,1,0:T(8,128)}) custom-call(f32[8]{0:T(128)} %multiply_multiply_fusion.lz, f32[256,128]{1,0:T(8,128)} %jit_solution_.3.lx, f32[2,1,128]{2,1,0:T(1,128)} %constant.258.clone.ly, bf16[2,2,256,256]{3,2,1,0:T(8,128)(2,1)} %constant.259.clone.xf, ...), custom_call_target="tpu_custom_call" | custom-call | flops 9663676416 | bytes 12582912 | tf_op jit(solution)/shard_map/pallas_call | solution.py:434
  747.9 10.2 shard_map.122
  758.1 42.0 %all-to-all-done.13 = f32[128,2,2,8,256]{4,3,2,1,0:T(8,128)} async-done(((f32[128,2,2,8,256]{4,3,2,1,0:T(8,128)}), f32[128,2,2,8,256]{4,3,2,1,0:T(8,128)}, u32[]{:S(2)}, u32[]{:S(2)}) %all-to-all-start.13) | async-done | bytes 4194336 | tf_op jit(solution)/shard_map/all_to_all | solution.py:572
  816.8 41.3 %all-to-all-done.14 = f32[128,2,2,8,256]{4,3,2,1,0:T(8,128)} async-done(((f32[128,2,2,8,256]{4,3,2,1,0:T(8,128)}), f32[128,2,2,8,256]{4,3,2,1,0:T(8,128)}, u32[]{:S(2)}, u32[]{:S(2)}) %all-to-all-start.14) | async-done | bytes 4194336 | tf_op jit(solution)/shard_map/all_to_all | solution.py:572
  872.0 14.0 %all_to_all.100 = f32[32,1,128]{2,1,0:T(1,128)S(1)} all-to-all(f32[32,1,128]{2,1,0:T(1,128)S(1)} %broadcast_in_dim.19), channel_id=1, replica_groups=mesh['src'=4,'half'=2,'rest'=4] {'src','half','rest'}, dimensions={0} | all-to-all | bytes 32768 | tf_op jit(solution)/shard_map/all_to_all | solution.py:457
  910.1 57.7 %collective-permute-done.4 = f32[3,64,8,256]{3,2,1,0:T(8,128)} collective-permute-done((f32[3,64,8,256]{3,2,1,0:T(8,128)}, f32[3,64,8,256]{3,2,1,0:T(8,128)}, u32[]{:S(2)}, u32[]{:S(2)}) %collective-permute-start.4) | collective-permute-done | bytes 1572896 | tf_op jit(solution)/shard_map/ppermute | solution.py:461
  977.1 9.5 collective-permute-start.5
  997.6 73.2 %all-to-all-done.16 = f32[4,2,64,8,256]{4,3,2,1,0:T(8,128)} async-done(((f32[4,2,64,8,256]{4,3,2,1,0:T(8,128)}), f32[4,2,64,8,256]{4,3,2,1,0:T(8,128)}, u32[]{:S(2)}, u32[]{:S(2)}) %all-to-all-start.16) | async-done | bytes 4194336 | tf_op jit(solution)/shard_map/all_to_all | solution.py:649
  1075.7 16.7 %collective-permute-done.8.refs_3_ = f32[1,64,2,8,256]{4,3,2,1,0:T(8,128)} collective-permute-done((f32[1,64,2,8,256]{4,3,2,1,0:T(8,128)S(1)}, f32[1,64,2,8,256]{4,3,2,1,0:T(8,128)}, u32[]{:S(2)}, u32[]{:S(2)}) %collective-permute-start.8) | collective-permute-done | bytes 1048608 | tf_op jit(solution)/shard_map/ppermute | solution.py:496
  (137 shorter events, 251.5 us)
Async XLA Ops:
  3.0 10.0 all-to-all-start.1
  28.6 58.7 %all-to-all-start.2 = ((f32[128,2,8,256]{3,2,1,0:T(8,128)}), f32[128,2,8,256]{3,2,1,0:T(8,128)}, u32[]{:S(2)}, u32[]{:S(2)}) async-start(f32[128,2,8,256]{3,2,1,0:T(8,128)} %get-tuple-element.96), calls=%async_computation.2 | async-start | bytes 4194304 | tf_op jit(solution)/shard_map/all_to_all | solution.py:587
  33.2 48.3 %collective-permute-start = (f32[2,64,8,256]{3,2,1,0:T(8,128)S(1)}, f32[2,64,8,256]{3,2,1,0:T(8,128)S(1)}, u32[]{:S(2)}, u32[]{:S(2)}) collective-permute-start(f32[2,64,8,256]{3,2,1,0:T(8,128)S(1)} %copy-done), channel_id=1, source_target_pairs={{0,4},{4,0},{1,5},{5,1},{2,6},{6,2},{3,7},{7,3},{8,12},{12,8},{9,1... | collective-permute-start | bytes 3145736 | tf_op jit(solution)/shard_map/ppermute | solution.py:461
  87.3 39.1 %copy-start.13 = (f32[256]{0:T(256)S(1)}, f32[256]{0:T(256)}, u32[]{:S(2)}) copy-start(f32[256]{0:T(256)} %constant.257.clone) | copy-start | bytes 3076
  87.3 34.9 %all-to-all-start.3 = ((f32[128,2,8,256]{3,2,1,0:T(8,128)}), f32[128,2,8,256]{3,2,1,0:T(8,128)S(1)}, u32[]{:S(2)}, u32[]{:S(2)}) async-start(f32[128,2,8,256]{3,2,1,0:T(8,128)} %get-tuple-element.97), calls=%async_computation.3 | async-start | bytes 4194304 | tf_op jit(solution)/shard_map/all_to_all | solution.py:587
  122.8 18.3 %all-to-all-start = ((f32[32,1,128]{2,1,0:T(1,128)}), f32[32,1,128]{2,1,0:T(1,128)S(1)}, u32[]{:S(2)}, u32[]{:S(2)}) async-start(f32[32,1,128]{2,1,0:T(1,128)} %broadcast_in_dim.14), calls=%async_computation | async-start | bytes 32768 | tf_op jit(solution)/shard_map/all_to_all | solution.py:457
  141.1 57.9 %all-to-all-start.4 = ((f32[128,2,2,8,256]{4,3,2,1,0:T(8,128)}), f32[128,2,2,8,256]{4,3,2,1,0:T(8,128)}, u32[]{:S(2)}, u32[]{:S(2)}) async-start(f32[128,2,2,8,256]{4,3,2,1,0:T(8,128)} %bitcast.73), calls=%async_computation.4 | async-start | bytes 8388608 | tf_op jit(solution)/shard_map/all_to_all | solution.py:572
  148.8 50.3 %collective-permute-start.1 = (f32[2,2,8,256]{3,2,1,0:T(8,128)S(1)}, f32[2,2,8,256]{3,2,1,0:T(8,128)S(1)}, u32[]{:S(2)}, u32[]{:S(2)}) collective-permute-start(f32[2,2,8,256]{3,2,1,0:T(8,128)S(1)} %get-tuple-element.162), channel_id=1, source_target_pairs={{0,4},{4,0},{1,5},{5,1},{2,6},{6,2},{3,7},{7,3},{8,12},{12,8},{9,1... | collective-permute-start | bytes 98312 | tf_op jit(solution)/shard_map/ppermute | solution.py:461
  207.0 59.0 %all-to-all-start.6 = ((f32[128,2,2,8,256]{4,3,2,1,0:T(8,128)}), f32[128,2,2,8,256]{4,3,2,1,0:T(8,128)}, u32[]{:S(2)}, u32[]{:S(2)}) async-start(f32[128,2,2,8,256]{4,3,2,1,0:T(8,128)} %get-tuple-element.100), calls=%async_computation.6 | async-start | bytes 8388608 | tf_op jit(solution)/shard_map/all_to_all | solution.py:606
  339.8 56.7 %all-to-all-start.7 = ((f32[128,2,2,8,256]{4,3,2,1,0:T(8,128)}), f32[128,2,2,8,256]{4,3,2,1,0:T(8,128)}, u32[]{:S(2)}, u32[]{:S(2)}) async-start(f32[128,2,2,8,256]{4,3,2,1,0:T(8,128)} %bitcast.78), calls=%async_computation.7 | async-start | bytes 8388608 | tf_op jit(solution)/shard_map/all_to_all | solution.py:572
  396.5 58.2 %all-to-all-start.8 = ((f32[128,2,2,8,256]{4,3,2,1,0:T(8,128)}), f32[128,2,2,8,256]{4,3,2,1,0:T(8,128)}, u32[]{:S(2)}, u32[]{:S(2)}) async-start(f32[128,2,2,8,256]{4,3,2,1,0:T(8,128)} %bitcast.76), calls=%async_computation.8 | async-start | bytes 8388608 | tf_op jit(solution)/shard_map/all_to_all | solution.py:572
  492.1 71.0 %collective-permute-start.2 = (f32[3,64,8,256]{3,2,1,0:T(8,128)}, f32[3,64,8,256]{3,2,1,0:T(8,128)S(1)}, u32[]{:S(2)}, u32[]{:S(2)}) collective-permute-start(f32[3,64,8,256]{3,2,1,0:T(8,128)} %get-tuple-element.114), channel_id=1, source_target_pairs={{0,4},{4,0},{1,5},{5,1},{2,6},{6,2},{3,7},{7,3},{8,12},{12,8},{9,1... | collective-permute-start | bytes 4718600 | tf_op jit(solution)/shard_map/ppermute | solution.py:461
  583.4 86.8 %all-to-all-start.11 = ((f32[128,2,2,8,256]{4,3,2,1,0:T(8,128)}), f32[128,2,2,8,256]{4,3,2,1,0:T(8,128)}, u32[]{:S(2)}, u32[]{:S(2)}) async-start(f32[128,2,2,8,256]{4,3,2,1,0:T(8,128)} %shard_map.117), calls=%async_computation.11 | async-start | bytes 8388608 | tf_op jit(solution)/shard_map/all_to_all | solution.py:606
  588.1 74.5 %collective-permute-start.3 = (f32[2,64,8,256]{3,2,1,0:T(8,128)S(1)}, f32[2,64,8,256]{3,2,1,0:T(8,128)S(1)}, u32[]{:S(2)}, u32[]{:S(2)}) collective-permute-start(f32[2,64,8,256]{3,2,1,0:T(8,128)S(1)} %copy-done.2), channel_id=1, source_target_pairs={{0,4},{4,0},{1,5},{5,1},{2,6},{6,2},{3,7},{7,3},{8,12},{12,8},{9,1... | collective-permute-start | bytes 3145736 | tf_op jit(solution)/shard_map/ppermute | solution.py:461
  743.3 56.7 %all-to-all-start.13 = ((f32[128,2,2,8,256]{4,3,2,1,0:T(8,128)}), f32[128,2,2,8,256]{4,3,2,1,0:T(8,128)}, u32[]{:S(2)}, u32[]{:S(2)}) async-start(f32[128,2,2,8,256]{4,3,2,1,0:T(8,128)} %bitcast.77), calls=%async_computation.13 | async-start | bytes 8388608 | tf_op jit(solution)/shard_map/all_to_all | solution.py:572
  800.0 58.1 %all-to-all-start.14 = ((f32[128,2,2,8,256]{4,3,2,1,0:T(8,128)}), f32[128,2,2,8,256]{4,3,2,1,0:T(8,128)}, u32[]{:S(2)}, u32[]{:S(2)}) async-start(f32[128,2,2,8,256]{4,3,2,1,0:T(8,128)} %bitcast.74), calls=%async_computation.14 | async-start | bytes 8388608 | tf_op jit(solution)/shard_map/all_to_all | solution.py:572
  896.7 71.1 %collective-permute-start.4 = (f32[3,64,8,256]{3,2,1,0:T(8,128)}, f32[3,64,8,256]{3,2,1,0:T(8,128)}, u32[]{:S(2)}, u32[]{:S(2)}) collective-permute-start(f32[3,64,8,256]{3,2,1,0:T(8,128)} %get-tuple-element.131), channel_id=1, source_target_pairs={{0,4},{4,0},{1,5},{5,1},{2,6},{6,2},{3,7},{7,3},{8,12},{12,8},{9,1... | collective-permute-start | bytes 4718600 | tf_op jit(solution)/shard_map/ppermute | solution.py:461
  905.5 62.3 %copy-start.6 = (f32[3,64,8,256]{3,2,1,0:T(8,128)S(1)}, f32[3,64,8,256]{3,2,1,0:T(8,128)}, u32[]{:S(2)}) copy-start(f32[3,64,8,256]{3,2,1,0:T(8,128)} %get-tuple-element.129) | copy-start | bytes 4718596
  972.1 16.4 %copy-start.7 = (f32[1,64,2,8,256]{4,3,2,1,0:T(8,128)S(1)}, f32[1,64,2,8,256]{4,3,2,1,0:T(8,128)}, u32[]{:S(2)}) copy-start(f32[1,64,2,8,256]{4,3,2,1,0:T(8,128)} %get-tuple-element.138) | copy-start | bytes 3145732
  972.1 98.7 %all-to-all-start.16 = ((f32[4,2,64,8,256]{4,3,2,1,0:T(8,128)}), f32[4,2,64,8,256]{4,3,2,1,0:T(8,128)}, u32[]{:S(2)}, u32[]{:S(2)}) async-start(f32[4,2,64,8,256]{4,3,2,1,0:T(8,128)} %broadcast_in_dim.20), calls=%async_computation.16 | async-start | bytes 8388608 | tf_op jit(solution)/shard_map/all_to_all | solution.py:649
  977.1 98.6 %collective-permute-start.5 = (f32[1,64,2,8,256]{4,3,2,1,0:T(8,128)}, f32[1,64,2,8,256]{4,3,2,1,0:T(8,128)}, u32[]{:S(2)}, u32[]{:S(2)}) collective-permute-start(f32[1,64,2,8,256]{4,3,2,1,0:T(8,128)} %get-tuple-element.136), channel_id=1, source_target_pairs={{0,0},{4,20},{8,4},{12,16},{16,8},{20,28},{24,12},{28,24},{1,1},{5... | collective-permute-start | bytes 3145736 | tf_op jit(solution)/shard_map/ppermute | solution.py:496
  986.6 89.1 %collective-permute-start.6 = (f32[1,64,2,8,256]{4,3,2,1,0:T(8,128)S(1)}, f32[1,64,2,8,256]{4,3,2,1,0:T(8,128)}, u32[]{:S(2)}, u32[]{:S(2)}) collective-permute-start(f32[1,64,2,8,256]{4,3,2,1,0:T(8,128)S(1)} %copy-done.8), channel_id=1, source_target_pairs={{0,4},{4,16},{8,8},{12,28},{16,12},{20,24},{24,0},{28,20},{1,5},{5... | collective-permute-start | bytes 3145736 | tf_op jit(solution)/shard_map/ppermute | solution.py:496
  988.5 87.2 %collective-permute-start.7 = (f32[1,64,2,8,256]{4,3,2,1,0:T(8,128)S(1)}, f32[1,64,2,8,256]{4,3,2,1,0:T(8,128)}, u32[]{:S(2)}, u32[]{:S(2)}) collective-permute-start(f32[1,64,2,8,256]{4,3,2,1,0:T(8,128)S(1)} %copy-done.7), channel_id=1, source_target_pairs={{0,8},{4,28},{8,12},{12,24},{16,0},{20,20},{24,4},{28,16},{1,9},{5... | collective-permute-start | bytes 3145736 | tf_op jit(solution)/shard_map/ppermute | solution.py:496
  990.4 101.9 %collective-permute-start.8 = (f32[1,64,2,8,256]{4,3,2,1,0:T(8,128)S(1)}, f32[1,64,2,8,256]{4,3,2,1,0:T(8,128)}, u32[]{:S(2)}, u32[]{:S(2)}) collective-permute-start(f32[1,64,2,8,256]{4,3,2,1,0:T(8,128)S(1)} %get-tuple-element.139), channel_id=1, source_target_pairs={{0,12},{4,24},{8,0},{12,20},{16,4},{20,16},{24,8},{28,28},{1,13},{... | collective-permute-start | bytes 3145736 | tf_op jit(solution)/shard_map/ppermute | solution.py:496
  (11 other events, 58.2 us)

commit v4 on v3

--- a/solution.py
+++ b/solution.py
@@ -114,12 +114,12 @@
     finish(spec, depth, rest, keep)
 
 
-def adjoint_kernel(first, scal, chi, inc, source, data, *refs):
+def adjoint_kernel(first, scal, chi, source, data, field, *refs):
     if first:
-        *fields, scat_out, spec, keep_in, keep, keep_resid = refs
+        *fields, total_out, spec, keep_in, keep, keep_resid = refs
     else:
-        field, spec, keep, keep_resid = refs
-    depth = inc.shape[1]
+        spec, keep, keep_resid = refs
+    depth = source.shape[1]
     width, rest = factors(depth)
     object_weight, data_weight = scal[0, 0], scal[0, 1]
     if first:
@@ -129,22 +129,19 @@
         values, resid = [], []
         for k0 in range(rest):
             z = k1 + width * k0
+            ur, ui = pair(field, z)
             if first:
-                sr, si = scattered[k0]
-                put(scat_out, z, (sr, si))
-            else:
-                sr, si = pair(field, z)
+                ur, ui = ur + scattered[k0][0], ui + scattered[k0][1]
+                put(total_out, z, (ur, ui))
             cr, ci = chi[0, z], chi[1, z]
-            er, ei = pair(inc, z)
             wr, wi = pair(source, z)
-            ur, ui = er + sr, ei + si
             rr = object_weight * (cr * ur - ci * ui - wr)
             ri = object_weight * (cr * ui + ci * ur - wi)
             vr = -(cr * rr + ci * ri)
             vi = ci * rr - cr * ri
             if z == 0:
-                vr = vr + data_weight * (data[0, 0] - sr)
-                vi = vi + data_weight * (data[0, 1] - si)
+                vr = vr + data_weight * (data[0, 0] - ur)
+                vi = vi + data_weight * (data[0, 1] - ui)
             values.append((vr, vi))
             resid.append((rr, ri))
         stage_one(values, k1, depth, -1, keep)
@@ -187,12 +184,12 @@
     sums[0, 0, 1] = plane
 
 
-def step_kernel(last, scal, source, descent, scattered, image, inc, source_out, *rest_refs):
+def step_kernel(last, scal, source, descent, field, image, source_out, *rest_refs):
     if last:
         (parts,) = rest_refs
     else:
-        scat_out, parts = rest_refs
-    sources, depth = inc.shape[:2]
+        field_out, parts = rest_refs
+    sources, depth = source.shape[:2]
     step = scal[0, 0]
 
     def body(z, _):
@@ -202,12 +199,11 @@
             wr, wi = source[s, z, 0] + step * dr, source[s, z, 1] + step * di
             source_out[s, z, 0] = wr
             source_out[s, z, 1] = wi
-            sr = scattered[s, z, 0] + step * image[s, z, 0]
-            si = scattered[s, z, 1] + step * image[s, z, 1]
+            ur = field[s, z, 0] + step * image[s, z, 0]
+            ui = field[s, z, 1] + step * image[s, z, 1]
             if not last:
-                scat_out[s, z, 0] = sr
-                scat_out[s, z, 1] = si
-            ur, ui = inc[s, z, 0] + sr, inc[s, z, 1] + si
+                field_out[s, z, 0] = ur
+                field_out[s, z, 1] = ui
             a, b, c = wr * ur + wi * ui, wi * ur - wr * ui, ur * ur + ui * ui
             nr, ni, power = (a, b, c) if s == 0 else (nr + a, ni + b, power + c)
         parts[0, z] = nr
@@ -586,7 +582,7 @@
         source[c], spec = slabs.call(start_kernel, c, ("chi", "field"), ("field", "spec"), 1, chi[c], inc[c])
         came[c] = lax.all_to_all(spec, GROUP, 0, 0, tiled=True)
     fields = exchange(call_planes(partial(plane_kernel, scale), tables, came, 8))
-    scattered = [None, None]
+    total = [None, None]
     for outer in range(OUTER):
         object_weight = 1.0 / object_total
         weights = jnp.stack([object_weight, data_weight]).reshape(1, 2)
@@ -596,13 +592,14 @@
             out = slabs.call(
                 partial(adjoint_kernel, first),
                 c,
-                ("scal", "chi", "field", "field", "data") + (piece_kinds if first else ("field",)),
+                ("scal", "chi", "field", "data", "field") + (piece_kinds if first else ()),
                 ("field", "twin") if first else ("twin",),
                 3 if first else 2,
-                weights, chi[c], inc[c], source[c], data[c], *((fields,) if first else (scattered[c],)),
+                weights, chi[c], source[c], data[c] + inc[c][:, 0],
+                *((inc[c], fields) if first else (total[c],)),
             )
             if first:
-                scattered[c] = out[0]
+                total[c] = out[0]
             came[c] = lax.all_to_all(out[-1], GROUP, 0, 0, tiled=True)
         part, kept = call_planes(partial(adjoint_plane_kernel, scale), tables, came, 12, keeps=True)
         fields = exchange(part)
@@ -627,14 +624,14 @@
             out = slabs.call(
                 partial(step_kernel, last),
                 c,
-                ("scal",) + ("every",) * 5,
+                ("scal",) + ("every",) * 4,
                 ("every",) * (1 if last else 2) + ("parts",),
                 0,
-                step.reshape(1, 1), source[c], descent[c], scattered[c], image[c], inc[c],
+                step.reshape(1, 1), source[c], descent[c], total[c], image[c],
             )
             source[c], parts[c] = out[0], out[-1]
             if not last:
-                scattered[c] = out[1]
+                total[c] = out[1]
         received = swap_halves(parts[1])
         if last:
             sent = payloads(source, shares, per_share, share)

time: 1100 us -> 1100 us (level)
  no operation moved by 1% of the time
where the time goes in v4:
time: 1100 us
  waiting for transfers between devices  612 us (56%)
  Pallas kernels  181 us (16%)
  blocking collectives  145 us (13%)
  starting transfers between devices  89.9 us (8%)
  other arithmetic  40.6 us (4%)
  local copies, waits for them, and re-layouts  18.8 us (2%)
    ppermute x5, waiting for transfers between devices, swap_halves(): return lax.ppermute(value, 'half', [(0, 1), (1, 0)])  283 us
    all_to_all x5, waiting for transfers between devices, exchange(): return lax.all_to_all(flat, GROUP, 0, 0, tiled=True).reshape(value.shape)  167 us
    all_to_all x2, blocking collectives, on_device(): came[c] = lax.all_to_all(out[-1], GROUP, 0, 0, tiled=True)  110 us
    pallas_call x18, Pallas kernels, call(): pl.pallas_call(kernel, grid=(self.ny // self.lanes, second), in_specs=[sp...  105 us
    all_to_all x1, waiting for transfers between devices, on_device(): contrast_new = lax.all_to_all(copies, 'src', 0, 0, tiled=True)  73.2 us
    pallas_call x5, Pallas kernels, plane_call(): pl.pallas_call(kernel, grid=(planes,), in_specs=[SMEM] + [whole(t) for t...  71.1 us
    all_to_all x2, waiting for transfers between devices, on_device(): came[c] = lax.all_to_all(out[-1], GROUP, 0, 0, tiled=True)  44.9 us
    all_to_all x3, blocking collectives, everyone(): return jnp.sum(lax.all_to_all(sent, ALL, 0, 0, tiled=True), axis=0)  35 us
  transfers between devices with their start and end apart: 21, of which 14 were waited for; matrix products, arithmetic and copies ran while one was open for 2% of the time, Pallas kernels for 8%

profile of v4, /device:TPU:0, one launch (start us, length us, event | category | flops | bytes accessed | tf_op | source)
XLA Modules:
  0.0 1097.0 jit_solution(406047749924778079)
XLA Ops:
  13.6 9.0 fusion.1
  40.4 42.7 %collective-permute-done.chi = f32[2,64,8,256]{3,2,1,0:T(8,128)S(1)} collective-permute-done((f32[2,64,8,256]{3,2,1,0:T(8,128)S(1)}, f32[2,64,8,256]{3,2,1,0:T(8,128)S(1)}, u32[]{:S(2)}, u32[]{:S(2)}) %collective-permute-start) | collective-permute-done | bytes 1048608 | tf_op jit(solution)/shard_map/ppermute | solution.py:457
  98.4 25.2 %all-to-all-done.3 = f32[128,2,8,256]{3,2,1,0:T(8,128)S(1)} async-done(((f32[128,2,8,256]{3,2,1,0:T(8,128)}), f32[128,2,8,256]{3,2,1,0:T(8,128)S(1)}, u32[]{:S(2)}, u32[]{:S(2)}) %all-to-all-start.3) | async-done | bytes 2097184 | tf_op jit(solution)/shard_map/all_to_all | solution.py:583
  128.6 14.0 %shard_map.106 = f32[16,8,2,2,8,256]{5,4,3,2,1,0:T(8,128)} custom-call(f32[8]{0:T(128)} %multiply_multiply_fusion.lz, f32[256,128]{1,0:T(8,128)} %jit_solution_.3.lx, f32[2,1,128]{2,1,0:T(1,128)} %constant.258.clone.ly, bf16[2,2,256,256]{3,2,1,0:T(8,128)(2,1)} %constant.259.clone.xf, bf16[2,2,256,256]{3,2,1,0:T(8,128)(2,1)} %constant.260.clone.xb, ...), custom_call_target="tpu_custom_call" | custom-call | flops 6442450944 | bytes 8388608 | tf_op jit(solution)/shard_map/pallas_call | solution.py:430
  154.2 46.4 %collective-permute-done.1 = f32[2,2,8,256]{3,2,1,0:T(8,128)S(1)} collective-permute-done((f32[2,2,8,256]{3,2,1,0:T(8,128)S(1)}, f32[2,2,8,256]{3,2,1,0:T(8,128)S(1)}, u32[]{:S(2)}, u32[]{:S(2)}) %collective-permute-start.1) | collective-permute-done | bytes 32800 | tf_op jit(solution)/shard_map/ppermute | solution.py:457
  222.8 44.9 %all-to-all-done.6 = f32[128,2,2,8,256]{4,3,2,1,0:T(8,128)} async-done(((f32[128,2,2,8,256]{4,3,2,1,0:T(8,128)}), f32[128,2,2,8,256]{4,3,2,1,0:T(8,128)}, u32[]{:S(2)}, u32[]{:S(2)}) %all-to-all-start.6) | async-done | bytes 4194336 | tf_op jit(solution)/shard_map/all_to_all | solution.py:603
  267.7 55.5 %all_to_all.96 = f32[128,2,2,8,256]{4,3,2,1,0:T(8,128)} all-to-all(f32[128,2,2,8,256]{4,3,2,1,0:T(8,128)} %get-tuple-element.98), channel_id=1, replica_groups=mesh['src'=4,'half'=2,'rest'=4] {'src','rest'}, dimensions={0} | all-to-all | bytes 8388608 | tf_op jit(solution)/shard_map/all_to_all | solution.py:603
  323.2 18.4 %shard_map.109 = (f32[16,8,2,2,8,256]{5,4,3,2,1,0:T(8,128)}, f32[8,2,2,256,128]{4,3,2,1,0:T(8,128)}) custom-call(f32[8]{0:T(128)} %multiply_multiply_fusion.lz, f32[256,128]{1,0:T(8,128)} %jit_solution_.3.lx, f32[2,1,128]{2,1,0:T(1,128)} %constant.258.clone.ly, bf16[2,2,256,256]{3,2,1,0:T(8,128)(2,1)} %constant.259.clone.xf, ...), custom_call_target="tpu_custom_call" | custom-call | flops 9663676416 | bytes 12582912 | tf_op jit(solution)/shard_map/pallas_call | solution.py:430
  346.1 10.1 shard_map.112
  356.3 42.0 %all-to-all-done.7 = f32[128,2,2,8,256]{4,3,2,1,0:T(8,128)} async-done(((f32[128,2,2,8,256]{4,3,2,1,0:T(8,128)}), f32[128,2,2,8,256]{4,3,2,1,0:T(8,128)}, u32[]{:S(2)}, u32[]{:S(2)}) %all-to-all-start.7) | async-done | bytes 4194336 | tf_op jit(solution)/shard_map/all_to_all | solution.py:568
  415.1 41.3 %all-to-all-done.8 = f32[128,2,2,8,256]{4,3,2,1,0:T(8,128)} async-done(((f32[128,2,2,8,256]{4,3,2,1,0:T(8,128)}), f32[128,2,2,8,256]{4,3,2,1,0:T(8,128)}, u32[]{:S(2)}, u32[]{:S(2)}) %all-to-all-start.8) | async-done | bytes 4194336 | tf_op jit(solution)/shard_map/all_to_all | solution.py:568
  470.4 12.1 %all_to_all.97 = f32[32,1,128]{2,1,0:T(1,128)S(1)} all-to-all(f32[32,1,128]{2,1,0:T(1,128)S(1)} %broadcast_in_dim.17), channel_id=1, replica_groups=mesh['src'=4,'half'=2,'rest'=4] {'src','half','rest'}, dimensions={0} | all-to-all | bytes 32768 | tf_op jit(solution)/shard_map/all_to_all | solution.py:453
  502.2 62.2 %collective-permute-done.2 = f32[3,64,8,256]{3,2,1,0:T(8,128)S(1)} collective-permute-done((f32[3,64,8,256]{3,2,1,0:T(8,128)}, f32[3,64,8,256]{3,2,1,0:T(8,128)S(1)}, u32[]{:S(2)}, u32[]{:S(2)}) %collective-permute-start.2) | collective-permute-done | bytes 1572896 | tf_op jit(solution)/shard_map/ppermute | solution.py:457
  589.6 73.9 %collective-permute-done.3.chi = f32[2,64,8,256]{3,2,1,0:T(8,128)S(1)} collective-permute-done((f32[2,64,8,256]{3,2,1,0:T(8,128)S(1)}, f32[2,64,8,256]{3,2,1,0:T(8,128)S(1)}, u32[]{:S(2)}, u32[]{:S(2)}) %collective-permute-start.3) | collective-permute-done | bytes 1048608 | tf_op jit(solution)/shard_map/ppermute | solution.py:457
  670.8 54.7 %all_to_all.99 = f32[128,2,2,8,256]{4,3,2,1,0:T(8,128)} all-to-all(f32[128,2,2,8,256]{4,3,2,1,0:T(8,128)} %shard_map.118), channel_id=1, replica_groups=mesh['src'=4,'half'=2,'rest'=4] {'src','rest'}, dimensions={0} | all-to-all | bytes 8388608 | tf_op jit(solution)/shard_map/all_to_all | solution.py:603
  725.5 18.4 %shard_map.119 = (f32[16,8,2,2,8,256]{5,4,3,2,1,0:T(8,128)}, f32[8,2,2,256,128]{4,3,2,1,0:T(8,128)}) custom-call(f32[8]{0:T(128)} %multiply_multiply_fusion.lz, f32[256,128]{1,0:T(8,128)} %jit_solution_.3.lx, f32[2,1,128]{2,1,0:T(1,128)} %constant.258.clone.ly, bf16[2,2,256,256]{3,2,1,0:T(8,128)(2,1)} %constant.259.clone.xf, ...), custom_call_target="tpu_custom_call" | custom-call | flops 9663676416 | bytes 12582912 | tf_op jit(solution)/shard_map/pallas_call | solution.py:430
  748.5 10.1 shard_map.122
  758.6 42.0 %all-to-all-done.13 = f32[128,2,2,8,256]{4,3,2,1,0:T(8,128)} async-done(((f32[128,2,2,8,256]{4,3,2,1,0:T(8,128)}), f32[128,2,2,8,256]{4,3,2,1,0:T(8,128)}, u32[]{:S(2)}, u32[]{:S(2)}) %all-to-all-start.13) | async-done | bytes 4194336 | tf_op jit(solution)/shard_map/all_to_all | solution.py:568
  817.4 41.3 %all-to-all-done.14 = f32[128,2,2,8,256]{4,3,2,1,0:T(8,128)} async-done(((f32[128,2,2,8,256]{4,3,2,1,0:T(8,128)}), f32[128,2,2,8,256]{4,3,2,1,0:T(8,128)}, u32[]{:S(2)}, u32[]{:S(2)}) %all-to-all-start.14) | async-done | bytes 4194336 | tf_op jit(solution)/shard_map/all_to_all | solution.py:568
  872.5 14.0 %all_to_all.100 = f32[32,1,128]{2,1,0:T(1,128)S(1)} all-to-all(f32[32,1,128]{2,1,0:T(1,128)S(1)} %broadcast_in_dim.19), channel_id=1, replica_groups=mesh['src'=4,'half'=2,'rest'=4] {'src','half','rest'}, dimensions={0} | all-to-all | bytes 32768 | tf_op jit(solution)/shard_map/all_to_all | solution.py:453
  909.7 58.2 %collective-permute-done.4 = f32[3,64,8,256]{3,2,1,0:T(8,128)} collective-permute-done((f32[3,64,8,256]{3,2,1,0:T(8,128)}, f32[3,64,8,256]{3,2,1,0:T(8,128)}, u32[]{:S(2)}, u32[]{:S(2)}) %collective-permute-start.4) | collective-permute-done | bytes 1572896 | tf_op jit(solution)/shard_map/ppermute | solution.py:457
  977.1 9.5 collective-permute-start.5
  997.7 73.2 %all-to-all-done.16 = f32[4,2,64,8,256]{4,3,2,1,0:T(8,128)} async-done(((f32[4,2,64,8,256]{4,3,2,1,0:T(8,128)}), f32[4,2,64,8,256]{4,3,2,1,0:T(8,128)}, u32[]{:S(2)}, u32[]{:S(2)}) %all-to-all-start.16) | async-done | bytes 4194336 | tf_op jit(solution)/shard_map/all_to_all | solution.py:646
  1075.7 16.7 %collective-permute-done.8.refs_3_ = f32[1,64,2,8,256]{4,3,2,1,0:T(8,128)} collective-permute-done((f32[1,64,2,8,256]{4,3,2,1,0:T(8,128)S(1)}, f32[1,64,2,8,256]{4,3,2,1,0:T(8,128)}, u32[]{:S(2)}, u32[]{:S(2)}) %collective-permute-start.8) | collective-permute-done | bytes 1048608 | tf_op jit(solution)/shard_map/ppermute | solution.py:492
  (146 shorter events, 251.2 us)
Async XLA Ops:
  3.0 10.0 all-to-all-start.1
  30.2 58.6 %all-to-all-start.2 = ((f32[128,2,8,256]{3,2,1,0:T(8,128)}), f32[128,2,8,256]{3,2,1,0:T(8,128)}, u32[]{:S(2)}, u32[]{:S(2)}) async-start(f32[128,2,8,256]{3,2,1,0:T(8,128)} %get-tuple-element.96), calls=%async_computation.2 | async-start | bytes 4194304 | tf_op jit(solution)/shard_map/all_to_all | solution.py:583
  34.8 48.3 %collective-permute-start = (f32[2,64,8,256]{3,2,1,0:T(8,128)S(1)}, f32[2,64,8,256]{3,2,1,0:T(8,128)S(1)}, u32[]{:S(2)}, u32[]{:S(2)}) collective-permute-start(f32[2,64,8,256]{3,2,1,0:T(8,128)S(1)} %copy-done), channel_id=1, source_target_pairs={{0,4},{4,0},{1,5},{5,1},{2,6},{6,2},{3,7},{7,3},{8,12},{12,8},{9,1... | collective-permute-start | bytes 3145736 | tf_op jit(solution)/shard_map/ppermute | solution.py:457
  88.7 39.1 %copy-start.16 = (f32[256]{0:T(256)S(1)}, f32[256]{0:T(256)}, u32[]{:S(2)}) copy-start(f32[256]{0:T(256)} %constant.257.clone) | copy-start | bytes 3076
  88.8 34.9 %all-to-all-start.3 = ((f32[128,2,8,256]{3,2,1,0:T(8,128)}), f32[128,2,8,256]{3,2,1,0:T(8,128)S(1)}, u32[]{:S(2)}, u32[]{:S(2)}) async-start(f32[128,2,8,256]{3,2,1,0:T(8,128)} %get-tuple-element.97), calls=%async_computation.3 | async-start | bytes 4194304 | tf_op jit(solution)/shard_map/all_to_all | solution.py:583
  124.3 18.3 %all-to-all-start = ((f32[32,1,128]{2,1,0:T(1,128)}), f32[32,1,128]{2,1,0:T(1,128)S(1)}, u32[]{:S(2)}, u32[]{:S(2)}) async-start(f32[32,1,128]{2,1,0:T(1,128)} %broadcast_in_dim.14), calls=%async_computation | async-start | bytes 32768 | tf_op jit(solution)/shard_map/all_to_all | solution.py:453
  142.6 58.6 %all-to-all-start.4 = ((f32[128,2,2,8,256]{4,3,2,1,0:T(8,128)}), f32[128,2,2,8,256]{4,3,2,1,0:T(8,128)}, u32[]{:S(2)}, u32[]{:S(2)}) async-start(f32[128,2,2,8,256]{4,3,2,1,0:T(8,128)} %bitcast.77), calls=%async_computation.4 | async-start | bytes 8388608 | tf_op jit(solution)/shard_map/all_to_all | solution.py:568
  147.7 52.9 %copy-start.3 = (f32[2,64,1,8,256]{4,3,2,0,1:T(8,128)S(1)}, f32[2,64,1,8,256]{4,3,2,0,1:T(8,128)}, u32[]{:S(2)}) copy-start(f32[2,64,1,8,256]{4,3,2,0,1:T(8,128)} %get-tuple-element.159) | copy-start | bytes 3145732
  151.1 49.5 %collective-permute-start.1 = (f32[2,2,8,256]{3,2,1,0:T(8,128)S(1)}, f32[2,2,8,256]{3,2,1,0:T(8,128)S(1)}, u32[]{:S(2)}, u32[]{:S(2)}) collective-permute-start(f32[2,2,8,256]{3,2,1,0:T(8,128)S(1)} %get-tuple-element.162), channel_id=1, source_target_pairs={{0,4},{4,0},{1,5},{5,1},{2,6},{6,2},{3,7},{7,3},{8,12},{12,8},{9,1... | collective-permute-start | bytes 98312 | tf_op jit(solution)/shard_map/ppermute | solution.py:457
  208.6 59.0 %all-to-all-start.6 = ((f32[128,2,2,8,256]{4,3,2,1,0:T(8,128)}), f32[128,2,2,8,256]{4,3,2,1,0:T(8,128)}, u32[]{:S(2)}, u32[]{:S(2)}) async-start(f32[128,2,2,8,256]{4,3,2,1,0:T(8,128)} %get-tuple-element.100), calls=%async_computation.6 | async-start | bytes 8388608 | tf_op jit(solution)/shard_map/all_to_all | solution.py:603
  341.6 56.7 %all-to-all-start.7 = ((f32[128,2,2,8,256]{4,3,2,1,0:T(8,128)}), f32[128,2,2,8,256]{4,3,2,1,0:T(8,128)}, u32[]{:S(2)}, u32[]{:S(2)}) async-start(f32[128,2,2,8,256]{4,3,2,1,0:T(8,128)} %bitcast.82), calls=%async_computation.7 | async-start | bytes 8388608 | tf_op jit(solution)/shard_map/all_to_all | solution.py:568
  398.3 58.2 %all-to-all-start.8 = ((f32[128,2,2,8,256]{4,3,2,1,0:T(8,128)}), f32[128,2,2,8,256]{4,3,2,1,0:T(8,128)}, u32[]{:S(2)}, u32[]{:S(2)}) async-start(f32[128,2,2,8,256]{4,3,2,1,0:T(8,128)} %bitcast.80), calls=%async_computation.8 | async-start | bytes 8388608 | tf_op jit(solution)/shard_map/all_to_all | solution.py:568
  493.4 71.0 %collective-permute-start.2 = (f32[3,64,8,256]{3,2,1,0:T(8,128)}, f32[3,64,8,256]{3,2,1,0:T(8,128)S(1)}, u32[]{:S(2)}, u32[]{:S(2)}) collective-permute-start(f32[3,64,8,256]{3,2,1,0:T(8,128)} %get-tuple-element.114), channel_id=1, source_target_pairs={{0,4},{4,0},{1,5},{5,1},{2,6},{6,2},{3,7},{7,3},{8,12},{12,8},{9,1... | collective-permute-start | bytes 4718600 | tf_op jit(solution)/shard_map/ppermute | solution.py:457
  584.4 86.4 %all-to-all-start.11 = ((f32[128,2,2,8,256]{4,3,2,1,0:T(8,128)}), f32[128,2,2,8,256]{4,3,2,1,0:T(8,128)}, u32[]{:S(2)}, u32[]{:S(2)}) async-start(f32[128,2,2,8,256]{4,3,2,1,0:T(8,128)} %shard_map.117), calls=%async_computation.11 | async-start | bytes 8388608 | tf_op jit(solution)/shard_map/all_to_all | solution.py:603
  589.0 74.5 %collective-permute-start.3 = (f32[2,64,8,256]{3,2,1,0:T(8,128)S(1)}, f32[2,64,8,256]{3,2,1,0:T(8,128)S(1)}, u32[]{:S(2)}, u32[]{:S(2)}) collective-permute-start(f32[2,64,8,256]{3,2,1,0:T(8,128)S(1)} %copy-done.2), channel_id=1, source_target_pairs={{0,4},{4,0},{1,5},{5,1},{2,6},{6,2},{3,7},{7,3},{8,12},{12,8},{9,1... | collective-permute-start | bytes 3145736 | tf_op jit(solution)/shard_map/ppermute | solution.py:457
  743.9 56.7 %all-to-all-start.13 = ((f32[128,2,2,8,256]{4,3,2,1,0:T(8,128)}), f32[128,2,2,8,256]{4,3,2,1,0:T(8,128)}, u32[]{:S(2)}, u32[]{:S(2)}) async-start(f32[128,2,2,8,256]{4,3,2,1,0:T(8,128)} %bitcast.81), calls=%async_computation.13 | async-start | bytes 8388608 | tf_op jit(solution)/shard_map/all_to_all | solution.py:568
  800.6 58.1 %all-to-all-start.14 = ((f32[128,2,2,8,256]{4,3,2,1,0:T(8,128)}), f32[128,2,2,8,256]{4,3,2,1,0:T(8,128)}, u32[]{:S(2)}, u32[]{:S(2)}) async-start(f32[128,2,2,8,256]{4,3,2,1,0:T(8,128)} %bitcast.78), calls=%async_computation.14 | async-start | bytes 8388608 | tf_op jit(solution)/shard_map/all_to_all | solution.py:568
  896.8 71.1 %collective-permute-start.4 = (f32[3,64,8,256]{3,2,1,0:T(8,128)}, f32[3,64,8,256]{3,2,1,0:T(8,128)}, u32[]{:S(2)}, u32[]{:S(2)}) collective-permute-start(f32[3,64,8,256]{3,2,1,0:T(8,128)} %get-tuple-element.131), channel_id=1, source_target_pairs={{0,4},{4,0},{1,5},{5,1},{2,6},{6,2},{3,7},{7,3},{8,12},{12,8},{9,1... | collective-permute-start | bytes 4718600 | tf_op jit(solution)/shard_map/ppermute | solution.py:457
  905.0 62.8 %copy-start.10 = (f32[3,64,8,256]{3,2,1,0:T(8,128)S(1)}, f32[3,64,8,256]{3,2,1,0:T(8,128)}, u32[]{:S(2)}) copy-start(f32[3,64,8,256]{3,2,1,0:T(8,128)} %get-tuple-element.129) | copy-start | bytes 4718596
  972.2 98.7 %all-to-all-start.16 = ((f32[4,2,64,8,256]{4,3,2,1,0:T(8,128)}), f32[4,2,64,8,256]{4,3,2,1,0:T(8,128)}, u32[]{:S(2)}, u32[]{:S(2)}) async-start(f32[4,2,64,8,256]{4,3,2,1,0:T(8,128)} %broadcast_in_dim.20), calls=%async_computation.16 | async-start | bytes 8388608 | tf_op jit(solution)/shard_map/all_to_all | solution.py:646
  977.1 98.6 %collective-permute-start.5 = (f32[1,64,2,8,256]{4,3,2,1,0:T(8,128)}, f32[1,64,2,8,256]{4,3,2,1,0:T(8,128)}, u32[]{:S(2)}, u32[]{:S(2)}) collective-permute-start(f32[1,64,2,8,256]{4,3,2,1,0:T(8,128)} %get-tuple-element.136), channel_id=1, source_target_pairs={{0,0},{4,20},{8,4},{12,16},{16,8},{20,28},{24,12},{28,24},{1,1},{5... | collective-permute-start | bytes 3145736 | tf_op jit(solution)/shard_map/ppermute | solution.py:492
  986.6 89.1 %collective-permute-start.6 = (f32[1,64,2,8,256]{4,3,2,1,0:T(8,128)S(1)}, f32[1,64,2,8,256]{4,3,2,1,0:T(8,128)}, u32[]{:S(2)}, u32[]{:S(2)}) collective-permute-start(f32[1,64,2,8,256]{4,3,2,1,0:T(8,128)S(1)} %copy-done.12), channel_id=1, source_target_pairs={{0,4},{4,16},{8,8},{12,28},{16,12},{20,24},{24,0},{28,20},{1,5},{5... | collective-permute-start | bytes 3145736 | tf_op jit(solution)/shard_map/ppermute | solution.py:492
  988.5 87.2 %collective-permute-start.7 = (f32[1,64,2,8,256]{4,3,2,1,0:T(8,128)S(1)}, f32[1,64,2,8,256]{4,3,2,1,0:T(8,128)}, u32[]{:S(2)}, u32[]{:S(2)}) collective-permute-start(f32[1,64,2,8,256]{4,3,2,1,0:T(8,128)S(1)} %copy-done.11), channel_id=1, source_target_pairs={{0,8},{4,28},{8,12},{12,24},{16,0},{20,20},{24,4},{28,16},{1,9},{5... | collective-permute-start | bytes 3145736 | tf_op jit(solution)/shard_map/ppermute | solution.py:492
  990.5 101.9 %collective-permute-start.8 = (f32[1,64,2,8,256]{4,3,2,1,0:T(8,128)S(1)}, f32[1,64,2,8,256]{4,3,2,1,0:T(8,128)}, u32[]{:S(2)}, u32[]{:S(2)}) collective-permute-start(f32[1,64,2,8,256]{4,3,2,1,0:T(8,128)S(1)} %get-tuple-element.139), channel_id=1, source_target_pairs={{0,12},{4,24},{8,0},{12,20},{16,4},{20,16},{24,8},{28,28},{1,13},{... | collective-permute-start | bytes 3145736 | tf_op jit(solution)/shard_map/ppermute | solution.py:492
  (14 other events, 82.8 us)

commit v5 on v4

--- a/solution.py
+++ b/solution.py
@@ -272,76 +272,100 @@
     )
 
 
-def lateral(own, other, xf, yf):
-    hx, ny = own[0].shape
+def lateral(items, xf, yf):
+    hx, ny = items[0][0][0].shape
     hy = ny // 2
-    across = [
-        left_mul(xf, 0, jnp.concatenate([own[0] + other[0], own[1] + other[1]], axis=0)),
-        left_mul(xf, 1, jnp.concatenate([own[0] - other[0], own[1] - other[1]], axis=0)),
+    joined = lambda pick: jnp.concatenate(
+        [jnp.concatenate([pick(own[c], other[c]) for c in (0, 1)], axis=0) for own, other in items], axis=1
+    )
+    across = [left_mul(xf, 0, joined(lambda a, b: a + b)), left_mul(xf, 1, joined(lambda a, b: a - b))]
+    spectra = [[], []]
+    for odd in (0, 1):
+        folded = []
+        for i in range(len(items)):
+            low, high = i * ny, i * ny + hy
+            parts = []
+            for c in (0, 1):
+                rows = slice(c * hx, (c + 1) * hx)
+                left = jnp.concatenate([across[p][rows, low : low + hy] for p in (0, 1)], axis=0)
+                right = jnp.concatenate([across[p][rows, high : high + hy] for p in (0, 1)], axis=0)
+                parts.append(left - right if odd else left + right)
+            folded.append(jnp.concatenate(parts, axis=1))
+        freq = right_mul(jnp.concatenate(folded, axis=0), yf, odd)
+        for i in range(len(items)):
+            piece = freq[i * 2 * hx : (i + 1) * 2 * hx]
+            spectra[odd].append((piece[:, :hy], piece[:, hy:]))
+    return spectra
+
+
+def lateral_back(spectra, xb, yb, out):
+    senders, count, _, _, rows, ny = out.shape
+    hx, hy = senders * rows, ny // 2
+    back = [
+        right_mul(jnp.concatenate([jnp.concatenate(v, axis=1) for v in spectra[odd]], axis=0), yb, odd)
+        for odd in (0, 1)
     ]
-    real = jnp.concatenate([across[0][:hx], across[1][:hx]], axis=0)
-    imag = jnp.concatenate([across[0][hx:], across[1][hx:]], axis=0)
+    plus, minus = back[0] + back[1], back[0] - back[1]
+
+    def joined(p):
+        items = []
+        for i in range(count):
+            rows = slice((2 * i + p) * hx, (2 * i + p + 1) * hx)
+            real = jnp.concatenate([plus[rows, :hy], minus[rows, :hy]], axis=1)
+            imag = jnp.concatenate([plus[rows, hy:], minus[rows, hy:]], axis=1)
+            items.append(jnp.concatenate([real, imag], axis=0))
+        return jnp.concatenate(items, axis=1)
+
+    even, odd = left_mul(xb, 0, joined(0)), left_mul(xb, 1, joined(1))
+    plus, minus = even + odd, even - odd
+    for i in range(count):
+        for c in (0, 1):
+            place = (slice(c * hx, (c + 1) * hx), slice(i * ny, (i + 1) * ny))
+            out[:, i, c, 0] = plus[place].reshape(senders, rows, ny)
+            out[:, i, c, 1] = minus[place].reshape(senders, rows, ny)
+
+
+def filtered(values, sign, scale, lz, lx, ly, odd):
+    wave_sq = WAVENUMBER * WAVENUMBER
+    out = []
+    for i, (fr, fi) in enumerate(values):
+        eigen = (lx[...] + lz[pl.program_id(0) * len(values) + i]) + ly[odd]
+        real_den = eigen - wave_sq
+        imag_den = wave_sq * DAMPING
+        factor = (wave_sq * scale) / (real_den * real_den + imag_den * imag_den)
+        gr, gi = factor * real_den, factor * (imag_den * sign)
+        out.append((fr * gr - fi * gi, fr * gi + fi * gr))
+    return out
+
+
+def loaded(own, other, *at):
+    plane = lambda ref, i: [ref[(slice(None), i, *at, c)].reshape(-1, ref.shape[-1]) for c in (0, 1)]
+    return [(plane(own, i), plane(other, i)) for i in range(own.shape[1])]
+
+
+def plane_kernel(scale, lz, lx, ly, xf, xb, yf, yb, own, other, out):
+    spectra = lateral(loaded(own, other), xf, yf)
+    lateral_back([filtered(spectra[odd], 1.0, scale, lz, lx, ly, odd) for odd in (0, 1)], xb, yb, out)
+
+
+def adjoint_plane_kernel(scale, lz, lx, ly, xf, xb, yf, yb, own, other, out, keep):
+    inner = lateral(loaded(own, other, 0), xf, yf)
+    resid = lateral(loaded(own, other, 1), xf, yf)
     spectra = []
     for odd in (0, 1):
-        flip = -1.0 if odd else 1.0
-        folded = jnp.concatenate(
-            [real[:, :hy] + flip * real[:, hy:], imag[:, :hy] + flip * imag[:, hy:]], axis=1
-        )
-        freq = right_mul(folded, yf, odd)
-        spectra.append((freq[:, :hy], freq[:, hy:]))
-    return spectra
-
-
-def lateral_back(spectra, xb, yb, out):
-    back = [right_mul(jnp.concatenate(spectra[odd], axis=1), yb, odd) for odd in (0, 1)]
-    senders, _, _, _, rows, ny = out.shape
-    hx, hy = senders * rows, ny // 2
-    plus, minus = back[0] + back[1], back[0] - back[1]
-    real = jnp.concatenate([plus[:, :hy], minus[:, :hy]], axis=1)
-    imag = jnp.concatenate([plus[:, hy:], minus[:, hy:]], axis=1)
-    even = left_mul(xb, 0, jnp.concatenate([real[:hx], imag[:hx]], axis=0))
-    odd = left_mul(xb, 1, jnp.concatenate([real[hx:], imag[hx:]], axis=0))
-    plus, minus = even + odd, even - odd
-    for c in (0, 1):
-        out[:, 0, c, 0] = plus[c * hx : (c + 1) * hx].reshape(senders, rows, ny)
-        out[:, 0, c, 1] = minus[c * hx : (c + 1) * hx].reshape(senders, rows, ny)
-
-
-def filtered(value, sign, scale, lz, lx, ly, odd):
-    wave_sq = WAVENUMBER * WAVENUMBER
-    eigen = (lx[...] + lz[pl.program_id(0)]) + ly[odd]
-    real_den = eigen - wave_sq
-    imag_den = wave_sq * DAMPING
-    factor = (wave_sq * scale) / (real_den * real_den + imag_den * imag_den)
-    gr, gi = factor * real_den, factor * (imag_den * sign)
-    fr, fi = value
-    return fr * gr - fi * gi, fr * gi + fi * gr
-
-
-def loaded(ref, *at):
-    return [ref[(slice(None), 0, *at, c)].reshape(-1, ref.shape[-1]) for c in (0, 1)]
-
-
-def plane_kernel(scale, lz, lx, ly, xf, xb, yf, yb, own, other, out):
-    spectra = lateral(loaded(own), loaded(other), xf, yf)
-    lateral_back([filtered(spectra[odd], 1.0, scale, lz, lx, ly, odd) for odd in (0, 1)], xb, yb, out)
-
-
-def adjoint_plane_kernel(scale, lz, lx, ly, xf, xb, yf, yb, own, other, out, keep):
-    inner = lateral(loaded(own, 0), loaded(other, 0), xf, yf)
-    resid = lateral(loaded(own, 1), loaded(other, 1), xf, yf)
-    spectra = []
-    for odd in (0, 1):
-        re, im = filtered(inner[odd], -1.0, scale, lz, lx, ly, odd)
-        re, im = re + scale * resid[odd][0], im + scale * resid[odd][1]
-        keep[0, odd, 0], keep[0, odd, 1] = re, im
-        spectra.append((re, im))
+        values = []
+        for i, (re, im) in enumerate(filtered(inner[odd], -1.0, scale, lz, lx, ly, odd)):
+            re, im = re + scale * resid[odd][i][0], im + scale * resid[odd][i][1]
+            keep[i, odd, 0], keep[i, odd, 1] = re, im
+            values.append((re, im))
+        spectra.append(values)
     lateral_back(spectra, xb, yb, out)
 
 
 def image_plane_kernel(lz, lx, ly, xb, yb, kept, out):
     spectra = [
-        filtered((kept[0, odd, 0], kept[0, odd, 1]), 1.0, 1.0, lz, lx, ly, odd) for odd in (0, 1)
+        filtered([(kept[i, odd, 0], kept[i, odd, 1]) for i in range(kept.shape[0])], 1.0, 1.0, lz, lx, ly, odd)
+        for odd in (0, 1)
     ]
     lateral_back(spectra, xb, yb, out)
 
@@ -404,6 +428,7 @@
 
 def plane_call(kernel, senders, lz, tables, ins, work, rows, ny, kept_in=None, keeps=False):
     planes = lz.shape[0]
+    group = 2 if planes % 2 == 0 else 1
     dense = rows % 8 != 0
     lead, deep = (1, senders * rows) if dense else (senders, rows)
 
@@ -418,10 +443,10 @@
     nx = 2 * senders * rows
     whole = lambda t: pl.BlockSpec(t.shape, lambda i, n=t.ndim: (0,) * n)
     plane = lambda shape: pl.BlockSpec(
-        (shape[0], 1) + tuple(shape[2:]), lambda i, n=len(shape): (0, i) + (0,) * (n - 2)
+        (shape[0], group) + tuple(shape[2:]), lambda i, n=len(shape): (0, i) + (0,) * (n - 2)
     )
     kept = (planes, 2, 2, nx, ny // 2)
-    kept_spec = pl.BlockSpec((1,) + kept[1:], lambda i: (i, 0, 0, 0, 0))
+    kept_spec = pl.BlockSpec((group,) + kept[1:], lambda i: (i, 0, 0, 0, 0))
     out_shape = (lead, planes, 2, 2, deep, ny)
     shapes, specs = [jax.ShapeDtypeStruct(out_shape, F32)], [plane(out_shape)]
     if keeps:
@@ -429,7 +454,7 @@
         specs.append(kept_spec)
     result = pl.pallas_call(
         kernel,
-        grid=(planes,),
+        grid=(planes // group,),
         in_specs=[SMEM] + [whole(t) for t in tables] + [plane(v.shape) for v in ins]
         + ([kept_spec] if kept_in is not None else []),
         out_specs=specs,

time: 1100 us -> 1100 us (level)
  transfers between devices with their start and end apart: 21 -> 21, of which waited for: 14 -> 14; matrix products, arithmetic and copies ran while one was open for 2% -> 2% of each run, Pallas kernels for 8% -> 7%
where the time goes in v5:
time: 1100 us; the launch traced here: 1090 us
  waiting for transfers between devices  616 us (56%)
  Pallas kernels  171 us (16%)
  blocking collectives  145 us (13%)
  starting transfers between devices  90 us (8%)
  other arithmetic  40.6 us (4%)
  local copies, waits for them, and re-layouts  18.8 us (2%)
    ppermute x5, waiting for transfers between devices, swap_halves(): return lax.ppermute(value, 'half', [(0, 1), (1, 0)])  283 us
    all_to_all x5, waiting for transfers between devices, exchange(): return lax.all_to_all(flat, GROUP, 0, 0, tiled=True).reshape(value.shape)  171 us
    all_to_all x2, blocking collectives, on_device(): came[c] = lax.all_to_all(out[-1], GROUP, 0, 0, tiled=True)  110 us
    pallas_call x18, Pallas kernels, call(): pl.pallas_call(kernel, grid=(self.ny // self.lanes, second), in_specs=[sp...  105 us
    all_to_all x1, waiting for transfers between devices, on_device(): contrast_new = lax.all_to_all(copies, 'src', 0, 0, tiled=True)  73.2 us
    pallas_call x5, Pallas kernels, plane_call(): pl.pallas_call(kernel, grid=(planes // group,), in_specs=[SMEM] + [whole(...  60.9 us
    all_to_all x2, waiting for transfers between devices, on_device(): came[c] = lax.all_to_all(out[-1], GROUP, 0, 0, tiled=True)  44.9 us
    all_to_all x3, blocking collectives, everyone(): return jnp.sum(lax.all_to_all(sent, ALL, 0, 0, tiled=True), axis=0)  35.2 us
  transfers between devices with their start and end apart: 21, of which 14 were waited for; matrix products, arithmetic and copies ran while one was open for 2% of the time, Pallas kernels for 7%

profile of v5, /device:TPU:0, one launch (start us, length us, event | category | flops | bytes accessed | tf_op | source)
XLA Modules:
  0.0 1091.2 jit_solution(15032199364756869763)
XLA Ops:
  13.6 9.0 fusion.1
  40.4 42.7 %collective-permute-done.chi = f32[2,64,8,256]{3,2,1,0:T(8,128)S(1)} collective-permute-done((f32[2,64,8,256]{3,2,1,0:T(8,128)S(1)}, f32[2,64,8,256]{3,2,1,0:T(8,128)S(1)}, u32[]{:S(2)}, u32[]{:S(2)}) %collective-permute-start) | collective-permute-done | bytes 1048608 | tf_op jit(solution)/shard_map/ppermute | solution.py:482
  98.4 25.2 %all-to-all-done.3 = f32[128,2,8,256]{3,2,1,0:T(8,128)S(1)} async-done(((f32[128,2,8,256]{3,2,1,0:T(8,128)}), f32[128,2,8,256]{3,2,1,0:T(8,128)S(1)}, u32[]{:S(2)}, u32[]{:S(2)}) %all-to-all-start.3) | async-done | bytes 2097184 | tf_op jit(solution)/shard_map/all_to_all | solution.py:608
  128.6 11.8 %shard_map.106 = f32[16,8,2,2,8,256]{5,4,3,2,1,0:T(8,128)} custom-call(f32[8]{0:T(128)} %multiply_multiply_fusion.lz, f32[256,128]{1,0:T(8,128)} %jit_solution_.3.lx, f32[2,1,128]{2,1,0:T(1,128)} %constant.258.clone.ly, bf16[2,2,256,256]{3,2,1,0:T(8,128)(2,1)} %constant.259.clone.xf, bf16[2,2,256,256]{3,2,1,0:T(8,128)(2,1)} %constant.260.clone.xb, ...), custom_call_target="tpu_custom_call" | custom-call | flops 6442450944 | bytes 8388608 | tf_op jit(solution)/shard_map/pallas_call | solution.py:455
  152.0 46.5 %collective-permute-done.1 = f32[2,2,8,256]{3,2,1,0:T(8,128)S(1)} collective-permute-done((f32[2,2,8,256]{3,2,1,0:T(8,128)S(1)}, f32[2,2,8,256]{3,2,1,0:T(8,128)S(1)}, u32[]{:S(2)}, u32[]{:S(2)}) %collective-permute-start.1) | collective-permute-done | bytes 32800 | tf_op jit(solution)/shard_map/ppermute | solution.py:482
  220.6 44.9 %all-to-all-done.6 = f32[128,2,2,8,256]{4,3,2,1,0:T(8,128)} async-done(((f32[128,2,2,8,256]{4,3,2,1,0:T(8,128)}), f32[128,2,2,8,256]{4,3,2,1,0:T(8,128)}, u32[]{:S(2)}, u32[]{:S(2)}) %all-to-all-start.6) | async-done | bytes 4194336 | tf_op jit(solution)/shard_map/all_to_all | solution.py:628
  265.5 55.5 %all_to_all.96 = f32[128,2,2,8,256]{4,3,2,1,0:T(8,128)} all-to-all(f32[128,2,2,8,256]{4,3,2,1,0:T(8,128)} %get-tuple-element.98), channel_id=1, replica_groups=mesh['src'=4,'half'=2,'rest'=4] {'src','rest'}, dimensions={0} | all-to-all | bytes 8388608 | tf_op jit(solution)/shard_map/all_to_all | solution.py:628
  321.0 16.4 %shard_map.109 = (f32[16,8,2,2,8,256]{5,4,3,2,1,0:T(8,128)}, f32[8,2,2,256,128]{4,3,2,1,0:T(8,128)}) custom-call(f32[8]{0:T(128)} %multiply_multiply_fusion.lz, f32[256,128]{1,0:T(8,128)} %jit_solution_.3.lx, f32[2,1,128]{2,1,0:T(1,128)} %constant.258.clone.ly, bf16[2,2,256,256]{3,2,1,0:T(8,128)(2,1)} %constant.259.clone.xf, ...), custom_call_target="tpu_custom_call" | custom-call | flops 9663676416 | bytes 12582912 | tf_op jit(solution)/shard_map/pallas_call | solution.py:455
  350.1 44.0 %all-to-all-done.7 = f32[128,2,2,8,256]{4,3,2,1,0:T(8,128)} async-done(((f32[128,2,2,8,256]{4,3,2,1,0:T(8,128)}), f32[128,2,2,8,256]{4,3,2,1,0:T(8,128)}, u32[]{:S(2)}, u32[]{:S(2)}) %all-to-all-start.7) | async-done | bytes 4194336 | tf_op jit(solution)/shard_map/all_to_all | solution.py:593
  411.0 41.2 %all-to-all-done.8 = f32[128,2,2,8,256]{4,3,2,1,0:T(8,128)} async-done(((f32[128,2,2,8,256]{4,3,2,1,0:T(8,128)}), f32[128,2,2,8,256]{4,3,2,1,0:T(8,128)}, u32[]{:S(2)}, u32[]{:S(2)}) %all-to-all-start.8) | async-done | bytes 4194336 | tf_op jit(solution)/shard_map/all_to_all | solution.py:593
  466.1 12.3 %all_to_all.97 = f32[32,1,128]{2,1,0:T(1,128)S(1)} all-to-all(f32[32,1,128]{2,1,0:T(1,128)S(1)} %broadcast_in_dim.17), channel_id=1, replica_groups=mesh['src'=4,'half'=2,'rest'=4] {'src','half','rest'}, dimensions={0} | all-to-all | bytes 32768 | tf_op jit(solution)/shard_map/all_to_all | solution.py:478
  481.0 8.3 shard_map.116
  498.1 62.2 %collective-permute-done.2 = f32[3,64,8,256]{3,2,1,0:T(8,128)S(1)} collective-permute-done((f32[3,64,8,256]{3,2,1,0:T(8,128)}, f32[3,64,8,256]{3,2,1,0:T(8,128)S(1)}, u32[]{:S(2)}, u32[]{:S(2)}) %collective-permute-start.2) | collective-permute-done | bytes 1572896 | tf_op jit(solution)/shard_map/ppermute | solution.py:482
  564.5 8.9 all_to_all.98
  585.5 73.9 %collective-permute-done.3.chi = f32[2,64,8,256]{3,2,1,0:T(8,128)S(1)} collective-permute-done((f32[2,64,8,256]{3,2,1,0:T(8,128)S(1)}, f32[2,64,8,256]{3,2,1,0:T(8,128)S(1)}, u32[]{:S(2)}, u32[]{:S(2)}) %collective-permute-start.3) | collective-permute-done | bytes 1048608 | tf_op jit(solution)/shard_map/ppermute | solution.py:482
  666.7 54.7 %all_to_all.99 = f32[128,2,2,8,256]{4,3,2,1,0:T(8,128)} all-to-all(f32[128,2,2,8,256]{4,3,2,1,0:T(8,128)} %shard_map.118), channel_id=1, replica_groups=mesh['src'=4,'half'=2,'rest'=4] {'src','rest'}, dimensions={0} | all-to-all | bytes 8388608 | tf_op jit(solution)/shard_map/all_to_all | solution.py:628
  721.4 16.4 %shard_map.119 = (f32[16,8,2,2,8,256]{5,4,3,2,1,0:T(8,128)}, f32[8,2,2,256,128]{4,3,2,1,0:T(8,128)}) custom-call(f32[8]{0:T(128)} %multiply_multiply_fusion.lz, f32[256,128]{1,0:T(8,128)} %jit_solution_.3.lx, f32[2,1,128]{2,1,0:T(1,128)} %constant.258.clone.ly, bf16[2,2,256,256]{3,2,1,0:T(8,128)(2,1)} %constant.259.clone.xf, ...), custom_call_target="tpu_custom_call" | custom-call | flops 9663676416 | bytes 12582912 | tf_op jit(solution)/shard_map/pallas_call | solution.py:455
  750.7 44.0 %all-to-all-done.13 = f32[128,2,2,8,256]{4,3,2,1,0:T(8,128)} async-done(((f32[128,2,2,8,256]{4,3,2,1,0:T(8,128)}), f32[128,2,2,8,256]{4,3,2,1,0:T(8,128)}, u32[]{:S(2)}, u32[]{:S(2)}) %all-to-all-start.13) | async-done | bytes 4194336 | tf_op jit(solution)/shard_map/all_to_all | solution.py:593
  811.6 41.3 %all-to-all-done.14 = f32[128,2,2,8,256]{4,3,2,1,0:T(8,128)} async-done(((f32[128,2,2,8,256]{4,3,2,1,0:T(8,128)}), f32[128,2,2,8,256]{4,3,2,1,0:T(8,128)}, u32[]{:S(2)}, u32[]{:S(2)}) %all-to-all-start.14) | async-done | bytes 4194336 | tf_op jit(solution)/shard_map/all_to_all | solution.py:593
  866.7 14.1 %all_to_all.100 = f32[32,1,128]{2,1,0:T(1,128)S(1)} all-to-all(f32[32,1,128]{2,1,0:T(1,128)S(1)} %broadcast_in_dim.19), channel_id=1, replica_groups=mesh['src'=4,'half'=2,'rest'=4] {'src','half','rest'}, dimensions={0} | all-to-all | bytes 32768 | tf_op jit(solution)/shard_map/all_to_all | solution.py:478
  903.9 58.2 %collective-permute-done.4 = f32[3,64,8,256]{3,2,1,0:T(8,128)} collective-permute-done((f32[3,64,8,256]{3,2,1,0:T(8,128)}, f32[3,64,8,256]{3,2,1,0:T(8,128)}, u32[]{:S(2)}, u32[]{:S(2)}) %collective-permute-start.4) | collective-permute-done | bytes 1572896 | tf_op jit(solution)/shard_map/ppermute | solution.py:482
  971.3 9.5 collective-permute-start.5
  991.9 73.2 %all-to-all-done.16 = f32[4,2,64,8,256]{4,3,2,1,0:T(8,128)} async-done(((f32[4,2,64,8,256]{4,3,2,1,0:T(8,128)}), f32[4,2,64,8,256]{4,3,2,1,0:T(8,128)}, u32[]{:S(2)}, u32[]{:S(2)}) %all-to-all-start.16) | async-done | bytes 4194336 | tf_op jit(solution)/shard_map/all_to_all | solution.py:671
  1069.9 16.7 %collective-permute-done.8.refs_3_ = f32[1,64,2,8,256]{4,3,2,1,0:T(8,128)} collective-permute-done((f32[1,64,2,8,256]{4,3,2,1,0:T(8,128)S(1)}, f32[1,64,2,8,256]{4,3,2,1,0:T(8,128)}, u32[]{:S(2)}, u32[]{:S(2)}) %collective-permute-start.8) | collective-permute-done | bytes 1048608 | tf_op jit(solution)/shard_map/ppermute | solution.py:517
  (146 shorter events, 250.3 us)
Async XLA Ops:
  3.0 10.0 all-to-all-start.1
  30.2 58.6 %all-to-all-start.2 = ((f32[128,2,8,256]{3,2,1,0:T(8,128)}), f32[128,2,8,256]{3,2,1,0:T(8,128)}, u32[]{:S(2)}, u32[]{:S(2)}) async-start(f32[128,2,8,256]{3,2,1,0:T(8,128)} %get-tuple-element.96), calls=%async_computation.2 | async-start | bytes 4194304 | tf_op jit(solution)/shard_map/all_to_all | solution.py:608
  34.8 48.3 %collective-permute-start = (f32[2,64,8,256]{3,2,1,0:T(8,128)S(1)}, f32[2,64,8,256]{3,2,1,0:T(8,128)S(1)}, u32[]{:S(2)}, u32[]{:S(2)}) collective-permute-start(f32[2,64,8,256]{3,2,1,0:T(8,128)S(1)} %copy-done), channel_id=1, source_target_pairs={{0,4},{4,0},{1,5},{5,1},{2,6},{6,2},{3,7},{7,3},{8,12},{12,8},{9,1... | collective-permute-start | bytes 3145736 | tf_op jit(solution)/shard_map/ppermute | solution.py:482
  88.7 39.1 %copy-start.16 = (f32[256]{0:T(256)S(1)}, f32[256]{0:T(256)}, u32[]{:S(2)}) copy-start(f32[256]{0:T(256)} %constant.257.clone) | copy-start | bytes 3076
  88.8 34.9 %all-to-all-start.3 = ((f32[128,2,8,256]{3,2,1,0:T(8,128)}), f32[128,2,8,256]{3,2,1,0:T(8,128)S(1)}, u32[]{:S(2)}, u32[]{:S(2)}) async-start(f32[128,2,8,256]{3,2,1,0:T(8,128)} %get-tuple-element.97), calls=%async_computation.3 | async-start | bytes 4194304 | tf_op jit(solution)/shard_map/all_to_all | solution.py:608
  124.3 16.1 %all-to-all-start = ((f32[32,1,128]{2,1,0:T(1,128)}), f32[32,1,128]{2,1,0:T(1,128)S(1)}, u32[]{:S(2)}, u32[]{:S(2)}) async-start(f32[32,1,128]{2,1,0:T(1,128)} %broadcast_in_dim.14), calls=%async_computation | async-start | bytes 32768 | tf_op jit(solution)/shard_map/all_to_all | solution.py:478
  140.5 58.7 %all-to-all-start.4 = ((f32[128,2,2,8,256]{4,3,2,1,0:T(8,128)}), f32[128,2,2,8,256]{4,3,2,1,0:T(8,128)}, u32[]{:S(2)}, u32[]{:S(2)}) async-start(f32[128,2,2,8,256]{4,3,2,1,0:T(8,128)} %bitcast.77), calls=%async_computation.4 | async-start | bytes 8388608 | tf_op jit(solution)/shard_map/all_to_all | solution.py:593
  145.6 52.9 %copy-start.3 = (f32[2,64,1,8,256]{4,3,2,0,1:T(8,128)S(1)}, f32[2,64,1,8,256]{4,3,2,0,1:T(8,128)}, u32[]{:S(2)}) copy-start(f32[2,64,1,8,256]{4,3,2,0,1:T(8,128)} %get-tuple-element.159) | copy-start | bytes 3145732
  149.0 49.5 %collective-permute-start.1 = (f32[2,2,8,256]{3,2,1,0:T(8,128)S(1)}, f32[2,2,8,256]{3,2,1,0:T(8,128)S(1)}, u32[]{:S(2)}, u32[]{:S(2)}) collective-permute-start(f32[2,2,8,256]{3,2,1,0:T(8,128)S(1)} %get-tuple-element.162), channel_id=1, source_target_pairs={{0,4},{4,0},{1,5},{5,1},{2,6},{6,2},{3,7},{7,3},{8,12},{12,8},{9,1... | collective-permute-start | bytes 98312 | tf_op jit(solution)/shard_map/ppermute | solution.py:482
  206.5 59.0 %all-to-all-start.6 = ((f32[128,2,2,8,256]{4,3,2,1,0:T(8,128)}), f32[128,2,2,8,256]{4,3,2,1,0:T(8,128)}, u32[]{:S(2)}, u32[]{:S(2)}) async-start(f32[128,2,2,8,256]{4,3,2,1,0:T(8,128)} %get-tuple-element.100), calls=%async_computation.6 | async-start | bytes 8388608 | tf_op jit(solution)/shard_map/all_to_all | solution.py:628
  337.4 56.7 %all-to-all-start.7 = ((f32[128,2,2,8,256]{4,3,2,1,0:T(8,128)}), f32[128,2,2,8,256]{4,3,2,1,0:T(8,128)}, u32[]{:S(2)}, u32[]{:S(2)}) async-start(f32[128,2,2,8,256]{4,3,2,1,0:T(8,128)} %bitcast.82), calls=%async_computation.7 | async-start | bytes 8388608 | tf_op jit(solution)/shard_map/all_to_all | solution.py:593
  394.1 58.1 %all-to-all-start.8 = ((f32[128,2,2,8,256]{4,3,2,1,0:T(8,128)}), f32[128,2,2,8,256]{4,3,2,1,0:T(8,128)}, u32[]{:S(2)}, u32[]{:S(2)}) async-start(f32[128,2,2,8,256]{4,3,2,1,0:T(8,128)} %bitcast.80), calls=%async_computation.8 | async-start | bytes 8388608 | tf_op jit(solution)/shard_map/all_to_all | solution.py:593
  489.3 71.0 %collective-permute-start.2 = (f32[3,64,8,256]{3,2,1,0:T(8,128)}, f32[3,64,8,256]{3,2,1,0:T(8,128)S(1)}, u32[]{:S(2)}, u32[]{:S(2)}) collective-permute-start(f32[3,64,8,256]{3,2,1,0:T(8,128)} %get-tuple-element.114), channel_id=1, source_target_pairs={{0,4},{4,0},{1,5},{5,1},{2,6},{6,2},{3,7},{7,3},{8,12},{12,8},{9,1... | collective-permute-start | bytes 4718600 | tf_op jit(solution)/shard_map/ppermute | solution.py:482
  580.3 86.4 %all-to-all-start.11 = ((f32[128,2,2,8,256]{4,3,2,1,0:T(8,128)}), f32[128,2,2,8,256]{4,3,2,1,0:T(8,128)}, u32[]{:S(2)}, u32[]{:S(2)}) async-start(f32[128,2,2,8,256]{4,3,2,1,0:T(8,128)} %shard_map.117), calls=%async_computation.11 | async-start | bytes 8388608 | tf_op jit(solution)/shard_map/all_to_all | solution.py:628
  585.0 74.5 %collective-permute-start.3 = (f32[2,64,8,256]{3,2,1,0:T(8,128)S(1)}, f32[2,64,8,256]{3,2,1,0:T(8,128)S(1)}, u32[]{:S(2)}, u32[]{:S(2)}) collective-permute-start(f32[2,64,8,256]{3,2,1,0:T(8,128)S(1)} %copy-done.2), channel_id=1, source_target_pairs={{0,4},{4,0},{1,5},{5,1},{2,6},{6,2},{3,7},{7,3},{8,12},{12,8},{9,1... | collective-permute-start | bytes 3145736 | tf_op jit(solution)/shard_map/ppermute | solution.py:482
  737.9 56.9 %all-to-all-start.13 = ((f32[128,2,2,8,256]{4,3,2,1,0:T(8,128)}), f32[128,2,2,8,256]{4,3,2,1,0:T(8,128)}, u32[]{:S(2)}, u32[]{:S(2)}) async-start(f32[128,2,2,8,256]{4,3,2,1,0:T(8,128)} %bitcast.81), calls=%async_computation.13 | async-start | bytes 8388608 | tf_op jit(solution)/shard_map/all_to_all | solution.py:593
  794.8 58.1 %all-to-all-start.14 = ((f32[128,2,2,8,256]{4,3,2,1,0:T(8,128)}), f32[128,2,2,8,256]{4,3,2,1,0:T(8,128)}, u32[]{:S(2)}, u32[]{:S(2)}) async-start(f32[128,2,2,8,256]{4,3,2,1,0:T(8,128)} %bitcast.78), calls=%async_computation.14 | async-start | bytes 8388608 | tf_op jit(solution)/shard_map/all_to_all | solution.py:593
  891.0 71.1 %collective-permute-start.4 = (f32[3,64,8,256]{3,2,1,0:T(8,128)}, f32[3,64,8,256]{3,2,1,0:T(8,128)}, u32[]{:S(2)}, u32[]{:S(2)}) collective-permute-start(f32[3,64,8,256]{3,2,1,0:T(8,128)} %get-tuple-element.131), channel_id=1, source_target_pairs={{0,4},{4,0},{1,5},{5,1},{2,6},{6,2},{3,7},{7,3},{8,12},{12,8},{9,1... | collective-permute-start | bytes 4718600 | tf_op jit(solution)/shard_map/ppermute | solution.py:482
  899.2 62.8 %copy-start.10 = (f32[3,64,8,256]{3,2,1,0:T(8,128)S(1)}, f32[3,64,8,256]{3,2,1,0:T(8,128)}, u32[]{:S(2)}) copy-start(f32[3,64,8,256]{3,2,1,0:T(8,128)} %get-tuple-element.129) | copy-start | bytes 4718596
  966.3 98.7 %all-to-all-start.16 = ((f32[4,2,64,8,256]{4,3,2,1,0:T(8,128)}), f32[4,2,64,8,256]{4,3,2,1,0:T(8,128)}, u32[]{:S(2)}, u32[]{:S(2)}) async-start(f32[4,2,64,8,256]{4,3,2,1,0:T(8,128)} %broadcast_in_dim.20), calls=%async_computation.16 | async-start | bytes 8388608 | tf_op jit(solution)/shard_map/all_to_all | solution.py:671
  971.3 98.6 %collective-permute-start.5 = (f32[1,64,2,8,256]{4,3,2,1,0:T(8,128)}, f32[1,64,2,8,256]{4,3,2,1,0:T(8,128)}, u32[]{:S(2)}, u32[]{:S(2)}) collective-permute-start(f32[1,64,2,8,256]{4,3,2,1,0:T(8,128)} %get-tuple-element.136), channel_id=1, source_target_pairs={{0,0},{4,20},{8,4},{12,16},{16,8},{20,28},{24,12},{28,24},{1,1},{5... | collective-permute-start | bytes 3145736 | tf_op jit(solution)/shard_map/ppermute | solution.py:517
  980.8 89.1 %collective-permute-start.6 = (f32[1,64,2,8,256]{4,3,2,1,0:T(8,128)S(1)}, f32[1,64,2,8,256]{4,3,2,1,0:T(8,128)}, u32[]{:S(2)}, u32[]{:S(2)}) collective-permute-start(f32[1,64,2,8,256]{4,3,2,1,0:T(8,128)S(1)} %copy-done.12), channel_id=1, source_target_pairs={{0,4},{4,16},{8,8},{12,28},{16,12},{20,24},{24,0},{28,20},{1,5},{5... | collective-permute-start | bytes 3145736 | tf_op jit(solution)/shard_map/ppermute | solution.py:517
  982.7 87.2 %collective-permute-start.7 = (f32[1,64,2,8,256]{4,3,2,1,0:T(8,128)S(1)}, f32[1,64,2,8,256]{4,3,2,1,0:T(8,128)}, u32[]{:S(2)}, u32[]{:S(2)}) collective-permute-start(f32[1,64,2,8,256]{4,3,2,1,0:T(8,128)S(1)} %copy-done.11), channel_id=1, source_target_pairs={{0,8},{4,28},{8,12},{12,24},{16,0},{20,20},{24,4},{28,16},{1,9},{5... | collective-permute-start | bytes 3145736 | tf_op jit(solution)/shard_map/ppermute | solution.py:517
  984.7 101.9 %collective-permute-start.8 = (f32[1,64,2,8,256]{4,3,2,1,0:T(8,128)S(1)}, f32[1,64,2,8,256]{4,3,2,1,0:T(8,128)}, u32[]{:S(2)}, u32[]{:S(2)}) collective-permute-start(f32[1,64,2,8,256]{4,3,2,1,0:T(8,128)S(1)} %get-tuple-element.139), channel_id=1, source_target_pairs={{0,12},{4,24},{8,0},{12,20},{16,4},{20,16},{24,8},{28,28},{1,13},{... | collective-permute-start | bytes 3145736 | tf_op jit(solution)/shard_map/ppermute | solution.py:517
  (14 other events, 82.9 us)

commit v6 on v5

--- a/solution.py
+++ b/solution.py
@@ -214,9 +214,9 @@
     lax.fori_loop(0, depth, body, 0, unroll=4)
 
 
-def assemble_kernel(spot, *refs):
+def assemble_kernel(shares, spot, *refs):
     *rounds, out = refs
-    turn = lax.rem(spot[0] + len(rounds) - pl.program_id(0), len(rounds))
+    turn = spot[0] * shares + lax.rem(pl.program_id(0) + shares - spot[1], shares)
     for t, ref in enumerate(rounds):
 
         @pl.when(turn == t)
@@ -498,34 +498,40 @@
 
 def payloads(chunks, shares, per_share, share):
     sent = []
-    for t in range(shares):
-        number = lax.rem(share + t, shares)
-        cut = [lax.dynamic_slice_in_dim(w, number // 2 * per_share, per_share, axis=0) for w in chunks]
-        sent.append(jnp.where(number % 2 == 0, cut[0], cut[1]))
+    for w in chunks:
+        for t in range(shares):
+            slot = lax.rem(share + shares - t, shares) // 2
+            sent.append(lax.dynamic_slice_in_dim(w, slot * per_share, per_share, axis=0))
     return sent
 
 
-def deliver(sent, shares, per_share, share, half, gate):
+def deliver(sent, shares, chunk):
     slots = shares // 2
     rounds = []
     for t in range(shares):
-        pairs = []
-        for a in range(shares):
-            g, c = divmod((a + t) % shares, 2)
-            for h in (0, 1):
-                pairs.append((a * 2 + h, (h * slots + g) * 2 + (h + c) % 2))
+        pairs = [
+            ((t + 2 * g) % shares * 2 + h, (h * slots + g) * 2 + (h + chunk) % 2)
+            for g in range(slots)
+            for h in (0, 1)
+        ]
         rounds.append(lax.ppermute(sent[t], ("src", "half"), pairs))
-    spot = after(2 * lax.rem(share, slots) + lax.rem(half + share // slots, 2), gate)
-    _, depth, _, rows, ny = rounds[0].shape
+    return rounds
+
+
+def assembled(rounds, shares, share, half, gate):
+    slots = shares // 2
+    chunk = lax.rem(share // slots + half, 2)
+    spot = after(jnp.stack([chunk, 2 * lax.rem(share, slots)]).astype(jnp.int32), gate)
+    per_share, depth, _, rows, ny = rounds[0].shape
     whole = pl.BlockSpec(rounds[0].shape, lambda a: (0, 0, 0, 0, 0))
     out = pl.pallas_call(
-        assemble_kernel,
+        partial(assemble_kernel, shares),
         grid=(shares,),
-        in_specs=[SMEM] + [whole] * shares,
+        in_specs=[SMEM] + [whole] * len(rounds),
         out_specs=pl.BlockSpec((per_share, 2, depth, None, rows, ny), lambda a: (0, 0, 0, a, 0, 0)),
         out_shape=jax.ShapeDtypeStruct((per_share, 2, depth, shares, rows, ny), F32),
         name="assemble",
-    )(spot.reshape(1).astype(jnp.int32), *rounds)
+    )(spot, *rounds)
     return out.reshape(per_share, 2, depth, shares * rows, ny)
 
 
@@ -660,7 +666,9 @@
         received = swap_halves(parts[1])
         if last:
             sent = payloads(source, shares, per_share, share)
-            received, *sent = lax.optimization_barrier((received, *sent))
+            rounds = deliver(sent[:shares], shares, 0)
+            received, *both_sets = lax.optimization_barrier((received, *rounds, *sent[shares:]))
+            rounds = both_sets[:shares] + deliver(both_sets[shares:], shares, 1)
         sums = parts[0] + received
         chi_own = bounded(sums[0], sums[1], sums[2], total_sources)
         if not last:
@@ -670,7 +678,7 @@
     copies = jnp.broadcast_to(chi_own[None], (shares,) + chi_own.shape)
     contrast_new = lax.all_to_all(copies, "src", 0, 0, tiled=True)
     contrast_new = contrast_new.transpose(1, 2, 0, 3, 4).reshape(contrast.shape)
-    contrast_sources = deliver(sent, shares, per_share, share, half, contrast_new)
+    contrast_sources = assembled(rounds, shares, share, half, contrast_new)
     return contrast_sources, contrast_new
 
 

time: 1100 us -> 1090 us (level)
    all_to_all x5, waiting for transfers between devices: 171 us -> 225 us  [exchange(): return lax.all_to_all(flat, GROUP, 0, 0, tiled=True).reshape(value.shape)]
    ppermute x5, waiting for transfers between devices: 283 us -> 238 us  [swap_halves(): return lax.ppermute(value, 'half', [(0, 1), (1, 0)])]
    all_to_all x2, waiting for transfers between devices: 44.9 us -> 0.01 us  [on_device(): came[c] = lax.all_to_all(out[-1], GROUP, 0, 0, tiled=True)]
    ppermute x4 -> x8, waiting for transfers between devices: 16.7 us -> 41.1 us  [deliver(): rounds.append(lax.ppermute(sent[t], ('src', 'half'), pairs))]
    ppermute x4 -> x8, starting transfers between devices: 20.5 us -> 22.1 us  [deliver(): rounds.append(lax.ppermute(sent[t], ('src', 'half'), pairs))]
  transfers between devices with their start and end apart: 21 -> 25, of which waited for: 14 -> 15; matrix products, arithmetic and copies ran while one was open for 2% -> 2% of each run, Pallas kernels for 7% -> 7%
where the time goes in v6:
time: 1090 us; the launch traced here: 1080 us
  waiting for transfers between devices  609 us (56%)
  Pallas kernels  172 us (16%)
  blocking collectives  146 us (13%)
  starting transfers between devices  91 us (8%)
  other arithmetic  31.5 us (3%)
  local copies, waits for them, and re-layouts  23.6 us (2%)
    ppermute x5, waiting for transfers between devices, swap_halves(): return lax.ppermute(value, 'half', [(0, 1), (1, 0)])  238 us
    all_to_all x5, waiting for transfers between devices, exchange(): return lax.all_to_all(flat, GROUP, 0, 0, tiled=True).reshape(value.shape)  225 us
    all_to_all x2, blocking collectives, on_device(): came[c] = lax.all_to_all(out[-1], GROUP, 0, 0, tiled=True)  111 us
    pallas_call x18, Pallas kernels, call(): pl.pallas_call(kernel, grid=(self.ny // self.lanes, second), in_specs=[sp...  105 us
    all_to_all x1, waiting for transfers between devices, on_device(): contrast_new = lax.all_to_all(copies, 'src', 0, 0, tiled=True)  77.9 us
    pallas_call x5, Pallas kernels, plane_call(): pl.pallas_call(kernel, grid=(planes // group,), in_specs=[SMEM] + [whole(...  60.9 us
    ppermute x8, waiting for transfers between devices, deliver(): rounds.append(lax.ppermute(sent[t], ('src', 'half'), pairs))  41.1 us
    all_to_all x3, blocking collectives, everyone(): return jnp.sum(lax.all_to_all(sent, ALL, 0, 0, tiled=True), axis=0)  35.2 us
  transfers between devices with their start and end apart: 25, of which 15 were waited for; matrix products, arithmetic and copies ran while one was open for 2% of the time, Pallas kernels for 7%

profile of v6, /device:TPU:0, one launch (start us, length us, event | category | flops | bytes accessed | tf_op | source)
XLA Modules:
  0.0 1083.4 jit_solution(7006226720564616144)
XLA Ops:
  13.6 9.0 fusion.1
  40.2 42.8 %collective-permute-done.chi = f32[2,64,8,256]{3,2,1,0:T(8,128)S(1)} collective-permute-done((f32[2,64,8,256]{3,2,1,0:T(8,128)S(1)}, f32[2,64,8,256]{3,2,1,0:T(8,128)S(1)}, u32[]{:S(2)}, u32[]{:S(2)}) %collective-permute-start) | collective-permute-done | bytes 1048608 | tf_op jit(solution)/shard_map/ppermute | solution.py:482
  98.4 25.2 %all-to-all-done.3 = f32[128,2,8,256]{3,2,1,0:T(8,128)S(1)} async-done(((f32[128,2,8,256]{3,2,1,0:T(8,128)}), f32[128,2,8,256]{3,2,1,0:T(8,128)S(1)}, u32[]{:S(2)}, u32[]{:S(2)}) %all-to-all-start.3) | async-done | bytes 2097184 | tf_op jit(solution)/shard_map/all_to_all | solution.py:614
  128.7 11.8 %shard_map.106 = f32[16,8,2,2,8,256]{5,4,3,2,1,0:T(8,128)} custom-call(f32[8]{0:T(128)} %multiply_multiply_fusion.lz, f32[256,128]{1,0:T(8,128)} %jit_solution_.3.lx, f32[2,1,128]{2,1,0:T(1,128)} %constant.243.clone.ly, bf16[2,2,256,256]{3,2,1,0:T(8,128)(2,1)} %constant.244.clone.xf, bf16[2,2,256,256]{3,2,1,0:T(8,128)(2,1)} %constant.245.clone.xb, ...), custom_call_target="tpu_custom_call" | custom-call | flops 6442450944 | bytes 8388608 | tf_op jit(solution)/shard_map/pallas_call | solution.py:455
  149.0 49.0 %all-to-all-done.4 = f32[128,2,2,8,256]{4,3,2,1,0:T(8,128)} async-done(((f32[128,2,2,8,256]{4,3,2,1,0:T(8,128)}), f32[128,2,2,8,256]{4,3,2,1,0:T(8,128)}, u32[]{:S(2)}, u32[]{:S(2)}) %all-to-all-start.4) | async-done | bytes 4194336 | tf_op jit(solution)/shard_map/all_to_all | solution.py:599
  213.7 50.4 %collective-permute-done.1 = f32[2,2,8,256]{3,2,1,0:T(8,128)S(1)} collective-permute-done((f32[2,2,8,256]{3,2,1,0:T(8,128)S(1)}, f32[2,2,8,256]{3,2,1,0:T(8,128)S(1)}, u32[]{:S(2)}, u32[]{:S(2)}) %collective-permute-start.1) | collective-permute-done | bytes 32800 | tf_op jit(solution)/shard_map/ppermute | solution.py:482
  272.1 56.5 %all_to_all.96 = f32[128,2,2,8,256]{4,3,2,1,0:T(8,128)} all-to-all(f32[128,2,2,8,256]{4,3,2,1,0:T(8,128)} %get-tuple-element.104), channel_id=1, replica_groups=mesh['src'=4,'half'=2,'rest'=4] {'src','rest'}, dimensions={0} | all-to-all | bytes 8388608 | tf_op jit(solution)/shard_map/all_to_all | solution.py:634
  328.6 16.4 %shard_map.109 = (f32[16,8,2,2,8,256]{5,4,3,2,1,0:T(8,128)}, f32[8,2,2,256,128]{4,3,2,1,0:T(8,128)}) custom-call(f32[8]{0:T(128)} %multiply_multiply_fusion.lz, f32[256,128]{1,0:T(8,128)} %jit_solution_.3.lx, f32[2,1,128]{2,1,0:T(1,128)} %constant.243.clone.ly, bf16[2,2,256,256]{3,2,1,0:T(8,128)(2,1)} %constant.244.clone.xf, ...), custom_call_target="tpu_custom_call" | custom-call | flops 9663676416 | bytes 12582912 | tf_op jit(solution)/shard_map/pallas_call | solution.py:455
  357.7 44.0 %all-to-all-done.7 = f32[128,2,2,8,256]{4,3,2,1,0:T(8,128)} async-done(((f32[128,2,2,8,256]{4,3,2,1,0:T(8,128)}), f32[128,2,2,8,256]{4,3,2,1,0:T(8,128)}, u32[]{:S(2)}, u32[]{:S(2)}) %all-to-all-start.7) | async-done | bytes 4194336 | tf_op jit(solution)/shard_map/all_to_all | solution.py:599
  415.8 44.0 %all-to-all-done.8 = f32[128,2,2,8,256]{4,3,2,1,0:T(8,128)} async-done(((f32[128,2,2,8,256]{4,3,2,1,0:T(8,128)}), f32[128,2,2,8,256]{4,3,2,1,0:T(8,128)}, u32[]{:S(2)}, u32[]{:S(2)}) %all-to-all-start.8) | async-done | bytes 4194336 | tf_op jit(solution)/shard_map/all_to_all | solution.py:599
  474.8 12.3 %all_to_all.97 = f32[32,1,128]{2,1,0:T(1,128)S(1)} all-to-all(f32[32,1,128]{2,1,0:T(1,128)S(1)} %broadcast_in_dim.17), channel_id=1, replica_groups=mesh['src'=4,'half'=2,'rest'=4] {'src','half','rest'}, dimensions={0} | all-to-all | bytes 32768 | tf_op jit(solution)/shard_map/all_to_all | solution.py:478
  506.8 62.1 %collective-permute-done.2 = f32[3,64,8,256]{3,2,1,0:T(8,128)S(1)} collective-permute-done((f32[3,64,8,256]{3,2,1,0:T(8,128)}, f32[3,64,8,256]{3,2,1,0:T(8,128)S(1)}, u32[]{:S(2)}, u32[]{:S(2)}) %collective-permute-start.2) | collective-permute-done | bytes 1572896 | tf_op jit(solution)/shard_map/ppermute | solution.py:482
  573.1 8.9 all_to_all.98
  594.1 73.9 %collective-permute-done.3.chi = f32[2,64,8,256]{3,2,1,0:T(8,128)S(1)} collective-permute-done((f32[2,64,8,256]{3,2,1,0:T(8,128)S(1)}, f32[2,64,8,256]{3,2,1,0:T(8,128)S(1)}, u32[]{:S(2)}, u32[]{:S(2)}) %collective-permute-start.3) | collective-permute-done | bytes 1048608 | tf_op jit(solution)/shard_map/ppermute | solution.py:482
  675.3 54.7 %all_to_all.99 = f32[128,2,2,8,256]{4,3,2,1,0:T(8,128)} all-to-all(f32[128,2,2,8,256]{4,3,2,1,0:T(8,128)} %shard_map.118), channel_id=1, replica_groups=mesh['src'=4,'half'=2,'rest'=4] {'src','rest'}, dimensions={0} | all-to-all | bytes 8388608 | tf_op jit(solution)/shard_map/all_to_all | solution.py:634
  730.0 16.4 %shard_map.119 = (f32[16,8,2,2,8,256]{5,4,3,2,1,0:T(8,128)}, f32[8,2,2,256,128]{4,3,2,1,0:T(8,128)}) custom-call(f32[8]{0:T(128)} %multiply_multiply_fusion.lz, f32[256,128]{1,0:T(8,128)} %jit_solution_.3.lx, f32[2,1,128]{2,1,0:T(1,128)} %constant.243.clone.ly, bf16[2,2,256,256]{3,2,1,0:T(8,128)(2,1)} %constant.244.clone.xf, ...), custom_call_target="tpu_custom_call" | custom-call | flops 9663676416 | bytes 12582912 | tf_op jit(solution)/shard_map/pallas_call | solution.py:455
  759.3 44.0 %all-to-all-done.13 = f32[128,2,2,8,256]{4,3,2,1,0:T(8,128)} async-done(((f32[128,2,2,8,256]{4,3,2,1,0:T(8,128)}), f32[128,2,2,8,256]{4,3,2,1,0:T(8,128)}, u32[]{:S(2)}, u32[]{:S(2)}) %all-to-all-start.13) | async-done | bytes 4194336 | tf_op jit(solution)/shard_map/all_to_all | solution.py:599
  817.5 44.0 %all-to-all-done.14 = f32[128,2,2,8,256]{4,3,2,1,0:T(8,128)} async-done(((f32[128,2,2,8,256]{4,3,2,1,0:T(8,128)}), f32[128,2,2,8,256]{4,3,2,1,0:T(8,128)}, u32[]{:S(2)}, u32[]{:S(2)}) %all-to-all-start.14) | async-done | bytes 4194336 | tf_op jit(solution)/shard_map/all_to_all | solution.py:599
  876.6 14.1 %all_to_all.100 = f32[32,1,128]{2,1,0:T(1,128)S(1)} all-to-all(f32[32,1,128]{2,1,0:T(1,128)S(1)} %broadcast_in_dim.19), channel_id=1, replica_groups=mesh['src'=4,'half'=2,'rest'=4] {'src','half','rest'}, dimensions={0} | all-to-all | bytes 32768 | tf_op jit(solution)/shard_map/all_to_all | solution.py:478
  921.7 17.3 %collective-permute-done.6.refs_1_ = f32[1,64,2,8,256]{4,3,2,1,0:T(8,128)S(1)} collective-permute-done((f32[1,64,2,8,256]{4,3,2,1,0:T(8,128)S(1)}, f32[1,64,2,8,256]{4,3,2,1,0:T(8,128)S(1)}, u32[]{:S(2)}, u32[]{:S(2)}) %collective-permute-start.6) | collective-permute-done | bytes 1048608 | tf_op jit(solution)/shard_map/ppermute | solution.py:517
  939.0 23.9 %collective-permute-done.7.refs_2_ = f32[1,64,2,8,256]{4,3,2,1,0:T(8,128)S(1)} collective-permute-done((f32[1,64,2,8,256]{4,3,2,1,0:T(8,128)S(1)}, f32[1,64,2,8,256]{4,3,2,1,0:T(8,128)S(1)}, u32[]{:S(2)}, u32[]{:S(2)}) %collective-permute-start.7) | collective-permute-done | bytes 1048608 | tf_op jit(solution)/shard_map/ppermute | solution.py:517
  962.8 8.9 collective-permute-done.4
  984.0 8.4 collective-permute-start.11
  994.6 77.9 %all-to-all-done.16 = f32[4,2,64,8,256]{4,3,2,1,0:T(8,128)} async-done(((f32[4,2,64,8,256]{4,3,2,1,0:T(8,128)}), f32[4,2,64,8,256]{4,3,2,1,0:T(8,128)}, u32[]{:S(2)}, u32[]{:S(2)}) %all-to-all-start.16) | async-done | bytes 4194336 | tf_op jit(solution)/shard_map/all_to_all | solution.py:679
  (176 shorter events, 257.7 us)
Async XLA Ops:
  3.0 10.0 all-to-all-start.1
  30.1 58.7 %all-to-all-start.2 = ((f32[128,2,8,256]{3,2,1,0:T(8,128)}), f32[128,2,8,256]{3,2,1,0:T(8,128)}, u32[]{:S(2)}, u32[]{:S(2)}) async-start(f32[128,2,8,256]{3,2,1,0:T(8,128)} %get-tuple-element.100), calls=%async_computation.2 | async-start | bytes 4194304 | tf_op jit(solution)/shard_map/all_to_all | solution.py:614
  34.7 48.3 %collective-permute-start = (f32[2,64,8,256]{3,2,1,0:T(8,128)S(1)}, f32[2,64,8,256]{3,2,1,0:T(8,128)S(1)}, u32[]{:S(2)}, u32[]{:S(2)}) collective-permute-start(f32[2,64,8,256]{3,2,1,0:T(8,128)S(1)} %copy-done), channel_id=1, source_target_pairs={{0,4},{4,0},{1,5},{5,1},{2,6},{6,2},{3,7},{7,3},{8,12},{12,8},{9,1... | collective-permute-start | bytes 3145736 | tf_op jit(solution)/shard_map/ppermute | solution.py:482
  88.8 34.9 %all-to-all-start.3 = ((f32[128,2,8,256]{3,2,1,0:T(8,128)}), f32[128,2,8,256]{3,2,1,0:T(8,128)S(1)}, u32[]{:S(2)}, u32[]{:S(2)}) async-start(f32[128,2,8,256]{3,2,1,0:T(8,128)} %get-tuple-element.101), calls=%async_computation.3 | async-start | bytes 4194304 | tf_op jit(solution)/shard_map/all_to_all | solution.py:614
  124.4 16.1 %all-to-all-start = ((f32[32,1,128]{2,1,0:T(1,128)}), f32[32,1,128]{2,1,0:T(1,128)S(1)}, u32[]{:S(2)}, u32[]{:S(2)}) async-start(f32[32,1,128]{2,1,0:T(1,128)} %broadcast_in_dim.14), calls=%async_computation | async-start | bytes 32768 | tf_op jit(solution)/shard_map/all_to_all | solution.py:478
  140.5 57.4 %all-to-all-start.4 = ((f32[128,2,2,8,256]{4,3,2,1,0:T(8,128)}), f32[128,2,2,8,256]{4,3,2,1,0:T(8,128)}, u32[]{:S(2)}, u32[]{:S(2)}) async-start(f32[128,2,2,8,256]{4,3,2,1,0:T(8,128)} %bitcast.78), calls=%async_computation.4 | async-start | bytes 8388608 | tf_op jit(solution)/shard_map/all_to_all | solution.py:599
  205.3 66.7 %all-to-all-start.5 = ((f32[128,2,2,8,256]{4,3,2,1,0:T(8,128)}), f32[128,2,2,8,256]{4,3,2,1,0:T(8,128)}, u32[]{:S(2)}, u32[]{:S(2)}) async-start(f32[128,2,2,8,256]{4,3,2,1,0:T(8,128)} %get-tuple-element.102), calls=%async_computation.5 | async-start | bytes 8388608 | tf_op jit(solution)/shard_map/all_to_all | solution.py:634
  211.1 53.0 %collective-permute-start.1 = (f32[2,2,8,256]{3,2,1,0:T(8,128)S(1)}, f32[2,2,8,256]{3,2,1,0:T(8,128)S(1)}, u32[]{:S(2)}, u32[]{:S(2)}) collective-permute-start(f32[2,2,8,256]{3,2,1,0:T(8,128)S(1)} %get-tuple-element.174), channel_id=1, source_target_pairs={{0,4},{4,0},{1,5},{5,1},{2,6},{6,2},{3,7},{7,3},{8,12},{12,8},{9,1... | collective-permute-start | bytes 98312 | tf_op jit(solution)/shard_map/ppermute | solution.py:482
  345.0 56.7 %all-to-all-start.7 = ((f32[128,2,2,8,256]{4,3,2,1,0:T(8,128)}), f32[128,2,2,8,256]{4,3,2,1,0:T(8,128)}, u32[]{:S(2)}, u32[]{:S(2)}) async-start(f32[128,2,2,8,256]{4,3,2,1,0:T(8,128)} %bitcast.84), calls=%async_computation.7 | async-start | bytes 8388608 | tf_op jit(solution)/shard_map/all_to_all | solution.py:599
  401.7 58.1 %all-to-all-start.8 = ((f32[128,2,2,8,256]{4,3,2,1,0:T(8,128)}), f32[128,2,2,8,256]{4,3,2,1,0:T(8,128)}, u32[]{:S(2)}, u32[]{:S(2)}) async-start(f32[128,2,2,8,256]{4,3,2,1,0:T(8,128)} %bitcast.81), calls=%async_computation.8 | async-start | bytes 8388608 | tf_op jit(solution)/shard_map/all_to_all | solution.py:599
  497.9 71.0 %collective-permute-start.2 = (f32[3,64,8,256]{3,2,1,0:T(8,128)}, f32[3,64,8,256]{3,2,1,0:T(8,128)S(1)}, u32[]{:S(2)}, u32[]{:S(2)}) collective-permute-start(f32[3,64,8,256]{3,2,1,0:T(8,128)} %get-tuple-element.118), channel_id=1, source_target_pairs={{0,4},{4,0},{1,5},{5,1},{2,6},{6,2},{3,7},{7,3},{8,12},{12,8},{9,1... | collective-permute-start | bytes 4718600 | tf_op jit(solution)/shard_map/ppermute | solution.py:482
  588.9 86.4 %all-to-all-start.11 = ((f32[128,2,2,8,256]{4,3,2,1,0:T(8,128)}), f32[128,2,2,8,256]{4,3,2,1,0:T(8,128)}, u32[]{:S(2)}, u32[]{:S(2)}) async-start(f32[128,2,2,8,256]{4,3,2,1,0:T(8,128)} %shard_map.117), calls=%async_computation.11 | async-start | bytes 8388608 | tf_op jit(solution)/shard_map/all_to_all | solution.py:634
  593.6 74.5 %collective-permute-start.3 = (f32[2,64,8,256]{3,2,1,0:T(8,128)S(1)}, f32[2,64,8,256]{3,2,1,0:T(8,128)S(1)}, u32[]{:S(2)}, u32[]{:S(2)}) collective-permute-start(f32[2,64,8,256]{3,2,1,0:T(8,128)S(1)} %copy-done.2), channel_id=1, source_target_pairs={{0,4},{4,0},{1,5},{5,1},{2,6},{6,2},{3,7},{7,3},{8,12},{12,8},{9,1... | collective-permute-start | bytes 3145736 | tf_op jit(solution)/shard_map/ppermute | solution.py:482
  746.4 56.9 %all-to-all-start.13 = ((f32[128,2,2,8,256]{4,3,2,1,0:T(8,128)}), f32[128,2,2,8,256]{4,3,2,1,0:T(8,128)}, u32[]{:S(2)}, u32[]{:S(2)}) async-start(f32[128,2,2,8,256]{4,3,2,1,0:T(8,128)} %bitcast.82), calls=%async_computation.13 | async-start | bytes 8388608 | tf_op jit(solution)/shard_map/all_to_all | solution.py:599
  803.3 58.1 %all-to-all-start.14 = ((f32[128,2,2,8,256]{4,3,2,1,0:T(8,128)}), f32[128,2,2,8,256]{4,3,2,1,0:T(8,128)}, u32[]{:S(2)}, u32[]{:S(2)}) async-start(f32[128,2,2,8,256]{4,3,2,1,0:T(8,128)} %bitcast.80), calls=%async_computation.14 | async-start | bytes 8388608 | tf_op jit(solution)/shard_map/all_to_all | solution.py:599
  900.8 71.0 %collective-permute-start.4 = (f32[3,64,8,256]{3,2,1,0:T(8,128)}, f32[3,64,8,256]{3,2,1,0:T(8,128)S(1)}, u32[]{:S(2)}, u32[]{:S(2)}) collective-permute-start(f32[3,64,8,256]{3,2,1,0:T(8,128)} %get-tuple-element.135), channel_id=1, source_target_pairs={{0,4},{4,0},{1,5},{5,1},{2,6},{6,2},{3,7},{7,3},{8,12},{12,8},{9,1... | collective-permute-start | bytes 4718600 | tf_op jit(solution)/shard_map/ppermute | solution.py:482
  912.4 26.5 %collective-permute-start.6 = (f32[1,64,2,8,256]{4,3,2,1,0:T(8,128)S(1)}, f32[1,64,2,8,256]{4,3,2,1,0:T(8,128)S(1)}, u32[]{:S(2)}, u32[]{:S(2)}) collective-permute-start(f32[1,64,2,8,256]{4,3,2,1,0:T(8,128)S(1)} %get-tuple-element.162), channel_id=1, source_target_pairs={{8,0},{12,20},{24,8},{28,28},{9,1},{13,21},{25,9},{29,29},{10,2},{... | collective-permute-start | bytes 3145736 | tf_op jit(solution)/shard_map/ppermute | solution.py:517
  913.7 49.1 %collective-permute-start.7 = (f32[1,64,2,8,256]{4,3,2,1,0:T(8,128)S(1)}, f32[1,64,2,8,256]{4,3,2,1,0:T(8,128)S(1)}, u32[]{:S(2)}, u32[]{:S(2)}) collective-permute-start(f32[1,64,2,8,256]{4,3,2,1,0:T(8,128)S(1)} %get-tuple-element.161), channel_id=1, source_target_pairs={{16,0},{20,20},{0,8},{4,28},{17,1},{21,21},{1,9},{5,29},{18,2},{22... | collective-permute-start | bytes 3145736 | tf_op jit(solution)/shard_map/ppermute | solution.py:517
  918.3 44.5 %collective-permute-start.8 = (f32[1,64,2,8,256]{4,3,2,1,0:T(8,128)S(1)}, f32[1,64,2,8,256]{4,3,2,1,0:T(8,128)S(1)}, u32[]{:S(2)}, u32[]{:S(2)}) collective-permute-start(f32[1,64,2,8,256]{4,3,2,1,0:T(8,128)S(1)} %get-tuple-element.160), channel_id=1, source_target_pairs={{24,0},{28,20},{8,8},{12,28},{25,1},{29,21},{9,9},{13,29},{26,2},{... | collective-permute-start | bytes 3145736 | tf_op jit(solution)/shard_map/ppermute | solution.py:517
  974.6 97.9 %all-to-all-start.16 = ((f32[4,2,64,8,256]{4,3,2,1,0:T(8,128)}), f32[4,2,64,8,256]{4,3,2,1,0:T(8,128)}, u32[]{:S(2)}, u32[]{:S(2)}) async-start(f32[4,2,64,8,256]{4,3,2,1,0:T(8,128)} %broadcast_in_dim.20), calls=%async_computation.16 | async-start | bytes 8388608 | tf_op jit(solution)/shard_map/all_to_all | solution.py:679
  979.8 97.7 %collective-permute-start.9 = (f32[1,64,2,8,256]{4,3,2,1,0:T(8,128)}, f32[1,64,2,8,256]{4,3,2,1,0:T(8,128)}, u32[]{:S(2)}, u32[]{:S(2)}) collective-permute-start(f32[1,64,2,8,256]{4,3,2,1,0:T(8,128)} %get-tuple-element.144), channel_id=1, source_target_pairs={{0,4},{4,16},{16,12},{20,24},{1,5},{5,17},{17,13},{21,25},{2,6},{6... | collective-permute-start | bytes 3145736 | tf_op jit(solution)/shard_map/ppermute | solution.py:517
  982.3 95.1 %collective-permute-start.10 = (f32[1,64,2,8,256]{4,3,2,1,0:T(8,128)S(1)}, f32[1,64,2,8,256]{4,3,2,1,0:T(8,128)}, u32[]{:S(2)}, u32[]{:S(2)}) collective-permute-start(f32[1,64,2,8,256]{4,3,2,1,0:T(8,128)S(1)} %copy-done.18), channel_id=1, source_target_pairs={{8,4},{12,16},{24,12},{28,24},{9,5},{13,17},{25,13},{29,25},{10,6}... | collective-permute-start | bytes 3145736 | tf_op jit(solution)/shard_map/ppermute | solution.py:517
  984.0 93.5 %collective-permute-start.11 = (f32[1,64,2,8,256]{4,3,2,1,0:T(8,128)S(1)}, f32[1,64,2,8,256]{4,3,2,1,0:T(8,128)}, u32[]{:S(2)}, u32[]{:S(2)}) collective-permute-start(f32[1,64,2,8,256]{4,3,2,1,0:T(8,128)S(1)} %copy-done.17), channel_id=1, source_target_pairs={{16,4},{20,16},{0,12},{4,24},{17,5},{21,17},{1,13},{5,25},{18,6},{... | collective-permute-start | bytes 3145736 | tf_op jit(solution)/shard_map/ppermute | solution.py:517
  992.4 85.1 %collective-permute-start.12 = (f32[1,64,2,8,256]{4,3,2,1,0:T(8,128)S(1)}, f32[1,64,2,8,256]{4,3,2,1,0:T(8,128)}, u32[]{:S(2)}, u32[]{:S(2)}) collective-permute-start(f32[1,64,2,8,256]{4,3,2,1,0:T(8,128)S(1)} %copy-done.16), channel_id=1, source_target_pairs={{24,4},{28,16},{8,12},{12,24},{25,5},{29,17},{9,13},{13,25},{26,6}... | collective-permute-start | bytes 3145736 | tf_op jit(solution)/shard_map/ppermute | solution.py:517
  (28 other events, 386.7 us)
